TPU v7x, 128 devices: a whole 4x4x4 slice. The times are simulated.
128 devices in a mesh: seq: 64 (over x_lo, y, z, core), fsdp: 2 (over x_hi).
Axes of the slice: x: 4 (x_hi: 2, x_lo: 2; x = x_hi * 2 + x_lo), y: 4, z: 4, core: 2. Of those that a mesh axis runs over, the one named last changes fastest.
Arguments:
- tokens: bfloat16 [32768, 5376], P(('seq', 'fsdp')), may hold values from -6 to 6
- norm_gain: float32 [5376], replicated, may hold values from 0.1 to 1.9
- query_weight: bfloat16 [5376, 2048], P('seq', 'fsdp'), may hold values from -0.078125 to 0.078125
- key_matrix: bfloat16 [5376, 1024], P('seq', 'fsdp'), may hold values from -0.078125 to 0.078125
- value_matrix: bfloat16 [5376, 1024], P('seq', 'fsdp'), may hold values from -0.078125 to 0.078125
- out_weight: bfloat16 [5376, 2048], P('seq', 'fsdp'), may hold values from -0.125 to 0.125
- query_gain: float32 [128], replicated, may hold values from 0.1 to 1.9
- key_gain: float32 [128], replicated, may hold values from 0.1 to 1.9
- post_gain: float32 [5376], replicated, may hold values from 0.1 to 1.9
Outputs:
- layer_out: bfloat16 [32768, 5376], P(('seq', 'fsdp'))
All inputs are finite; a program needn't handle non-finite values.
Results may differ from a plain program's by a relative error of at most 0.011.
Values may be sent and summed in bfloat16 or wider, within the bound.
No kernel may reach another device: no remote copies, remote signals or barrier semaphores. Data moves between devices by JAX's collectives and lax.ppermute only.
A program may use at most 192 MiB of HBM per device.

v0:
```python
import jax
import jax.numpy as jnp
from jax import lax
from jax.sharding import PartitionSpec as P

HEAD_SIZE = 128
WINDOW_LENGTH = 1024


epsilon = 1e-06
score_scale = 168.0 ** (-0.5)
rope_base = 10000.0
masked_score = -1e30


def in_one_piece(arrays, axis, dim, along):
    both = jnp.concatenate(arrays, axis=along)
    result, at, outs = (lax.all_gather(both, axis, axis=dim, tiled=True), 0, [])
    for a in arrays:
        outs.append(lax.slice_in_dim(result, at, at + a.shape[along], axis=along))
        at += a.shape[along]
    return tuple(outs)


def passed_along(block, axis, distance):
    devices = range(lax.axis_size(axis))
    route = [(i - distance, i) for i in devices if i - distance in devices]
    return lax.ppermute(block, axis, route)


def in_blocks(x, dim, peers):
    shape = x.shape
    blocks = x.reshape(*shape[:dim], peers, shape[dim] // peers, *shape[dim + 1 :])
    return jnp.moveaxis(blocks, dim, 0)


def sent_and_summed(x, axis, dim):
    peers = lax.axis_size(axis)
    blocks = lax.all_to_all(in_blocks(x, dim, peers), axis, 0, 0, tiled=True)
    return jnp.sum(blocks.astype(jnp.float32), axis=0)


def rms_scaled(values, gain):
    mean_square = jnp.mean(values * values, axis=-1, keepdims=True)
    return values * lax.rsqrt(mean_square + epsilon) * gain


def rotary(values, positions):
    half_width = values.shape[-1] // 2
    exponents = jnp.arange(half_width, dtype=jnp.float32) * (2.0 / values.shape[-1])
    frequency = jnp.exp(-exponents * jnp.log(jnp.float32(rope_base)))
    angles = positions.astype(jnp.float32)[:, None] * frequency[None, :]
    cosine = jnp.cos(angles)[:, None, :]
    sine = jnp.sin(angles)[:, None, :]
    first_half = values[..., :half_width]
    second_half = values[..., half_width:]
    return jnp.concatenate(
        [first_half * cosine - second_half * sine, second_half * cosine + first_half * sine],
        axis=-1,
    )


def head_states(projected, gain, positions):
    shaped = projected.reshape(projected.shape[0], -1, HEAD_SIZE)
    return rotary(rms_scaled(shaped, gain), positions).astype(jnp.bfloat16)


def window_block(query_block, key_block, value_block, query_pos, key_pos):
    scores = (
        jnp.einsum("rkgd,lkd->kgrl", query_block, key_block, preferred_element_type=jnp.float32)
        * score_scale
    )
    offset = query_pos[:, None] - key_pos[None, :]
    allowed = (offset >= 0) & (offset < WINDOW_LENGTH) & (key_pos[None, :] >= 0)
    scores = jnp.where(allowed, scores, masked_score)
    highest = jnp.max(scores, axis=-1, keepdims=True)
    raised = jnp.exp(scores - highest)
    weights = (raised / jnp.sum(raised, axis=-1, keepdims=True)).astype(jnp.bfloat16)
    mixed = jnp.einsum("kgrl,lkd->rkgd", weights, value_block, preferred_element_type=jnp.float32)
    return mixed.astype(jnp.bfloat16).reshape(query_block.shape[0], -1)


def on_device(
    tokens,
    norm_gain,
    query_weight,
    key_matrix,
    value_matrix,
    out_weight,
    query_gain,
    key_gain,
    post_gain,
):
    pair_rows = lax.all_gather(tokens, "fsdp", axis=0, tiled=True)
    shard_rows = pair_rows.shape[0]
    first_row = lax.axis_index("seq") * shard_rows
    normed_input = rms_scaled(pair_rows.astype(jnp.float32), norm_gain).astype(jnp.bfloat16)
    query_width = query_weight.shape[1]
    key_width = key_matrix.shape[1]
    local_heads = key_width // HEAD_SIZE
    query_groups = query_width // key_width
    query_full, key_full, value_full, out_full = in_one_piece(
        (query_weight, key_matrix, value_matrix, out_weight), "seq", 0, 1
    )
    queries_raw = jnp.dot(normed_input, query_full, preferred_element_type=jnp.float32)
    keys_raw = jnp.dot(normed_input, key_full, preferred_element_type=jnp.float32)
    values_raw = jnp.dot(normed_input, value_full, preferred_element_type=jnp.float32)
    positions = first_row + jnp.arange(shard_rows, dtype=jnp.int32)
    query_states = head_states(queries_raw, query_gain, positions).reshape(
        shard_rows, local_heads, query_groups, HEAD_SIZE
    )
    keys_now = head_states(keys_raw, key_gain, positions).reshape(shard_rows, key_width)
    values_now = values_raw.astype(jnp.bfloat16)
    stacked = jnp.stack([keys_now, values_now])
    reach = min(WINDOW_LENGTH, shard_rows)
    count = WINDOW_LENGTH // reach
    received = []
    for distance in range(1, count + 1):
        received = [passed_along(stacked, "seq", distance)] + received
    window_rows = jnp.concatenate(received + [stacked], axis=1)
    key_rows = window_rows.shape[1]
    keys_window = window_rows[0].reshape(key_rows, local_heads, HEAD_SIZE)
    values_window = window_rows[1].reshape(key_rows, local_heads, HEAD_SIZE)
    key_pos = first_row - WINDOW_LENGTH + jnp.arange(key_rows, dtype=jnp.int32)
    attended = window_block(query_states, keys_window, values_window, positions, key_pos)
    partial_out = lax.dot_general(
        attended, out_full, (((1,), (1,)), ((), ())), preferred_element_type=jnp.float32
    )
    summed = sent_and_summed(partial_out.astype(jnp.bfloat16), "fsdp", 0)
    return (tokens.astype(jnp.float32) + rms_scaled(summed, post_gain)).astype(jnp.bfloat16)


def solution(mesh):
    in_specs = (
        P(("seq", "fsdp"), None),
        P(),
        P("seq", "fsdp"),
        P("seq", "fsdp"),
        P("seq", "fsdp"),
        P("seq", "fsdp"),
        P(),
        P(),
        P(),
    )
    out_specs = P(("seq", "fsdp"), None)
    return jax.shard_map(
        on_device, mesh=mesh, in_specs=in_specs, out_specs=out_specs, check_vma=False
    )
```

profile of v0, /device:TPU:125, one launch (start us, length us, event | category | flops | bytes accessed | tf_op | source)
XLA Modules:
  0.0 492.2 jit_solution(15956823468113958190)
XLA Ops:
  6.5 0.0 all-gather.4.cloned.1.call-start
  6.5 0.7 all-gather.4.cloned.1.call-update
  7.3 0.0 all-gather.6.cloned.1.call-start
  7.3 1.9 maximum_bitcast_fusion
  9.2 0.0 all-gather.6.cloned.1.call-update
  9.3 1.0 multiply_cosine_fusion
  10.3 0.1 copy.44
  10.4 0.1 copy.43
  10.6 2.0 fusion.23
  12.5 70.6 %all-gather.4.cloned.1.call-done = bf16[512,5376]{1,0:T(8,128)(2,1)} async-done(((bf16[256,5376]{1,0:T(8,128)(2,1)}), bf16[512,5376]{1,0:T(8,128)(2,1)}) %all-gather.4.cloned.1.call-update) | async-done | bytes 5505040 | tf_op jit(solution)/shard_map/all_gather | solution.py:94
  83.1 3.7 fusion.6
  86.9 192.5 %all-gather.6.cloned.1.call-done = bf16[64,84,3072]{2,1,0:T(8,128)(2,1)} async-done(((bf16[1,84,3072]{2,1,0:T(8,128)(2,1)}), bf16[64,84,3072]{2,1,0:T(8,128)(2,1)}) %all-gather.6.cloned.1.call-update) | async-done | bytes 33030160 | tf_op jit(solution)/shard_map/all_gather | solution.py:18
  279.4 36.1 %reshape.140 = bf16[5376,3072]{1,0:T(8,128)(2,1)} reshape(bf16[64,84,3072]{2,1,0:T(8,128)(2,1)} %all-gather.6.cloned.1.call-done) | data formatting | bytes 66060288
  315.5 0.0 copy-done.8
  315.5 7.4 %multiply_reduce_fusion.2 = (f32[512,4]{0,1:T(4,128)S(1)}, f32[512,512]{0,1:T(8,128)S(1)}) fusion(bf16[5376,3072]{1,0:T(8,128)(2,1)} %reshape.140, bf16[512,5376]{1,0:T(8,128)(2,1)} %all-gather.4.cloned.1.call-done, f32[5376]{0:T(1024)S(1)} %copy-done.8, f32[512]{0:T(512)S(1)} %add_rsqrt_fusion.2), kind=kOutput, calls=%fused_computation.46 | convolution fusion | flops 2830104576 | bytes 12090368 | tf_op jit(solution)/shard_map/dot_general | solution.py:106
  322.9 0.0 copy-done.6
  322.9 0.2 multiply_multiply_fusion.1
  323.1 0.2 subtract_convert_fusion.1
  323.3 0.0 slice-start
  323.4 0.2 copy.56
  323.6 0.0 slice-start.1
  323.6 7.4 %fusion.35 = bf16[1,512,512]{2,1,0:T(8,128)(2,1)S(1)} fusion(bf16[5376,3072]{1,0:T(8,128)(2,1)} %reshape.140, bf16[512,5376]{1,0:T(8,128)(2,1)} %all-gather.4.cloned.1.call-done, f32[5376]{0:T(1024)S(1)} %copy-done.8, f32[512]{0:T(512)S(1)} %add_rsqrt_fusion.2), kind=kOutput, calls=%fused_computation.42 | convolution fusion | flops 2829844480 | bytes 11557888 | tf_op jit(solution)/shard_map/dot_general | solution.py:107
  331.0 0.0 copy-start.2
  331.0 1.1 pad_maximum_fusion
  332.1 2.9 collective-permute-start.1
  335.0 3.4 collective-permute-start
  338.5 0.0 copy-done.2
  338.5 0.0 slice-done
  338.5 0.0 slice-done.1
  338.5 8.7 %fusion.24 = f32[64,8,8,128]{3,1,2,0:T(8,128)S(1)} fusion(bf16[5376,3072]{1,0:T(8,128)(2,1)} %reshape.140, bf16[512,5376]{1,0:T(8,128)(2,1)S(1)} %bitcast.43, f32[5376]{0:T(1024)S(1)} %copy-done.8, f32[512]{0:T(512)S(1)} %add_rsqrt_fusion.2), kind=kOutput, calls=%fused_computation.36 | convolution fusion | flops 5648154624 | bytes 18635776 | tf_op jit(solution)/shard_map/dot_general | solution.py:105
  347.2 0.0 copy-start.7
  347.2 0.5 copy.60
  347.7 0.6 multiply_reduce_fusion.1
  348.3 0.1 copy.46
  348.5 0.1 copy.47
  348.6 0.0 copy-done.7
  348.6 0.9 multiply_multiply_fusion
  349.5 0.0 copy-start.3
  349.5 0.9 subtract_convert_fusion
  350.3 1.2 copy.49
  351.5 1.2 copy.48
  352.7 2.8 collective-permute-done.1
  355.5 15.1 %collective-permute-done = bf16[2,512,512]{2,1,0:T(8,128)(2,1)} collective-permute-done((bf16[2,512,512]{2,1,0:T(8,128)(2,1)}, bf16[2,512,512]{2,1,0:T(8,128)(2,1)}, u32[]{:S(2)}, u32[]{:S(2)}) %collective-permute-start) | collective-permute-done | bytes 1048608 | tf_op jit(solution)/shard_map/ppermute | solution.py:28
  370.6 0.0 copy-done.3
  370.6 1.7 maximum_maximum_fusion
  372.3 0.2 fusion.52
  372.5 1.6 copy.57
  374.1 0.4 reshape_squeeze.7
  374.5 0.0 copy-start.1
  374.5 0.0 copy-start.4
  374.5 13.5 %fusion.30 = f32[4,1536,512,2]{2,1,3,0:T(8,128)} fusion(bf16[1536,4,128,1]{2,1,0,3:T(4,128)(2,1)S(1)} %bitcast.40, bf16[512,4,2,64]{3,0,2,1:T(8,128)(2,1)} %bitcast.45, bf16[512,4,2,64]{3,0,2,1:T(8,128)(2,1)} %bitcast.47), kind=kOutput, calls=%fused_computation.39 | convolution fusion | flops 1612709888 | bytes 27787264 | tf_op jit(solution)/shard_map/rkgd,lkd->kgrl/dot_general | solution.py:70
  388.0 0.0 copy-done.1
  388.0 0.0 copy-done.4
  388.0 10.4 %fusion.53 = f32[4,2,512]{2,1,0:T(2,128)S(1)} fusion(pred[512,1536]{0,1:T(8,128)(4,1)S(1)} %copy-done.4, bf16[1536,4,128,1]{2,1,0,3:T(4,128)(2,1)S(1)} %bitcast.41, bf16[512,4,2,64]{3,0,2,1:T(8,128)(2,1)S(1)} %bitcast.46, bf16[512,4,2,64]{3,0,2,1:T(8,128)(2,1)} %bitcast.48), kind=kOutput, calls=%fused_computation.70 | convolution fusion | flops 1637877248 | bytes 3424256 | tf_op jit(solution)/shard_map/sub | solution.py:77
  398.4 14.2 %fusion.27 = bf16[4,128,2,512]{3,1,2,0:T(8,128)(2,1)S(1)} fusion(bf16[1536,4,128,1]{0,2,3,1:T(8,128)(2,1)} %bitcast.50, f32[4,2,512]{2,1,0:T(2,128)S(1)} %fusion.53, f32[4,1536,512,2]{2,1,3,0:T(8,128)} %fusion.30, pred[512,1536]{0,1:T(8,128)(4,1)S(1)} %copy-done.4), kind=kOutput, calls=%fused_computation.37 | convolution fusion | flops 1642599936 | bytes 28590080 | tf_op jit(solution)/shard_map/kgrl,lkd->rkgd/dot_general | solution.py:79
  412.7 10.4 %fusion.13 = bf16[512,5376]{1,0:T(8,128)(2,1)S(1)} fusion(bf16[512,1024]{0,1:T(8,128)(2,1)S(1)} %bitcast.51, bf16[5376,3072]{1,0:T(8,128)(2,1)} %reshape.140), kind=kOutput, calls=%fused_computation.19 | convolution fusion | flops 5639897088 | bytes 17563648 | tf_op jit(solution)/shard_map/dot_general | solution.py:126
  423.1 56.9 %all_to_all.5 = bf16[2,256,5376]{2,1,0:T(8,128)(2,1)S(1)} all-to-all(bf16[2,256,5376]{2,1,0:T(8,128)(2,1)S(1)} %bitcast.44), channel_id=1, replica_groups=mesh['seq'=64,'fsdp'=2] {'fsdp'}, dimensions={0} | all-to-all | bytes 11010048 | tf_op jit(solution)/shard_map/all_to_all | solution.py:39
  480.0 0.9 convert_reduce_fusion
  481.0 0.0 copy-start
  481.0 0.0 copy-start.5
  481.0 0.5 multiply_reduce_fusion
  481.5 1.3 copy-done
  482.8 0.0 copy-done.5
  482.8 2.6 add_convert_fusion
  (12 shorter events, 0.1 us)
Async XLA Ops:
  6.5 76.6 %all-gather.4.cloned.1.call-start = ((), (), s32[]{:S(2)}) async-start(), calls=%async_computation.1 | async-start | bytes 8257536 | tf_op jit(solution)/shard_map/all_gather | solution.py:94
  7.3 272.1 %all-gather.6.cloned.1.call-start = ((), (), s32[]{:S(2)}) async-start(), calls=%async_computation.2 | async-start | bytes 35143680 | tf_op jit(solution)/shard_map/all_gather | solution.py:18
  86.8 228.7 %copy-start.8 = (f32[5376]{0:T(1024)S(1)}, f32[5376]{0:T(1024)}, u32[]{:S(2)}) copy-start(f32[5376]{0:T(1024)} %param.10) | copy-start | bytes 64516
  315.5 7.4 %copy-start.6 = (f32[128]{0:T(128)S(1)}, f32[128]{0:T(128)}, u32[]{:S(2)}) copy-start(f32[128]{0:T(128)} %param.16) | copy-start | bytes 1540
  323.3 15.2 %slice-start = ((s8[5505024]{0:T(1024)(128)(4,1)}), s8[1310720]{0:T(1024)(128)(4,1)S(1)}, s32[]{:S(2)}) async-start(s8[5505024]{0:T(1024)(128)(4,1)} %bitcast.42), calls=%async_computation.3 | async-start | bytes 2621440
  323.6 14.9 %slice-start.1 = ((s8[5505024]{0:T(1024)(128)(4,1)}), s8[4194304]{0:T(1024)(128)(4,1)S(1)}, s32[]{:S(2)}) async-start(s8[5505024]{0:T(1024)(128)(4,1)} %bitcast.42), calls=%async_computation.4 | async-start | bytes 8388608
  331.0 7.5 %copy-start.2 = (bf16[1,512,512]{2,1,0:T(8,128)(2,1)}, bf16[1,512,512]{2,1,0:T(8,128)(2,1)S(1)}, u32[]{:S(2)}) copy-start(bf16[1,512,512]{2,1,0:T(8,128)(2,1)S(1)} %fusion.35) | copy-start | bytes 1572868
  332.1 23.4 %collective-permute-start.1 = (bf16[2,512,512]{2,1,0:T(8,128)(2,1)}, bf16[2,512,512]{2,1,0:T(8,128)(2,1)}, u32[]{:S(2)}, u32[]{:S(2)}) collective-permute-start(bf16[2,512,512]{2,1,0:T(8,128)(2,1)} %pad_maximum_fusion), channel_id=1, source_target_pairs={{0,2},{2,4},{4,6},{6,8},{8,10},{10,12},{12,14},{14,16},{16,18},{18... | collective-permute-start | bytes 3145736 | tf_op jit(solution)/shard_map/ppermute | solution.py:28
  335.0 35.5 %collective-permute-start = (bf16[2,512,512]{2,1,0:T(8,128)(2,1)}, bf16[2,512,512]{2,1,0:T(8,128)(2,1)}, u32[]{:S(2)}, u32[]{:S(2)}) collective-permute-start(bf16[2,512,512]{2,1,0:T(8,128)(2,1)} %pad_maximum_fusion), channel_id=1, source_target_pairs={{0,4},{2,6},{4,8},{6,10},{8,12},{10,14},{12,16},{14,18},{16,20},{1... | collective-permute-start | bytes 3145736 | tf_op jit(solution)/shard_map/ppermute | solution.py:28
  347.2 1.4 copy-start.7
  349.5 21.1 %copy-start.3 = (bf16[1,512,512]{2,1,0:T(8,128)(2,1)S(1)}, bf16[1,512,512]{2,1,0:T(8,128)(2,1)}, u32[]{:S(2)}) copy-start(bf16[1,512,512]{2,1,0:T(8,128)(2,1)} %copy-done.2) | copy-start | bytes 1572868
  374.5 13.5 %copy-start.1 = (bf16[512,8,64]{2,0,1:T(8,128)(2,1)S(1)}, bf16[512,8,64]{2,0,1:T(8,128)(2,1)}, u32[]{:S(2)}) copy-start(bf16[512,8,64]{2,0,1:T(8,128)(2,1)} %copy.49) | copy-start | bytes 1572868
  374.5 13.5 %copy-start.4 = (pred[512,1536]{0,1:T(8,128)(4,1)S(1)}, pred[512,1536]{0,1:T(8,128)(4,1)}, u32[]{:S(2)}) copy-start(pred[512,1536]{0,1:T(8,128)(4,1)} %fusion.23) | copy-start | bytes 2359300
  481.0 1.8 copy-start
  481.0 1.8 copy-start.5
Sparse Core Ops, SparseCore 0:
  9.0 74.0 all-gather.3
  84.8 194.4 all-gather.5
where the time goes:
time: 501 us; the launch traced here: 492 us
  waiting for transfers between devices  282 us (56%)
  matrix products  72 us (14%)
  blocking collectives  56.9 us (11%)
  local copies, waits for them, and re-layouts  43.2 us (9%)
  other arithmetic  18.2 us (4%)
  between operations  13.8 us (3%)
  starting transfers between devices  6.39 us (1%)
    all_gather x1, waiting for transfers between devices, in_one_piece(): result, at, outs = (lax.all_gather(both, axis, axis=dim, tiled=True), 0, [])  193 us
    all_gather x1, waiting for transfers between devices, on_device(): pair_rows = lax.all_gather(tokens, 'fsdp', axis=0, tiled=True)  70.6 us
    all_to_all x1, blocking collectives, sent_and_summed(): blocks = lax.all_to_all(in_blocks(x, dim, peers), axis, 0, 0, tiled=True)  56.9 us
    unnamed x24, local copies, waits for them, and re-layouts  38 us
    ppermute x2, waiting for transfers between devices, passed_along(): return lax.ppermute(block, axis, route)  17.9 us
    dot_general x1, matrix products, window_block(): jnp.einsum('kgrl,lkd->rkgd', weights, value_block, preferred_element_type...  14.2 us
    dot_general x1, matrix products, window_block(): jnp.einsum('rkgd,lkd->kgrl', query_block, key_block, preferred_element_ty...  13.5 us
    dot_general x1, matrix products, on_device(): lax.dot_general(attended, out_full, (((1,), (1,)), ((), ())), preferred_e...  10.4 us
  transfers between devices with their start and end apart: 4, of which 4 were waited for; matrix products, arithmetic and copies ran while one was open for 5% of the time, Pallas kernels for 0%

commit v1 on v0

v1 whole, which is shorter than its diff:
```python
import math

import jax
import jax.numpy as jnp
from jax import lax
from jax.experimental import pallas as pl
from jax.experimental.pallas import tpu as pltpu
from jax.sharding import Mesh, PartitionSpec as P

HEAD = 128
HALF = HEAD // 2
BLOCK = 256
WIDTH = 5376
AXES = ("x_lo", "y", "z", "core", "x_hi")
CHIPS = ("x_lo", "y", "z")
GATHER = ("x_hi", "x_lo", "y", "z")
epsilon = 1e-06
query_scale = 168.0 ** (-0.5) * math.log2(math.e)
rope_base = 10000.0
BF = jnp.bfloat16
F32 = jnp.float32
MIB = 1 << 20


def cost(flops, size, exps=0):
    return pl.CostEstimate(flops=int(flops), bytes_accessed=int(size), transcendentals=int(exps))


def params(mib):
    return pltpu.CompilerParams(vmem_limit_bytes=mib * MIB)


def turned(raw, gain, cosine, sine, scale):
    mean_square = jnp.mean(raw * raw, axis=-1, keepdims=True)
    unit = raw * (lax.rsqrt(mean_square + epsilon) * scale) * gain
    return unit * cosine + pltpu.roll(unit, HALF, axis=1) * sine


def key_value_kernel(x_ref, w_ref, gain_ref, cos_ref, sin_ref, out_ref):
    raw = jnp.dot(x_ref[...], w_ref[...], preferred_element_type=F32)

    @pl.when(pl.program_id(0) < 2)
    def _():
        for h in range(2):
            at = slice(h * HEAD, (h + 1) * HEAD)
            key = turned(raw[:, at], gain_ref[...], cos_ref[...], sin_ref[...], 1.0)
            out_ref[:, at] = key.astype(BF)

    @pl.when(pl.program_id(0) >= 2)
    def _():
        out_ref[...] = raw.astype(BF)


def query_kernel(x_ref, w_ref, gain_ref, cos_ref, sin_ref, out_ref):
    raw = jnp.dot(x_ref[...], w_ref[...], preferred_element_type=F32)
    for h in range(2):
        at = slice(h * HEAD, (h + 1) * HEAD)
        query = turned(raw[:, at], gain_ref[...], cos_ref[...], sin_ref[...], query_scale)
        out_ref[:, at] = query.astype(BF)


def projection(kernel, x, weights, gain, cosine, sine, where):
    rows = x.shape[0]
    whole = pl.BlockSpec(memory_space=pltpu.VMEM)
    return pl.pallas_call(
        kernel,
        out_shape=jax.ShapeDtypeStruct((rows, 1024), BF),
        grid=(4,),
        in_specs=[whole, pl.BlockSpec((WIDTH, 256), where), whole, whole, whole],
        out_specs=pl.BlockSpec((rows, 256), lambda t: (0, t)),
        compiler_params=params(48),
        cost_estimate=cost(2 * rows * WIDTH * 1024, 2 * WIDTH * 1536),
    )(x, weights, gain, cosine, sine)


def attention_kernel(flag_ref, q_ref, ok, ov, zk, zv, ak, av, bk, bv, ck, cv, out_ref):
    core = flag_ref[2]
    lane = lax.broadcasted_iota(jnp.int32, (BLOCK, HEAD), 1)
    ones = jnp.where(lane == 0, 1.0, 0.0).astype(F32)
    early = (ones * flag_ref[0].astype(F32)).astype(BF)
    before = (ones * flag_ref[1].astype(F32)).astype(BF)
    ones = ones.astype(BF)
    first, second = slice(0, BLOCK), slice(BLOCK, 2 * BLOCK)
    own0 = (ok.at[first], ov.at[first], ones)
    own1 = (ok.at[second], ov.at[second], ones)
    far = (zk.at[first], zv.at[first], early)
    mid = (zk.at[second], zv.at[second], early)
    prior = (ak, av, before)
    gap = (bk, bv, early)
    link = (ck, cv, ones)
    row = lax.rem(lax.broadcasted_iota(jnp.int32, (2 * BLOCK, BLOCK), 0), BLOCK)
    col = lax.broadcasted_iota(jnp.int32, (2 * BLOCK, BLOCK), 1)
    for part, keys in enumerate(((far, gap, mid, prior, own0), (mid, prior, own0, link, own1))):
        at = slice(part * BLOCK, (part + 1) * BLOCK)
        query = jnp.concatenate([q_ref[at, :HEAD], q_ref[at, HEAD:]], axis=0)
        total = jnp.zeros((2 * BLOCK, 2 * HEAD), F32)
        for n, (k, v, tail) in enumerate(keys):
            score = lax.dot_general(
                query, k[...], (((1,), (1,)), ((), ())), preferred_element_type=F32
            )
            raised = jnp.exp2(score)
            if n == 0:
                raised = jnp.where(col > row, raised, 0.0)
            if n == 4:
                raised = jnp.where(col <= row, raised, 0.0)
            value = jnp.concatenate([v[...], tail], axis=1)
            total += jnp.dot(raised.astype(BF), value, preferred_element_type=F32)
        mixed = (total[:, :HEAD] / total[:, HEAD : HEAD + 1]).astype(BF)
        to = pl.multiple_of(lax.rem(part + core, 2) * BLOCK, BLOCK)
        out_ref[pl.ds(to, BLOCK), :HEAD] = mixed[:BLOCK]
        out_ref[pl.ds(to, BLOCK), HEAD:] = mixed[BLOCK:]


def attention(flags, queries, own, behind, prior, gap, link):
    def pair(rows):
        return [
            pl.BlockSpec((rows, HEAD), lambda j: (0, j)),
            pl.BlockSpec((rows, HEAD), lambda j: (0, j + 4)),
        ]

    wide = pl.BlockSpec((2 * BLOCK, 2 * HEAD), lambda j: (0, j))
    return pl.pallas_call(
        attention_kernel,
        out_shape=jax.ShapeDtypeStruct((2 * BLOCK, 1024), BF),
        grid=(4,),
        in_specs=[pl.BlockSpec(memory_space=pltpu.SMEM), wide]
        + pair(512) + pair(512) + pair(256) + pair(256) + pair(256),
        out_specs=wide,
        compiler_params=params(32),
        cost_estimate=cost(8 * 512 * 1280 * 512, 6 * MIB, 8 * 512 * 1280),
    )(flags, queries, own, own, behind, behind, prior, prior, gap, gap, link, link)


def out_kernel(att_ref, low_ref, high_ref, own_ref, other_ref):
    dims = (((1,), (1,)), ((), ()))
    got = lax.dot_general(att_ref[:, :512], low_ref[...], dims, preferred_element_type=F32)
    got += lax.dot_general(att_ref[:, 512:], high_ref[...], dims, preferred_element_type=F32)
    own_ref[...] = got[:BLOCK]
    other_ref[...] = got[BLOCK:].astype(BF)


def out_projection(attended, weights, half):
    tile, steps = 896, 3
    first = half * steps
    return pl.pallas_call(
        out_kernel,
        out_shape=(
            jax.ShapeDtypeStruct((BLOCK, WIDTH // 2), F32),
            jax.ShapeDtypeStruct((BLOCK, WIDTH // 2), BF),
        ),
        grid=(steps,),
        in_specs=[
            pl.BlockSpec(memory_space=pltpu.VMEM),
            pl.BlockSpec((tile, 512), lambda i: (first + i, 0)),
            pl.BlockSpec((tile, 512), lambda i: (first + i + 2 * steps, 0)),
        ],
        out_specs=(
            pl.BlockSpec((BLOCK, tile), lambda i: (0, i)),
            pl.BlockSpec((BLOCK, tile), lambda i: (0, i)),
        ),
        compiler_params=params(32),
        cost_estimate=cost(2 * 512 * 1024 * WIDTH // 2, 10 * MIB),
    )(attended, weights, weights)


def end_kernel(tok_ref, own0, own1, got0, got1, gain_ref, out_ref):
    middle = WIDTH // 2
    left = own0[...] + got0[...].astype(F32)
    right = own1[...] + got1[...].astype(F32)
    square = jnp.sum(left * left, axis=-1, keepdims=True)
    square += jnp.sum(right * right, axis=-1, keepdims=True)
    factor = lax.rsqrt(square * (1.0 / WIDTH) + epsilon)
    for n, part in enumerate((left, right)):
        at = slice(n * middle, (n + 1) * middle)
        scaled = part * factor * gain_ref[:, at]
        out_ref[:, at] = (tok_ref[:, at].astype(F32) + scaled).astype(BF)


def ending(tokens, own0, own1, got0, got1, gain):
    rows = 64
    half = pl.BlockSpec((rows, WIDTH // 2), lambda i: (i, 0))
    wide = pl.BlockSpec((rows, WIDTH), lambda i: (i, 0))
    return pl.pallas_call(
        end_kernel,
        out_shape=jax.ShapeDtypeStruct((BLOCK, WIDTH), BF),
        grid=(BLOCK // rows,),
        in_specs=[wide, half, half, half, half, pl.BlockSpec((1, WIDTH), lambda i: (0, 0))],
        out_specs=wide,
        compiler_params=params(32),
        cost_estimate=cost(10 * BLOCK * WIDTH, 14 * MIB),
    )(tokens, own0, own1, got0, got1, gain)


def rotations(positions):
    exponents = jnp.arange(HALF, dtype=F32) * (2.0 / HEAD)
    frequency = jnp.exp(-exponents * jnp.log(jnp.float32(rope_base)))
    angles = positions.astype(F32)[:, None] * frequency[None, :]
    cosine, sine = jnp.cos(angles), jnp.sin(angles)
    return (
        jnp.concatenate([cosine, cosine], axis=1),
        jnp.concatenate([-sine, sine], axis=1),
    )


def quarter_rows(pieces):
    rows = pieces[0].shape[0]
    sides = [
        jnp.concatenate([p[:, s * p.shape[1] // 2 : (s + 1) * p.shape[1] // 2] for p in pieces], 1)
        for s in range(2)
    ]
    swapped = lax.all_to_all(jnp.stack(sides), "core", 0, 0, tiled=True)
    return swapped.reshape(2 * rows, -1)


def on_device(
    tokens,
    norm_gain,
    query_weight,
    key_matrix,
    value_matrix,
    out_weight,
    query_gain,
    key_gain,
    post_gain,
):
    core = lax.axis_index("core")
    side = lax.axis_index("x_hi")
    chip = lax.axis_index(CHIPS)
    qkv = lax.all_gather(
        quarter_rows([query_weight, key_matrix, value_matrix]), GATHER, axis=0, tiled=True
    )
    out_rows = quarter_rows([out_weight])

    plain = tokens.astype(F32)
    mean_square = jnp.mean(plain * plain, axis=-1, keepdims=True)
    normed = (plain * lax.rsqrt(mean_square + epsilon) * norm_gain).astype(BF)
    other = lax.ppermute(normed, "core", [(0, 1), (1, 0)])
    x = jnp.concatenate(
        [jnp.where(core == 0, normed, other), jnp.where(core == 0, other, normed)], axis=0
    )
    row = jnp.arange(2 * BLOCK, dtype=jnp.int32)
    positions = (4 * chip + side) * BLOCK + row + (row // BLOCK) * BLOCK
    cosine, sine = rotations(positions)

    qkv, out_rows = lax.optimization_barrier((qkv, out_rows))
    out_full = lax.all_gather(out_rows, GATHER, axis=0, tiled=True)

    own = projection(
        key_value_kernel, x, qkv, key_gain.reshape(1, HEAD), cosine, sine,
        lambda t: (lax.rem(t, 2), 2 + t // 2),
    )
    first, second = own[:BLOCK], own[BLOCK:]
    mine = jnp.where(side == 0, first, second)
    swap = jnp.where(side == 0, second, first)
    line = CHIPS + ("x_hi",)
    chips = 32
    prior = lax.ppermute(mine, line, [(i, i + 1) for i in range(2 * chips - 1)])
    gap = lax.ppermute(
        swap, line,
        [(2 * i + 1, 2 * i + 2) for i in range(chips - 1)]
        + [(2 * i, 2 * i + 3) for i in range(chips - 1)],
    )
    link = lax.ppermute(swap, "x_hi", [(0, 1), (1, 0)])
    behind = lax.ppermute(own, CHIPS, [(i, i + 1) for i in range(chips - 1)])
    queries = projection(
        query_kernel, x, qkv, query_gain.reshape(1, HEAD), cosine, sine,
        lambda t: (t // 2, lax.rem(t, 2)),
    )
    later = (chip > 0).astype(jnp.int32)
    flags = jnp.stack([later, jnp.maximum(later, side), core]).astype(jnp.int32)
    attended = attention(flags, queries, own, behind, prior, gap, link)
    own0, send0 = out_projection(attended, out_full, 0)
    got0 = lax.ppermute(send0, "core", [(0, 1), (1, 0)])
    own1, send1 = out_projection(attended, out_full, 1)
    got1 = lax.ppermute(send1, "core", [(0, 1), (1, 0)])
    return ending(tokens, own0, own1, got0, got1, post_gain.reshape(1, WIDTH))


def solution(mesh):
    spread = Mesh(mesh.devices.reshape(2, 4, 4, 2, 2), AXES)
    whole = P(AXES, None)
    rows = P(AXES[:4], "x_hi")
    return jax.shard_map(
        on_device,
        mesh=spread,
        in_specs=(whole, P(), rows, rows, rows, rows, P(), P(), P()),
        out_specs=whole,
        check_vma=False,
    )
```

time: 501 us -> 293 us (0.58)
  waiting for transfers between devices: 282 us -> 186 us
  matrix products: 72 us -> 0 us
  blocking collectives: 56.9 us -> 8.19 us
  Pallas kernels: 0 us -> 44.6 us
  local copies, waits for them, and re-layouts: 43.2 us -> 10.6 us
  starting transfers between devices: 6.39 us -> 14.2 us
  other arithmetic: 18.2 us -> 11.5 us
    all_gather x2, waiting for transfers between devices: 263 us -> 142 us  [the longest x1 115 us: on_device(): lax.all_gather(quarter_rows([query_weight, key_matrix, value_matrix]), GA...]
    dot_general x6 -> x0, matrix products: 61.6 us -> none  [the longest x1 14.2 us: window_block(): jnp.einsum('kgrl,lkd->rkgd', weights, value_block, preferred_element_type...]
    all_to_all x1 -> x2, blocking collectives: 56.9 us -> 8.19 us  [quarter_rows(): swapped = lax.all_to_all(jnp.stack(sides), 'core', 0, 0, tiled=True)]
    pallas_call x0 -> x6, Pallas kernels: none -> 44.6 us  [the longest x2 23.8 us: projection(): pl.pallas_call(kernel, out_shape=jax.ShapeDtypeStruct((rows, 1024), BF),...]
    unnamed x24 -> x18, local copies, waits for them, and re-layouts: 38 us -> 6.34 us
    ppermute x2 -> x7, waiting for transfers between devices: 17.9 us -> 43.7 us  [the longest x1 36.8 us: on_device(): prior = lax.ppermute(mine, line, [(i, i + 1) for i in range(2 * chips - 1)])]
    sub x1 -> x0, matrix products: 10.4 us -> none  [window_block(): raised = jnp.exp(scores - highest)]
    ppermute x2 -> x7, starting transfers between devices: 6.35 us -> 14.2 us  [the longest x1 4.16 us: on_device(): behind = lax.ppermute(own, CHIPS, [(i, i + 1) for i in range(chips - 1)])]
  transfers between devices with their start and end apart: 4 -> 9, of which waited for: 4 -> 5; matrix products, arithmetic and copies ran while one was open for 5% -> 4% of each run, Pallas kernels for 0% -> 13%
where the time goes in v1:
time: 293 us; the launch traced here: 289 us
  waiting for transfers between devices  186 us (63%)
  Pallas kernels  44.6 us (15%)
  starting transfers between devices  14.2 us (5%)
  between operations  13.6 us (5%)
  other arithmetic  11.5 us (4%)
  local copies, waits for them, and re-layouts  10.6 us (4%)
  blocking collectives  8.19 us (3%)
    all_gather x1, waiting for transfers between devices, on_device(): lax.all_gather(quarter_rows([query_weight, key_matrix, value_matrix]), GA...  115 us
    ppermute x1, waiting for transfers between devices, on_device(): prior = lax.ppermute(mine, line, [(i, i + 1) for i in range(2 * chips - 1)])  36.8 us
    all_gather x1, waiting for transfers between devices, on_device(): out_full = lax.all_gather(out_rows, GATHER, axis=0, tiled=True)  27.2 us
    pallas_call x2, Pallas kernels, projection(): pl.pallas_call(kernel, out_shape=jax.ShapeDtypeStruct((rows, 1024), BF),...  23.8 us
    pallas_call x1, Pallas kernels, attention(): pl.pallas_call(attention_kernel, out_shape=jax.ShapeDtypeStruct((2 * BLOC...  9.2 us
    pallas_call x2, Pallas kernels, out_projection(): pl.pallas_call(out_kernel, out_shape=(jax.ShapeDtypeStruct((BLOCK, WIDTH...  8.24 us
    all_to_all x2, blocking collectives, quarter_rows(): swapped = lax.all_to_all(jnp.stack(sides), 'core', 0, 0, tiled=True)  8.19 us
    unnamed x18, local copies, waits for them, and re-layouts  6.34 us
  transfers between devices with their start and end apart: 9, of which 5 were waited for; matrix products, arithmetic and copies ran while one was open for 4% of the time, Pallas kernels for 13%

profile of v1, /device:TPU:125, one launch (start us, length us, event | category | flops | bytes accessed | tf_op | source)
XLA Modules:
  0.0 288.8 jit_solution(9108424639700348468)
XLA Ops:
  6.5 0.0 copy-start.6
  6.5 0.0 copy-start.1
  6.5 0.0 all-gather.3.cloned.1.call-start
  6.5 1.0 fusion.12
  7.5 0.8 fusion.11
  8.3 0.9 fusion.10
  9.4 4.3 %all_to_all.10 = bf16[2,84,1024]{2,1,0:T(8,128)(2,1)S(1)} all-to-all(bf16[2,84,1024]{2,1,0:T(8,128)(2,1)S(1)} %pad_maximum_fusion.1), channel_id=1, replica_groups=mesh['x_lo'=2,'y'=4,'z'=4,'core'=2,'x_hi'=2] {'core'}, dimensions={0} | all-to-all | bytes 688128 | tf_op jit(solution)/shard_map/all_to_all | solution.py:211
  13.7 0.0 copy-start.7
  13.7 0.8 reshape.49
  14.5 0.0 all-gather.3.cloned.1.call-update
  14.5 0.0 all-gather.5.cloned.1.call-start
  14.6 0.0 copy-done.6
  14.6 3.9 %all_to_all.11 = bf16[2,84,512]{2,1,0:T(8,128)(2,1)S(1)} all-to-all(bf16[2,84,512]{2,1,0:T(8,128)(2,1)S(1)} %pad_maximum_fusion.4), channel_id=1, replica_groups=mesh['x_lo'=2,'y'=4,'z'=4,'core'=2,'x_hi'=2] {'core'}, dimensions={0} | all-to-all | bytes 344064 | tf_op jit(solution)/shard_map/all_to_all | solution.py:211
  18.5 0.7 reshape.50
  19.2 115.1 %all-gather.3.cloned.1.call-done.w_ref = bf16[10752,1024]{1,0:T(8,128)(2,1)} async-done(((bf16[168,1024]{1,0:T(8,128)(2,1)}), bf16[10752,1024]{1,0:T(8,128)(2,1)}) %all-gather.3.cloned.1.call-update) | async-done | bytes 22020112 | tf_op jit(solution)/shard_map/all_gather | solution.py:229
  134.4 0.0 all-gather.5.cloned.1.call-update
  134.4 0.0 copy-done.1
  134.4 0.6 fusion
  135.0 0.0 copy-done.7
  135.0 2.3 fusion.2
  137.3 0.7 collective-permute-start
  138.0 1.0 fusion.3
  139.0 0.2 pad_maximum_fusion.2
  139.2 3.8 %collective-permute-done = bf16[256,5376]{1,0:T(8,128)(2,1)} collective-permute-done((bf16[256,5376]{1,0:T(8,128)(2,1)}, bf16[256,5376]{1,0:T(8,128)(2,1)}, u32[]{:S(2)}, u32[]{:S(2)}) %collective-permute-start) | collective-permute-done | bytes 2752544 | tf_op jit(solution)/shard_map/ppermute | solution.py:237
  143.0 3.2 %broadcast_select_fusion.1 = (bf16[256,5376]{1,0:T(8,128)(2,1)S(1)}, bf16[256,5376]{1,0:T(8,128)(2,1)S(1)}) fusion(bf16[256,5376]{1,0:T(8,128)(2,1)} %collective-permute-done, pred[]{:T(512)S(6)} %eq.8, f32[5376]{0:T(1024)S(1)} %copy-done.7, f32[256]{0:T(256)S(1)} %add_rsqrt_fusion, bf16[256,5376]{1,0:T(8,128)(2,1)S(1)} %copy-done.1), kind=kLoop, calls=%fused_computation.7 | loop fusion | flops 8257536 | bytes 11032577 | tf_op jit(solution)/shard_map/jit(_where)/select_n | solution.py:239
  146.2 0.0 copy-start.4
  146.2 2.8 pad_maximum_fusion.x_ref
  149.0 0.0 copy-done.4
  149.0 0.0 copy-start.5
  149.0 11.7 %shard_map.92.ok.ov = bf16[512,1024]{1,0:T(8,128)(2,1)} custom-call(bf16[512,5376]{1,0:T(8,128)(2,1)} %pad_maximum_fusion.x_ref, bf16[10752,1024]{1,0:T(8,128)(2,1)} %all-gather.3.cloned.1.call-done.w_ref, f32[1,128]{1,0:T(1,128)S(1)} %bitcast.13, f32[512,128]{1,0:T(8,128)S(1)} %get-tuple-element.34.cos_ref, f32[512,128]{1,0:T(8,128)S(1)} %get-tuple-element.35.sin_ref), custom_call_target="tpu_custom_call" | custom-call | flops 5637144576 | bytes 16515072 | tf_op jit(solution)/shard_map/pallas_call | solution.py:65
  160.8 4.2 %collective-permute-start.1 = (bf16[512,1024]{1,0:T(8,128)(2,1)}, bf16[512,1024]{1,0:T(8,128)(2,1)}, u32[]{:S(2)}, u32[]{:S(2)}) collective-permute-start(bf16[512,1024]{1,0:T(8,128)(2,1)} %shard_map.92.ok.ov), channel_id=1, source_target_pairs={{0,4},{4,8},{8,12},{12,16},{16,20},{20,24},{24,28},{28,32},{32,36}... | collective-permute-start | bytes 3145736 | tf_op jit(solution)/shard_map/ppermute | solution.py:264
  165.0 0.1 pad_add_fusion.flag_ref
  165.0 1.3 broadcast_select_fusion.2
  166.3 2.3 collective-permute-start.3
  168.7 2.5 collective-permute-start.4
  171.1 3.6 %collective-permute-start.2 = (bf16[256,1024]{1,0:T(8,128)(2,1)S(1)}, bf16[256,1024]{1,0:T(8,128)(2,1)S(1)}, u32[]{:S(2)}, u32[]{:S(2)}) collective-permute-start(bf16[256,1024]{1,0:T(8,128)(2,1)S(1)} %get-tuple-element.20), channel_id=1, source_target_pairs={{0,1},{1,4},{4,5},{5,8},{8,9},{9,12},{12,13},{13,16},{16,17},{17,2... | collective-permute-start | bytes 1572872 | tf_op jit(solution)/shard_map/ppermute | solution.py:257
  174.8 0.0 copy-done.5
  174.8 12.0 %shard_map.91.q_ref = bf16[512,1024]{1,0:T(8,128)(2,1)S(1)} custom-call(bf16[512,5376]{1,0:T(8,128)(2,1)} %pad_maximum_fusion.x_ref, bf16[10752,1024]{1,0:T(8,128)(2,1)} %all-gather.3.cloned.1.call-done.w_ref, f32[1,128]{1,0:T(1,128)S(1)} %bitcast.14, f32[512,128]{1,0:T(8,128)S(1)} %get-tuple-element.34.cos_ref, f32[512,128]{1,0:T(8,128)S(1)} %get-tuple-element.35.sin_ref), custom_call_target="tpu_custom_call" | custom-call | flops 5637144576 | bytes 16515072 | tf_op jit(solution)/shard_map/pallas_call | solution.py:65
  186.8 36.8 %collective-permute-done.2.ak.av = bf16[256,1024]{1,0:T(8,128)(2,1)S(1)} collective-permute-done((bf16[256,1024]{1,0:T(8,128)(2,1)S(1)}, bf16[256,1024]{1,0:T(8,128)(2,1)S(1)}, u32[]{:S(2)}, u32[]{:S(2)}) %collective-permute-start.2) | collective-permute-done | bytes 524320 | tf_op jit(solution)/shard_map/ppermute | solution.py:257
  223.6 0.0 collective-permute-done.3.bk.bv
  223.6 0.0 collective-permute-done.4.ck.cv
  223.6 0.0 collective-permute-done.1.zk.zv
  223.6 9.2 %shard_map.93.att_ref = bf16[512,1024]{1,0:T(8,128)(2,1)S(1)} custom-call(s32[3]{0:T(128)S(1)} %pad_add_fusion.flag_ref, bf16[512,1024]{1,0:T(8,128)(2,1)S(1)} %shard_map.91.q_ref, bf16[512,1024]{1,0:T(8,128)(2,1)} %shard_map.92.ok.ov, bf16[512,1024]{1,0:T(8,128)(2,1)} %shard_map.92.ok.ov, bf16[512,1024]{1,0:T(8,128)(2,1)} %collective-permute-done.1.zk.zv, ...), custom_call_target="tpu_custom_call" | custom-call | flops 2684354560 | bytes 6291456 | tf_op jit(solution)/shard_map/pallas_call | solution.py:122
  232.8 0.0 copy-start.2
  232.8 1.0 copy-done.2
  233.8 27.2 %all-gather.5.cloned.1.call-done.low_ref.high_ref = bf16[10752,512]{1,0:T(8,128)(2,1)} async-done(((bf16[168,512]{1,0:T(8,128)(2,1)}), bf16[10752,512]{1,0:T(8,128)(2,1)}) %all-gather.5.cloned.1.call-update) | async-done | bytes 11010064 | tf_op jit(solution)/shard_map/all_gather | solution.py:246
  261.0 0.0 copy-start
  261.0 4.1 %copy-done = bf16[10752,512]{1,0:T(8,128)(2,1)S(1)} copy-done((bf16[10752,512]{1,0:T(8,128)(2,1)S(1)}, bf16[10752,512]{1,0:T(8,128)(2,1)}, u32[]{:S(2)}) %copy-start) | copy-done | bytes 11010072
  265.1 0.0 copy-start.3
  265.1 1.2 copy-done.3
  266.3 4.1 %shard_map.94 = (f32[256,2688]{1,0:T(8,128)S(1)}, bf16[256,2688]{1,0:T(8,128)(2,1)S(1)}) custom-call(bf16[512,1024]{1,0:T(8,128)(2,1)S(1)} %copy-done.3, bf16[10752,512]{1,0:T(8,128)(2,1)S(1)} %copy-done, bf16[10752,512]{1,0:T(8,128)(2,1)S(1)} %copy-done), custom_call_target="tpu_custom_call" | custom-call | flops 2818572288 | bytes 10485760 | tf_op jit(solution)/shard_map/pallas_call | solution.py:145
  270.5 0.0 copy-start.8
  270.5 0.8 collective-permute-start.5
  271.2 4.1 %shard_map.95 = (f32[256,2688]{1,0:T(8,128)S(1)}, bf16[256,2688]{1,0:T(8,128)(2,1)S(1)}) custom-call(bf16[512,1024]{1,0:T(8,128)(2,1)S(1)} %copy-done.3, bf16[10752,512]{1,0:T(8,128)(2,1)S(1)} %copy-done, bf16[10752,512]{1,0:T(8,128)(2,1)S(1)} %copy-done), custom_call_target="tpu_custom_call" | custom-call | flops 2818572288 | bytes 10485760 | tf_op jit(solution)/shard_map/pallas_call | solution.py:145
  275.4 0.1 collective-permute-start.6
  275.5 0.0 copy-done.8
  275.5 0.0 collective-permute-done.5.got0
  275.5 3.1 %collective-permute-done.6.got1 = bf16[256,2688]{1,0:T(8,128)(2,1)S(1)} collective-permute-done((bf16[256,2688]{1,0:T(8,128)(2,1)S(1)}, bf16[256,2688]{1,0:T(8,128)(2,1)S(1)}, u32[]{:S(2)}, u32[]{:S(2)}) %collective-permute-start.6) | collective-permute-done | bytes 1376288 | tf_op jit(solution)/shard_map/ppermute | solution.py:275
  278.6 3.4 %shard_map.96 = bf16[256,5376]{1,0:T(8,128)(2,1)} custom-call(bf16[256,5376]{1,0:T(8,128)(2,1)S(1)} %copy-done.1, f32[256,2688]{1,0:T(8,128)S(1)} %get-tuple-element.13.own0, f32[256,2688]{1,0:T(8,128)S(1)} %get-tuple-element.14.own1, bf16[256,2688]{1,0:T(8,128)(2,1)S(1)} %collective-permute-done.5.got0, bf16[256,2688]{1,0:T(8,128)(2,1)S(1)} %collective-permute-done.6.got1, ...), custom_call_target="tpu_custom_call" | custom-call | flops 13762560 | bytes 14680064 | tf_op jit(solution)/shard_map/pallas_call | solution.py:183
  (8 shorter events, 0.1 us)
Async XLA Ops:
  6.5 8.0 %copy-start.6 = (bf16[84,1024]{1,0:T(8,128)(2,1)S(1)}, bf16[84,1024]{1,0:T(8,128)(2,1)}, u32[]{:S(2)}) copy-start(bf16[84,1024]{1,0:T(8,128)(2,1)} %param.14) | copy-start | bytes 516100
  6.5 127.8 %copy-start.1 = (bf16[256,5376]{1,0:T(8,128)(2,1)S(1)}, bf16[256,5376]{1,0:T(8,128)(2,1)}, u32[]{:S(2)}) copy-start(bf16[256,5376]{1,0:T(8,128)(2,1)} %tok_ref.1) | copy-start | bytes 8257540
  6.5 127.8 %all-gather.3.cloned.1.call-start = ((), (), s32[]{:S(2)}) async-start(), calls=%async_computation.2 | async-start | bytes 22364160 | tf_op jit(solution)/shard_map/all_gather | solution.py:229
  13.7 121.3 %copy-start.7 = (f32[5376]{0:T(1024)S(1)}, f32[5376]{0:T(1024)}, u32[]{:S(2)}) copy-start(f32[5376]{0:T(1024)} %param.10) | copy-start | bytes 64516
  14.5 246.5 %all-gather.5.cloned.1.call-start = ((), (), s32[]{:S(2)}) async-start(), calls=%async_computation.3 | async-start | bytes 11182080 | tf_op jit(solution)/shard_map/all_gather | solution.py:246
  137.3 5.7 %collective-permute-start = (bf16[256,5376]{1,0:T(8,128)(2,1)}, bf16[256,5376]{1,0:T(8,128)(2,1)}, u32[]{:S(2)}, u32[]{:S(2)}) collective-permute-start(bf16[256,5376]{1,0:T(8,128)(2,1)} %fusion.2), channel_id=1, source_target_pairs={{0,2},{2,0},{1,3},{3,1},{4,6},{6,4},{5,7},{7,5},{8,10},{10,8},{9,1... | collective-permute-start | bytes 8257544 | tf_op jit(solution)/shard_map/ppermute | solution.py:237
  146.2 2.8 copy-start.4
  149.0 25.8 %copy-start.5 = (f32[128]{0:T(128)S(1)}, f32[128]{0:T(128)}, u32[]{:S(2)}) copy-start(f32[128]{0:T(128)} %param.15) | copy-start | bytes 1540
  160.8 62.8 %collective-permute-start.1 = (bf16[512,1024]{1,0:T(8,128)(2,1)}, bf16[512,1024]{1,0:T(8,128)(2,1)}, u32[]{:S(2)}, u32[]{:S(2)}) collective-permute-start(bf16[512,1024]{1,0:T(8,128)(2,1)} %shard_map.92.ok.ov), channel_id=1, source_target_pairs={{0,4},{4,8},{8,12},{12,16},{16,20},{20,24},{24,28},{28,32},{32,36}... | collective-permute-start | bytes 3145736 | tf_op jit(solution)/shard_map/ppermute | solution.py:264
  166.3 57.3 %collective-permute-start.3 = (bf16[256,1024]{1,0:T(8,128)(2,1)S(1)}, bf16[256,1024]{1,0:T(8,128)(2,1)S(1)}, u32[]{:S(2)}, u32[]{:S(2)}) collective-permute-start(bf16[256,1024]{1,0:T(8,128)(2,1)S(1)} %get-tuple-element.19), channel_id=1, source_target_pairs={{1,4},{5,8},{9,12},{13,16},{17,20},{21,24},{25,28},{29,32},{33,36}... | collective-permute-start | bytes 1572872 | tf_op jit(solution)/shard_map/ppermute | solution.py:258
  168.7 55.0 %collective-permute-start.4 = (bf16[256,1024]{1,0:T(8,128)(2,1)S(1)}, bf16[256,1024]{1,0:T(8,128)(2,1)S(1)}, u32[]{:S(2)}, u32[]{:S(2)}) collective-permute-start(bf16[256,1024]{1,0:T(8,128)(2,1)S(1)} %get-tuple-element.19), channel_id=1, source_target_pairs={{0,1},{1,0},{2,3},{3,2},{4,5},{5,4},{6,7},{7,6},{8,9},{9,8},{10,11... | collective-permute-start | bytes 1572872 | tf_op jit(solution)/shard_map/ppermute | solution.py:263
  171.1 52.5 %collective-permute-start.2 = (bf16[256,1024]{1,0:T(8,128)(2,1)S(1)}, bf16[256,1024]{1,0:T(8,128)(2,1)S(1)}, u32[]{:S(2)}, u32[]{:S(2)}) collective-permute-start(bf16[256,1024]{1,0:T(8,128)(2,1)S(1)} %get-tuple-element.20), channel_id=1, source_target_pairs={{0,1},{1,4},{4,5},{5,8},{8,9},{9,12},{12,13},{13,16},{16,17},{17,2... | collective-permute-start | bytes 1572872 | tf_op jit(solution)/shard_map/ppermute | solution.py:257
  232.8 1.0 copy-start.2
  261.0 4.1 %copy-start = (bf16[10752,512]{1,0:T(8,128)(2,1)S(1)}, bf16[10752,512]{1,0:T(8,128)(2,1)}, u32[]{:S(2)}) copy-start(bf16[10752,512]{1,0:T(8,128)(2,1)} %all-gather.5.cloned.1.call-done.low_ref.high_ref) | copy-start | bytes 33030148
  265.1 1.2 copy-start.3
  270.5 5.0 %copy-start.8 = (f32[5376]{0:T(1024)S(1)}, f32[5376]{0:T(1024)}, u32[]{:S(2)}) copy-start(f32[5376]{0:T(1024)} %param.17) | copy-start | bytes 64516
  270.5 5.0 %collective-permute-start.5 = (bf16[256,2688]{1,0:T(8,128)(2,1)S(1)}, bf16[256,2688]{1,0:T(8,128)(2,1)S(1)}, u32[]{:S(2)}, u32[]{:S(2)}) collective-permute-start(bf16[256,2688]{1,0:T(8,128)(2,1)S(1)} %get-tuple-element.15), channel_id=1, source_target_pairs={{0,2},{2,0},{1,3},{3,1},{4,6},{6,4},{5,7},{7,5},{8,10},{10,8},{9,1... | collective-permute-start | bytes 4128776 | tf_op jit(solution)/shard_map/ppermute | solution.py:273
  275.4 3.2 %collective-permute-start.6 = (bf16[256,2688]{1,0:T(8,128)(2,1)S(1)}, bf16[256,2688]{1,0:T(8,128)(2,1)S(1)}, u32[]{:S(2)}, u32[]{:S(2)}) collective-permute-start(bf16[256,2688]{1,0:T(8,128)(2,1)S(1)} %get-tuple-element.16), channel_id=1, source_target_pairs={{0,2},{2,0},{1,3},{3,1},{4,6},{6,4},{5,7},{7,5},{8,10},{10,8},{9,1... | collective-permute-start | bytes 4128776 | tf_op jit(solution)/shard_map/ppermute | solution.py:275
Sparse Core Ops, SparseCore 0:
  14.6 119.6 all-gather.2
  137.2 123.7 all-gather.4

commit v2 on v1

--- a/solution.py
+++ b/solution.py
@@ -151,8 +151,8 @@
         grid=(steps,),
         in_specs=[
             pl.BlockSpec(memory_space=pltpu.VMEM),
-            pl.BlockSpec((tile, 512), lambda i: (first + i, 0)),
-            pl.BlockSpec((tile, 512), lambda i: (first + i + 2 * steps, 0)),
+            pl.BlockSpec((tile, 512), lambda i: (first + i, 2)),
+            pl.BlockSpec((tile, 512), lambda i: (first + i + 2 * steps, 2)),
         ],
         out_specs=(
             pl.BlockSpec((BLOCK, tile), lambda i: (0, i)),
@@ -226,10 +226,12 @@
     core = lax.axis_index("core")
     side = lax.axis_index("x_hi")
     chip = lax.axis_index(CHIPS)
-    qkv = lax.all_gather(
-        quarter_rows([query_weight, key_matrix, value_matrix]), GATHER, axis=0, tiled=True
-    )
-    out_rows = quarter_rows([out_weight])
+    full = lax.all_gather(
+        quarter_rows([query_weight, key_matrix, value_matrix, out_weight]),
+        GATHER,
+        axis=0,
+        tiled=True,
+    )
 
     plain = tokens.astype(F32)
     mean_square = jnp.mean(plain * plain, axis=-1, keepdims=True)
@@ -242,11 +244,10 @@
     positions = (4 * chip + side) * BLOCK + row + (row // BLOCK) * BLOCK
     cosine, sine = rotations(positions)
 
-    qkv, out_rows = lax.optimization_barrier((qkv, out_rows))
-    out_full = lax.all_gather(out_rows, GATHER, axis=0, tiled=True)
+    full, x, cosine, sine = lax.optimization_barrier((full, x, cosine, sine))
 
     own = projection(
-        key_value_kernel, x, qkv, key_gain.reshape(1, HEAD), cosine, sine,
+        key_value_kernel, x, full, key_gain.reshape(1, HEAD), cosine, sine,
         lambda t: (lax.rem(t, 2), 2 + t // 2),
     )
     first, second = own[:BLOCK], own[BLOCK:]
@@ -263,15 +264,15 @@
     link = lax.ppermute(swap, "x_hi", [(0, 1), (1, 0)])
     behind = lax.ppermute(own, CHIPS, [(i, i + 1) for i in range(chips - 1)])
     queries = projection(
-        query_kernel, x, qkv, query_gain.reshape(1, HEAD), cosine, sine,
+        query_kernel, x, full, query_gain.reshape(1, HEAD), cosine, sine,
         lambda t: (t // 2, lax.rem(t, 2)),
     )
     later = (chip > 0).astype(jnp.int32)
     flags = jnp.stack([later, jnp.maximum(later, side), core]).astype(jnp.int32)
     attended = attention(flags, queries, own, behind, prior, gap, link)
-    own0, send0 = out_projection(attended, out_full, 0)
+    own0, send0 = out_projection(attended, full, 0)
     got0 = lax.ppermute(send0, "core", [(0, 1), (1, 0)])
-    own1, send1 = out_projection(attended, out_full, 1)
+    own1, send1 = out_projection(attended, full, 1)
     got1 = lax.ppermute(send1, "core", [(0, 1), (1, 0)])
     return ending(tokens, own0, own1, got0, got1, post_gain.reshape(1, WIDTH))
 

time: 293 us -> 280 us (0.956); the launches traced: 289 us -> 279 us
  local copies, waits for them, and re-layouts: 10.6 us -> 4.62 us
  blocking collectives: 8.19 us -> 4.44 us
  Pallas kernels: 44.6 us -> 47.7 us
  waiting for transfers between devices: 186 us -> 183 us
    unnamed x18 -> x10, local copies, waits for them, and re-layouts: 6.34 us -> 0.03 us
    ppermute x1, waiting for transfers between devices: 36.8 us -> 30.7 us  [on_device(): prior = lax.ppermute(mine, line, [(i, i + 1) for i in range(2 * chips - 1)])]
    all_to_all x2 -> x1, blocking collectives: 8.19 us -> 4.44 us  [quarter_rows(): swapped = lax.all_to_all(jnp.stack(sides), 'core', 0, 0, tiled=True)]
    pallas_call x2, Pallas kernels: 8.24 us -> 11.4 us  [out_projection(): pl.pallas_call(out_kernel, out_shape=(jax.ShapeDtypeStruct((BLOCK, WIDTH...]
    all_gather x2 -> x1, waiting for transfers between devices: 142 us -> 143 us  [on_device(): lax.all_gather(quarter_rows([query_weight, key_matrix, value_matrix, out_...]
  transfers between devices with their start and end apart: 9 -> 8, of which waited for: 5 -> 5; matrix products, arithmetic and copies ran while one was open for 4% -> 4% of each run, Pallas kernels for 13% -> 4%
where the time goes in v2:
time: 280 us; the launch traced here: 279 us
  waiting for transfers between devices  183 us (65%)
  Pallas kernels  47.7 us (17%)
  starting transfers between devices  14.8 us (5%)
  between operations  13.6 us (5%)
  other arithmetic  11.5 us (4%)
  local copies, waits for them, and re-layouts  4.62 us (2%)
  blocking collectives  4.44 us (2%)
    all_gather x1, waiting for transfers between devices, on_device(): lax.all_gather(quarter_rows([query_weight, key_matrix, value_matrix, out_...  143 us
    ppermute x1, waiting for transfers between devices, on_device(): prior = lax.ppermute(mine, line, [(i, i + 1) for i in range(2 * chips - 1)])  30.7 us
    pallas_call x2, Pallas kernels, projection(): pl.pallas_call(kernel, out_shape=jax.ShapeDtypeStruct((rows, 1024), BF),...  23.6 us
    pallas_call x2, Pallas kernels, out_projection(): pl.pallas_call(out_kernel, out_shape=(jax.ShapeDtypeStruct((BLOCK, WIDTH...  11.4 us
    pallas_call x1, Pallas kernels, attention(): pl.pallas_call(attention_kernel, out_shape=jax.ShapeDtypeStruct((2 * BLOC...  9.21 us
  transfers between devices with their start and end apart: 8, of which 5 were waited for; matrix products, arithmetic and copies ran while one was open for 4% of the time, Pallas kernels for 4%

profile of v2, /device:TPU:125, one launch (start us, length us, event | category | flops | bytes accessed | tf_op | source)
XLA Modules:
  0.0 279.3 jit_solution(2352670608430735469)
XLA Ops:
  6.5 0.0 all-gather.2.cloned.1.call-start
  6.5 0.9 fusion.11
  7.5 0.0 copy-start
  7.5 1.0 fusion.13
  8.5 0.8 fusion.12
  9.3 0.9 fusion.10
  10.3 0.1 pad_maximum_fusion.1
  10.3 0.0 copy-start.3
  10.4 4.4 %all_to_all.5 = bf16[2,84,1536]{2,1,0:T(8,128)(2,1)S(1)} all-to-all(bf16[2,84,1536]{2,1,0:T(8,128)(2,1)S(1)} %pad_maximum_fusion.1), channel_id=1, replica_groups=mesh['x_lo'=2,'y'=4,'z'=4,'core'=2,'x_hi'=2] {'core'}, dimensions={0} | all-to-all | bytes 1032192 | tf_op jit(solution)/shard_map/all_to_all | solution.py:211
  14.8 0.9 reshape.46
  15.7 0.0 all-gather.2.cloned.1.call-update
  15.7 0.0 copy-done
  15.7 0.6 fusion
  16.4 0.0 copy-done.3
  16.4 2.3 fusion.2
  18.6 0.4 collective-permute-start
  19.0 1.0 fusion.3
  20.0 0.2 pad_maximum_fusion.2
  20.2 3.8 %collective-permute-done = bf16[256,5376]{1,0:T(8,128)(2,1)} collective-permute-done((bf16[256,5376]{1,0:T(8,128)(2,1)}, bf16[256,5376]{1,0:T(8,128)(2,1)}, u32[]{:S(2)}, u32[]{:S(2)}) %collective-permute-start) | collective-permute-done | bytes 2752544 | tf_op jit(solution)/shard_map/ppermute | solution.py:239
  24.1 3.2 %broadcast_select_fusion.1 = (bf16[256,5376]{1,0:T(8,128)(2,1)S(1)}, bf16[256,5376]{1,0:T(8,128)(2,1)S(1)}) fusion(bf16[256,5376]{1,0:T(8,128)(2,1)} %collective-permute-done, pred[]{:T(512)S(6)} %eq.8, f32[5376]{0:T(1024)S(1)} %copy-done.3, f32[256]{0:T(256)S(1)} %add_rsqrt_fusion, bf16[256,5376]{1,0:T(8,128)(2,1)S(1)} %copy-done), kind=kLoop, calls=%fused_computation.7 | loop fusion | flops 8257536 | bytes 11032577 | tf_op jit(solution)/shard_map/jit(_where)/select_n | solution.py:241
  27.2 0.0 copy-start.1
  27.2 2.8 %pad_maximum_fusion.x_ref = bf16[512,5376]{1,0:T(8,128)(2,1)} fusion(bf16[256,5376]{1,0:T(8,128)(2,1)S(1)} %get-tuple-element.22, bf16[256,5376]{1,0:T(8,128)(2,1)S(1)} %get-tuple-element.21), kind=kLoop, calls=%fused_computation.5 | loop fusion | flops 11010048 | bytes 11010048 | tf_op jit(solution)/shard_map/concatenate | solution.py:240
  30.1 143.5 %all-gather.2.cloned.1.call-done.w_ref.low_ref.high_ref = bf16[10752,1536]{1,0:T(8,128)(2,1)} async-done(((bf16[168,1536]{1,0:T(8,128)(2,1)}), bf16[10752,1536]{1,0:T(8,128)(2,1)}) %all-gather.2.cloned.1.call-update) | async-done | bytes 33030160 | tf_op jit(solution)/shard_map/all_gather | solution.py:229
  173.5 0.0 copy-done.1
  173.5 0.0 copy-start.2
  173.5 11.7 %shard_map.92.ok.ov = bf16[512,1024]{1,0:T(8,128)(2,1)} custom-call(bf16[512,5376]{1,0:T(8,128)(2,1)} %pad_maximum_fusion.x_ref, bf16[10752,1536]{1,0:T(8,128)(2,1)} %all-gather.2.cloned.1.call-done.w_ref.low_ref.high_ref, f32[1,128]{1,0:T(1,128)S(1)} %bitcast.9, f32[512,128]{1,0:T(8,128)S(1)} %get-tuple-element.15.cos_ref, ...), custom_call_target="tpu_custom_call" | custom-call | flops 5637144576 | bytes 16515072 | tf_op jit(solution)/shard_map/pallas_call | solution.py:65
  185.2 4.2 %collective-permute-start.1 = (bf16[512,1024]{1,0:T(8,128)(2,1)}, bf16[512,1024]{1,0:T(8,128)(2,1)}, u32[]{:S(2)}, u32[]{:S(2)}) collective-permute-start(bf16[512,1024]{1,0:T(8,128)(2,1)} %shard_map.92.ok.ov), channel_id=1, source_target_pairs={{0,4},{4,8},{8,12},{12,16},{16,20},{20,24},{24,28},{28,32},{32,36}... | collective-permute-start | bytes 3145736 | tf_op jit(solution)/shard_map/ppermute | solution.py:265
  189.4 0.1 pad_add_fusion.flag_ref
  189.5 1.3 broadcast_select_fusion.2
  190.7 2.4 collective-permute-start.3
  193.1 2.5 collective-permute-start.4
  195.6 3.6 %collective-permute-start.2 = (bf16[256,1024]{1,0:T(8,128)(2,1)S(1)}, bf16[256,1024]{1,0:T(8,128)(2,1)S(1)}, u32[]{:S(2)}, u32[]{:S(2)}) collective-permute-start(bf16[256,1024]{1,0:T(8,128)(2,1)S(1)} %get-tuple-element.24), channel_id=1, source_target_pairs={{0,1},{1,4},{4,5},{5,8},{8,9},{9,12},{12,13},{13,16},{16,17},{17,2... | collective-permute-start | bytes 1572872 | tf_op jit(solution)/shard_map/ppermute | solution.py:258
  199.3 0.0 copy-done.2
  199.3 12.0 %shard_map.91.q_ref = bf16[512,1024]{1,0:T(8,128)(2,1)S(1)} custom-call(bf16[512,5376]{1,0:T(8,128)(2,1)} %pad_maximum_fusion.x_ref, bf16[10752,1536]{1,0:T(8,128)(2,1)} %all-gather.2.cloned.1.call-done.w_ref.low_ref.high_ref, f32[1,128]{1,0:T(1,128)S(1)} %bitcast.10, f32[512,128]{1,0:T(8,128)S(1)} %get-tuple-element.15.cos_ref, ...), custom_call_target="tpu_custom_call" | custom-call | flops 5637144576 | bytes 16515072 | tf_op jit(solution)/shard_map/pallas_call | solution.py:65
  211.3 30.7 %collective-permute-done.2.ak.av = bf16[256,1024]{1,0:T(8,128)(2,1)S(1)} collective-permute-done((bf16[256,1024]{1,0:T(8,128)(2,1)S(1)}, bf16[256,1024]{1,0:T(8,128)(2,1)S(1)}, u32[]{:S(2)}, u32[]{:S(2)}) %collective-permute-start.2) | collective-permute-done | bytes 524320 | tf_op jit(solution)/shard_map/ppermute | solution.py:258
  241.9 0.0 collective-permute-done.3.bk.bv
  241.9 0.0 collective-permute-done.4.ck.cv
  241.9 0.0 collective-permute-done.1.zk.zv
  242.0 9.2 %shard_map.93.att_ref = bf16[512,1024]{1,0:T(8,128)(2,1)S(1)} custom-call(s32[3]{0:T(128)S(1)} %pad_add_fusion.flag_ref, bf16[512,1024]{1,0:T(8,128)(2,1)S(1)} %shard_map.91.q_ref, bf16[512,1024]{1,0:T(8,128)(2,1)} %shard_map.92.ok.ov, bf16[512,1024]{1,0:T(8,128)(2,1)} %shard_map.92.ok.ov, bf16[512,1024]{1,0:T(8,128)(2,1)} %collective-permute-done.1.zk.zv, ...), custom_call_target="tpu_custom_call" | custom-call | flops 2684354560 | bytes 6291456 | tf_op jit(solution)/shard_map/pallas_call | solution.py:122
  251.2 5.7 %shard_map.94 = (f32[256,2688]{1,0:T(8,128)S(1)}, bf16[256,2688]{1,0:T(8,128)(2,1)S(1)}) custom-call(bf16[512,1024]{1,0:T(8,128)(2,1)S(1)} %shard_map.93.att_ref, bf16[10752,1536]{1,0:T(8,128)(2,1)} %all-gather.2.cloned.1.call-done.w_ref.low_ref.high_ref, bf16[10752,1536]{1,0:T(8,128)(2,1)} %all-gather.2.cloned.1.call-done.w_ref.low_ref.high_ref), custom_call_target="tpu_custom_call" | custom-call | flops 2818572288 | bytes 10485760 | tf_op jit(solution)/shard_map/pallas_call | solution.py:145
  256.9 0.0 copy-start.4
  256.9 5.7 %shard_map.95 = (f32[256,2688]{1,0:T(8,128)S(1)}, bf16[256,2688]{1,0:T(8,128)(2,1)S(1)}) custom-call(bf16[512,1024]{1,0:T(8,128)(2,1)S(1)} %shard_map.93.att_ref, bf16[10752,1536]{1,0:T(8,128)(2,1)} %all-gather.2.cloned.1.call-done.w_ref.low_ref.high_ref, bf16[10752,1536]{1,0:T(8,128)(2,1)} %all-gather.2.cloned.1.call-done.w_ref.low_ref.high_ref), custom_call_target="tpu_custom_call" | custom-call | flops 2818572288 | bytes 10485760 | tf_op jit(solution)/shard_map/pallas_call | solution.py:145
  262.6 1.6 collective-permute-start.5
  264.2 0.1 collective-permute-start.6
  264.3 0.0 copy-done.4
  264.4 2.6 collective-permute-done.5.got0
  267.0 2.0 collective-permute-done.6.got1
  269.0 3.4 %shard_map.96 = bf16[256,5376]{1,0:T(8,128)(2,1)} custom-call(bf16[256,5376]{1,0:T(8,128)(2,1)S(1)} %copy-done, f32[256,2688]{1,0:T(8,128)S(1)} %get-tuple-element.17.own0, f32[256,2688]{1,0:T(8,128)S(1)} %get-tuple-element.18.own1, bf16[256,2688]{1,0:T(8,128)(2,1)S(1)} %collective-permute-done.5.got0, bf16[256,2688]{1,0:T(8,128)(2,1)S(1)} %collective-permute-done.6.got1, ...), custom_call_target="tpu_custom_call" | custom-call | flops 13762560 | bytes 14680064 | tf_op jit(solution)/shard_map/pallas_call | solution.py:183
  (5 shorter events, 0.1 us)
Async XLA Ops:
  6.5 167.0 %all-gather.2.cloned.1.call-start = ((), (), s32[]{:S(2)}) async-start(), calls=%async_computation.1 | async-start | bytes 33546240 | tf_op jit(solution)/shard_map/all_gather | solution.py:229
  7.5 8.2 %copy-start = (bf16[256,5376]{1,0:T(8,128)(2,1)S(1)}, bf16[256,5376]{1,0:T(8,128)(2,1)}, u32[]{:S(2)}) copy-start(bf16[256,5376]{1,0:T(8,128)(2,1)} %tok_ref.1) | copy-start | bytes 8257540
  10.3 6.0 %copy-start.3 = (f32[5376]{0:T(1024)S(1)}, f32[5376]{0:T(1024)}, u32[]{:S(2)}) copy-start(f32[5376]{0:T(1024)} %param.10) | copy-start | bytes 64516
  18.6 5.4 %collective-permute-start = (bf16[256,5376]{1,0:T(8,128)(2,1)}, bf16[256,5376]{1,0:T(8,128)(2,1)}, u32[]{:S(2)}, u32[]{:S(2)}) collective-permute-start(bf16[256,5376]{1,0:T(8,128)(2,1)} %fusion.2), channel_id=1, source_target_pairs={{0,2},{2,0},{1,3},{3,1},{4,6},{6,4},{5,7},{7,5},{8,10},{10,8},{9,1... | collective-permute-start | bytes 8257544 | tf_op jit(solution)/shard_map/ppermute | solution.py:239
  27.2 146.3 %copy-start.1 = (f32[128]{0:T(128)S(1)}, f32[128]{0:T(128)}, u32[]{:S(2)}) copy-start(f32[128]{0:T(128)} %param.16) | copy-start | bytes 1540
  173.5 25.7 %copy-start.2 = (f32[128]{0:T(128)S(1)}, f32[128]{0:T(128)}, u32[]{:S(2)}) copy-start(f32[128]{0:T(128)} %param.15) | copy-start | bytes 1540
  185.2 56.8 %collective-permute-start.1 = (bf16[512,1024]{1,0:T(8,128)(2,1)}, bf16[512,1024]{1,0:T(8,128)(2,1)}, u32[]{:S(2)}, u32[]{:S(2)}) collective-permute-start(bf16[512,1024]{1,0:T(8,128)(2,1)} %shard_map.92.ok.ov), channel_id=1, source_target_pairs={{0,4},{4,8},{8,12},{12,16},{16,20},{20,24},{24,28},{28,32},{32,36}... | collective-permute-start | bytes 3145736 | tf_op jit(solution)/shard_map/ppermute | solution.py:265
  190.7 51.2 %collective-permute-start.3 = (bf16[256,1024]{1,0:T(8,128)(2,1)S(1)}, bf16[256,1024]{1,0:T(8,128)(2,1)S(1)}, u32[]{:S(2)}, u32[]{:S(2)}) collective-permute-start(bf16[256,1024]{1,0:T(8,128)(2,1)S(1)} %get-tuple-element.23), channel_id=1, source_target_pairs={{1,4},{5,8},{9,12},{13,16},{17,20},{21,24},{25,28},{29,32},{33,36}... | collective-permute-start | bytes 1572872 | tf_op jit(solution)/shard_map/ppermute | solution.py:259
  193.1 48.8 %collective-permute-start.4 = (bf16[256,1024]{1,0:T(8,128)(2,1)S(1)}, bf16[256,1024]{1,0:T(8,128)(2,1)S(1)}, u32[]{:S(2)}, u32[]{:S(2)}) collective-permute-start(bf16[256,1024]{1,0:T(8,128)(2,1)S(1)} %get-tuple-element.23), channel_id=1, source_target_pairs={{0,1},{1,0},{2,3},{3,2},{4,5},{5,4},{6,7},{7,6},{8,9},{9,8},{10,11... | collective-permute-start | bytes 1572872 | tf_op jit(solution)/shard_map/ppermute | solution.py:264
  195.6 46.3 %collective-permute-start.2 = (bf16[256,1024]{1,0:T(8,128)(2,1)S(1)}, bf16[256,1024]{1,0:T(8,128)(2,1)S(1)}, u32[]{:S(2)}, u32[]{:S(2)}) collective-permute-start(bf16[256,1024]{1,0:T(8,128)(2,1)S(1)} %get-tuple-element.24), channel_id=1, source_target_pairs={{0,1},{1,4},{4,5},{5,8},{8,9},{9,12},{12,13},{13,16},{16,17},{17,2... | collective-permute-start | bytes 1572872 | tf_op jit(solution)/shard_map/ppermute | solution.py:258
  256.9 7.5 %copy-start.4 = (f32[5376]{0:T(1024)S(1)}, f32[5376]{0:T(1024)}, u32[]{:S(2)}) copy-start(f32[5376]{0:T(1024)} %param.17) | copy-start | bytes 64516
  262.6 4.4 %collective-permute-start.5 = (bf16[256,2688]{1,0:T(8,128)(2,1)S(1)}, bf16[256,2688]{1,0:T(8,128)(2,1)S(1)}, u32[]{:S(2)}, u32[]{:S(2)}) collective-permute-start(bf16[256,2688]{1,0:T(8,128)(2,1)S(1)} %get-tuple-element.19), channel_id=1, source_target_pairs={{0,2},{2,0},{1,3},{3,1},{4,6},{6,4},{5,7},{7,5},{8,10},{10,8},{9,1... | collective-permute-start | bytes 4128776 | tf_op jit(solution)/shard_map/ppermute | solution.py:274
  264.2 4.7 %collective-permute-start.6 = (bf16[256,2688]{1,0:T(8,128)(2,1)S(1)}, bf16[256,2688]{1,0:T(8,128)(2,1)S(1)}, u32[]{:S(2)}, u32[]{:S(2)}) collective-permute-start(bf16[256,2688]{1,0:T(8,128)(2,1)S(1)} %get-tuple-element.20), channel_id=1, source_target_pairs={{0,2},{2,0},{1,3},{3,1},{4,6},{6,4},{5,7},{7,5},{8,10},{10,8},{9,1... | collective-permute-start | bytes 4128776 | tf_op jit(solution)/shard_map/ppermute | solution.py:276
Sparse Core Ops, SparseCore 0:
  15.8 157.6 all-gather.1

commit v3 on v2

--- a/solution.py
+++ b/solution.py
@@ -36,8 +36,10 @@
     return unit * cosine + pltpu.roll(unit, HALF, axis=1) * sine
 
 
-def key_value_kernel(x_ref, w_ref, gain_ref, cos_ref, sin_ref, out_ref):
-    raw = jnp.dot(x_ref[...], w_ref[...], preferred_element_type=F32)
+def key_value_kernel(slot_ref, x_ref, *refs):
+    unit_refs, (gain_ref, cos_ref, sin_ref, out_ref) = refs[:8], refs[8:]
+    weights = jnp.concatenate([ref[0] for ref in unit_refs], axis=0)
+    raw = jnp.dot(x_ref[...], weights, preferred_element_type=F32)
 
     @pl.when(pl.program_id(0) < 2)
     def _():
@@ -57,6 +59,29 @@
         at = slice(h * HEAD, (h + 1) * HEAD)
         query = turned(raw[:, at], gain_ref[...], cos_ref[...], sin_ref[...], query_scale)
         out_ref[:, at] = query.astype(BF)
+
+
+def key_values(slots, x, units, gain, cosine, sine):
+    rows = x.shape[0]
+    whole = pl.BlockSpec(memory_space=pltpu.VMEM)
+
+    def unit(n):
+        return pl.BlockSpec(
+            (1, units.shape[1], 256), lambda t, slot: (slot[lax.rem(t, 2) * 8 + n], 0, t // 2)
+        )
+
+    return pl.pallas_call(
+        key_value_kernel,
+        out_shape=jax.ShapeDtypeStruct((rows, 1024), BF),
+        grid_spec=pltpu.PrefetchScalarGridSpec(
+            num_scalar_prefetch=1,
+            grid=(4,),
+            in_specs=[whole] + [unit(n) for n in range(8)] + [whole, whole, whole],
+            out_specs=pl.BlockSpec((rows, 256), lambda t, slot: (0, t)),
+        ),
+        compiler_params=params(48),
+        cost_estimate=cost(2 * rows * WIDTH * 1024, 2 * WIDTH * 1536),
+    )(slots, x, *([units] * 8), gain, cosine, sine)
 
 
 def projection(kernel, x, weights, gain, cosine, sine, where):
@@ -151,8 +176,8 @@
         grid=(steps,),
         in_specs=[
             pl.BlockSpec(memory_space=pltpu.VMEM),
-            pl.BlockSpec((tile, 512), lambda i: (first + i, 2)),
-            pl.BlockSpec((tile, 512), lambda i: (first + i + 2 * steps, 2)),
+            pl.BlockSpec((tile, 512), lambda i: (first + i, 1)),
+            pl.BlockSpec((tile, 512), lambda i: (first + i + 2 * steps, 1)),
         ],
         out_specs=(
             pl.BlockSpec((BLOCK, tile), lambda i: (0, i)),
@@ -200,6 +225,43 @@
         jnp.concatenate([cosine, cosine], axis=1),
         jnp.concatenate([-sine, sine], axis=1),
     )
+
+
+def index_of(at):
+    x_lo, y, z, core, x_hi = at["x"] % 2, at["y"], at["z"], at["core"], at["x"] // 2
+    return (((x_lo * 4 + y) * 4 + z) * 2 + core) * 2 + x_hi
+
+
+def ring_step(block, dims, step):
+    pairs = []
+    for n in range(128):
+        at = {"x": n % 2 * 2 + n // 64, "core": n // 2 % 2, "z": n // 4 % 4, "y": n // 16 % 4}
+        to = dict(at)
+        dim = dims[at["core"]]
+        to[dim] = (at[dim] + step) % 4
+        pairs.append((index_of(at), index_of(to)))
+    return lax.ppermute(block, AXES, pairs)
+
+
+def ring(block, dims):
+    middle = block.shape[0] // 2
+    left, right = ring_step(block, dims, 1), ring_step(block, dims, -1)
+    opposite = [ring_step(left[:middle], dims, 1), ring_step(right[middle:], dims, -1)]
+    return jnp.concatenate([block, right, *opposite, left], axis=0)
+
+
+def ringed_units(rows, x, y, z, core):
+    count = rows.shape[0]
+    stack = jnp.zeros((4 * count, rows.shape[1]), rows.dtype)
+    for step in range(4):
+        piece = rows if step == 0 else ring_step(rows, ("z", "z"), -step)
+        at = lax.rem(z + step, 4) * count
+        stack = lax.dynamic_update_slice(stack, piece, (at, jnp.int32(0)))
+    units = ring(ring(stack, ("y", "x")), ("x", "y"))
+    n = jnp.arange(16, dtype=jnp.int32)
+    off_x, off_y = (n // 4 - x) % 4, (n % 4 - y) % 4
+    slots = jnp.where(core == 0, off_x * 4 + off_y, off_y * 4 + off_x)
+    return units.reshape(16, 4 * count, -1), slots
 
 
 def quarter_rows(pieces):
@@ -227,10 +289,12 @@
     side = lax.axis_index("x_hi")
     chip = lax.axis_index(CHIPS)
     full = lax.all_gather(
-        quarter_rows([query_weight, key_matrix, value_matrix, out_weight]),
-        GATHER,
-        axis=0,
-        tiled=True,
+        quarter_rows([query_weight, out_weight]), GATHER, axis=0, tiled=True
+    )
+    place = [lax.axis_index(name) for name in ("x_hi", "x_lo", "y", "z")]
+    units, slots = ringed_units(
+        quarter_rows([key_matrix, value_matrix]),
+        place[0] * 2 + place[1], place[2], place[3], core,
     )
 
     plain = tokens.astype(F32)
@@ -244,12 +308,7 @@
     positions = (4 * chip + side) * BLOCK + row + (row // BLOCK) * BLOCK
     cosine, sine = rotations(positions)
 
-    full, x, cosine, sine = lax.optimization_barrier((full, x, cosine, sine))
-
-    own = projection(
-        key_value_kernel, x, full, key_gain.reshape(1, HEAD), cosine, sine,
-        lambda t: (lax.rem(t, 2), 2 + t // 2),
-    )
+    own = key_values(slots, x, units, key_gain.reshape(1, HEAD), cosine, sine)
     first, second = own[:BLOCK], own[BLOCK:]
     mine = jnp.where(side == 0, first, second)
     swap = jnp.where(side == 0, second, first)
@@ -263,6 +322,7 @@
     )
     link = lax.ppermute(swap, "x_hi", [(0, 1), (1, 0)])
     behind = lax.ppermute(own, CHIPS, [(i, i + 1) for i in range(chips - 1)])
+    full, prior, gap, link, behind = lax.optimization_barrier((full, prior, gap, link, behind))
     queries = projection(
         query_kernel, x, full, query_gain.reshape(1, HEAD), cosine, sine,
         lambda t: (t // 2, lax.rem(t, 2)),

time: 280 us -> 299 us (1.068)
  waiting for transfers between devices: 183 us -> 159 us
  local copies, waits for them, and re-layouts: 4.62 us -> 25.1 us
  starting transfers between devices: 14.8 us -> 30 us
  blocking collectives: 4.44 us -> 8.46 us
    all_gather x1, waiting for transfers between devices: 143 us -> 0.01 us  [on_device(): lax.all_gather(quarter_rows([query_weight, out_weight]), GATHER, axis=0,...]
    ppermute x0 -> x11, waiting for transfers between devices: none -> 112 us  [ring_step(): return lax.ppermute(block, AXES, pairs)]
    pallas_call x0 -> x1, Pallas kernels: none -> 12.8 us  [key_values(): pl.pallas_call(key_value_kernel, out_shape=jax.ShapeDtypeStruct((rows, 10...]
    pallas_call x2 -> x1, Pallas kernels: 23.6 us -> 12 us  [projection(): pl.pallas_call(kernel, out_shape=jax.ShapeDtypeStruct((rows, 1024), BF),...]
    unnamed x10 -> x21, local copies, waits for them, and re-layouts: 0.03 us -> 10.2 us
    ppermute x0 -> x11, starting transfers between devices: none -> 9.54 us  [ring_step(): return lax.ppermute(block, AXES, pairs)]
    ppermute x1, starting transfers between devices: 0.37 us -> 8.67 us  [on_device(): other = lax.ppermute(normed, 'core', [(0, 1), (1, 0)])]
    ppermute x1, waiting for transfers between devices: 0.01 us -> 7.85 us  [on_device(): link = lax.ppermute(swap, 'x_hi', [(0, 1), (1, 0)])]
  transfers between devices with their start and end apart: 8 -> 19, of which waited for: 5 -> 13; matrix products, arithmetic and copies ran while one was open for 4% -> 12% of each run, Pallas kernels for 4% -> 4%
where the time goes in v3:
time: 299 us; the launch traced here: 298 us
  waiting for transfers between devices  159 us (53%)
  Pallas kernels  48.8 us (16%)
  starting transfers between devices  30 us (10%)
  local copies, waits for them, and re-layouts  25.1 us (8%)
  between operations  13.7 us (5%)
  other arithmetic  12.6 us (4%)
  blocking collectives  8.46 us (3%)
    ppermute x11, waiting for transfers between devices, ring_step(): return lax.ppermute(block, AXES, pairs)  112 us
    ppermute x1, waiting for transfers between devices, on_device(): prior = lax.ppermute(mine, line, [(i, i + 1) for i in range(2 * chips - 1)])  31.2 us
    pallas_call x1, Pallas kernels, key_values(): pl.pallas_call(key_value_kernel, out_shape=jax.ShapeDtypeStruct((rows, 10...  12.8 us
    pallas_call x1, Pallas kernels, projection(): pl.pallas_call(kernel, out_shape=jax.ShapeDtypeStruct((rows, 1024), BF),...  12 us
    pallas_call x2, Pallas kernels, out_projection(): pl.pallas_call(out_kernel, out_shape=(jax.ShapeDtypeStruct((BLOCK, WIDTH...  11.4 us
    unnamed x21, local copies, waits for them, and re-layouts  10.2 us
    ppermute x11, starting transfers between devices, ring_step(): return lax.ppermute(block, AXES, pairs)  9.54 us
    pallas_call x1, Pallas kernels, attention(): pl.pallas_call(attention_kernel, out_shape=jax.ShapeDtypeStruct((2 * BLOC...  9.13 us
  transfers between devices with their start and end apart: 19, of which 13 were waited for; matrix products, arithmetic and copies ran while one was open for 12% of the time, Pallas kernels for 4%

profile of v3, /device:TPU:125, one launch (start us, length us, event | category | flops | bytes accessed | tf_op | source)
XLA Modules:
  0.0 297.7 jit_solution(8224908740583499385)
XLA Ops:
  6.5 1.0 fusion.14
  7.5 0.9 fusion.15
  8.6 4.6 %all_to_all.10 = bf16[2,84,1024]{2,1,0:T(8,128)(2,1)S(1)} all-to-all(bf16[2,84,1024]{2,1,0:T(8,128)(2,1)S(1)} %pad_maximum_fusion.1), channel_id=1, replica_groups=mesh['x_lo'=2,'y'=4,'z'=4,'core'=2,'x_hi'=2] {'core'}, dimensions={0} | all-to-all | bytes 688128 | tf_op jit(solution)/shard_map/all_to_all | solution.py:273
  13.2 0.8 reshape.52
  14.1 3.9 %all_to_all.11 = bf16[2,84,512]{2,1,0:T(8,128)(2,1)S(1)} all-to-all(bf16[2,84,512]{2,1,0:T(8,128)(2,1)S(1)} %pad_maximum_fusion.4), channel_id=1, replica_groups=mesh['x_lo'=2,'y'=4,'z'=4,'core'=2,'x_hi'=2] {'core'}, dimensions={0} | all-to-all | bytes 344064 | tf_op jit(solution)/shard_map/all_to_all | solution.py:273
  18.0 0.7 reshape.53
  18.7 0.1 collective-permute-start.1
  18.8 0.2 collective-permute-start.2
  19.0 2.4 collective-permute-start.3
  21.4 1.0 constant_dynamic-update-slice_fusion.17
  22.4 8.4 %collective-permute-done.1 = bf16[168,512]{1,0:T(8,128)(2,1)} collective-permute-done((bf16[168,512]{1,0:T(8,128)(2,1)}, bf16[168,512]{1,0:T(8,128)(2,1)}, u32[]{:S(2)}, u32[]{:S(2)}) %collective-permute-start.1) | collective-permute-done | bytes 172064 | tf_op jit(solution)/shard_map/ppermute | solution.py:243
  30.8 0.9 constant_dynamic-update-slice_fusion.16
  31.7 0.9 constant_dynamic-update-slice_fusion.15
  32.7 0.9 constant_dynamic-update-slice_fusion.14
  33.6 1.0 collective-permute-start.5
  34.6 0.5 collective-permute-start.4
  35.2 0.6 fusion
  35.8 8.3 %collective-permute-done.5 = bf16[672,512]{1,0:T(8,128)(2,1)S(1)} collective-permute-done((bf16[672,512]{1,0:T(8,128)(2,1)S(1)}, bf16[672,512]{1,0:T(8,128)(2,1)S(1)}, u32[]{:S(2)}, u32[]{:S(2)}) %collective-permute-start.5) | collective-permute-done | bytes 688160 | tf_op jit(solution)/shard_map/ppermute | solution.py:243
  44.1 1.1 collective-permute-start.6
  45.2 0.6 collective-permute-start.7
  45.8 1.2 constant_dynamic-update-slice_fusion.4
  46.9 1.2 constant_dynamic-update-slice_fusion.3
  48.1 5.1 %collective-permute-done.6 = bf16[336,512]{1,0:T(8,128)(2,1)S(1)} collective-permute-done((bf16[336,512]{1,0:T(8,128)(2,1)S(1)}, bf16[336,512]{1,0:T(8,128)(2,1)S(1)}, u32[]{:S(2)}, u32[]{:S(2)}) %collective-permute-start.6) | collective-permute-done | bytes 344096 | tf_op jit(solution)/shard_map/ppermute | solution.py:243
  53.2 0.9 constant_dynamic-update-slice_fusion.2
  54.2 1.6 collective-permute-done.7
  55.8 0.9 constant_dynamic-update-slice_fusion.1
  56.7 1.3 constant_dynamic-update-slice_fusion
  58.0 2.3 fusion.2
  60.2 8.7 %collective-permute-start = (bf16[256,5376]{1,0:T(8,128)(2,1)}, bf16[256,5376]{1,0:T(8,128)(2,1)}, u32[]{:S(2)}, u32[]{:S(2)}) collective-permute-start(bf16[256,5376]{1,0:T(8,128)(2,1)} %fusion.2), channel_id=1, source_target_pairs={{0,2},{2,0},{1,3},{3,1},{4,6},{6,4},{5,7},{7,5},{8,10},{10,8},{9,1... | collective-permute-start | bytes 8257544 | tf_op jit(solution)/shard_map/ppermute | solution.py:303
  68.9 1.0 fusion.3
  69.9 0.2 pad_maximum_fusion.2
  70.1 56.3 %collective-permute-done.9 = bf16[2688,512]{1,0:T(8,128)(2,1)} collective-permute-done((bf16[2688,512]{1,0:T(8,128)(2,1)}, bf16[2688,512]{1,0:T(8,128)(2,1)}, u32[]{:S(2)}, u32[]{:S(2)}) %collective-permute-start.9) | collective-permute-done | bytes 2752544 | tf_op jit(solution)/shard_map/ppermute | solution.py:243
  126.5 1.4 slice.58
  127.9 3.5 %collective-permute-start.10 = (bf16[1344,512]{1,0:T(8,128)(2,1)S(1)}, bf16[1344,512]{1,0:T(8,128)(2,1)S(1)}, u32[]{:S(2)}, u32[]{:S(2)}) collective-permute-start(bf16[1344,512]{1,0:T(8,128)(2,1)S(1)} %slice.58), channel_id=1, source_target_pairs={{0,64},{1,65},{2,18},{3,19},{4,68},{5,69},{6,22},{7,23},{8,72},{9,... | collective-permute-start | bytes 4128776 | tf_op jit(solution)/shard_map/ppermute | solution.py:243
  131.4 3.2 %broadcast_select_fusion.1 = (bf16[256,5376]{1,0:T(8,128)(2,1)S(1)}, bf16[256,5376]{1,0:T(8,128)(2,1)S(1)}) fusion(bf16[256,5376]{1,0:T(8,128)(2,1)} %collective-permute-done, pred[]{:T(512)S(6)} %eq.13, f32[5376]{0:T(1024)S(1)} %copy-done.3, f32[256]{0:T(256)S(1)} %add_rsqrt_fusion, bf16[256,5376]{1,0:T(8,128)(2,1)S(1)} %copy-done), kind=kLoop, calls=%fused_computation.7 | loop fusion | flops 8257536 | bytes 11032577 | tf_op jit(solution)/shard_map/jit(_where)/select_n | solution.py:305
  134.6 9.3 %collective-permute-done.8 = bf16[2688,512]{1,0:T(8,128)(2,1)} collective-permute-done((bf16[2688,512]{1,0:T(8,128)(2,1)}, bf16[2688,512]{1,0:T(8,128)(2,1)}, u32[]{:S(2)}, u32[]{:S(2)}) %collective-permute-start.8) | collective-permute-done | bytes 2752544 | tf_op jit(solution)/shard_map/ppermute | solution.py:243
  143.8 1.4 slice.59
  145.3 0.3 collective-permute-start.11
  145.5 2.8 pad_maximum_fusion.x_ref
  148.3 3.6 %constant_dynamic-update-slice_fusion.8 = bf16[10752,512]{1,0:T(8,128)(2,1)} fusion(bf16[10752,512]{1,0:T(8,128)(2,1)} %get-tuple-element.28, bf16[2688,512]{1,0:T(8,128)(2,1)} %collective-permute-done.8), kind=kLoop, calls=%fused_computation.29 | loop fusion | bytes 5505024
  151.9 18.8 %collective-permute-done.10 = bf16[1344,512]{1,0:T(8,128)(2,1)S(1)} collective-permute-done((bf16[1344,512]{1,0:T(8,128)(2,1)S(1)}, bf16[1344,512]{1,0:T(8,128)(2,1)S(1)}, u32[]{:S(2)}, u32[]{:S(2)}) %collective-permute-start.10) | collective-permute-done | bytes 1376288 | tf_op jit(solution)/shard_map/ppermute | solution.py:243
  170.7 1.2 constant_dynamic-update-slice_fusion.7
  171.9 4.1 %collective-permute-done.11 = bf16[1344,512]{1,0:T(8,128)(2,1)S(1)} collective-permute-done((bf16[1344,512]{1,0:T(8,128)(2,1)S(1)}, bf16[1344,512]{1,0:T(8,128)(2,1)S(1)}, u32[]{:S(2)}, u32[]{:S(2)}) %collective-permute-start.11) | collective-permute-done | bytes 1376288 | tf_op jit(solution)/shard_map/ppermute | solution.py:243
  175.9 1.2 constant_dynamic-update-slice_fusion.6
  177.2 3.5 %constant_dynamic-update-slice_fusion.5 = bf16[10752,512]{1,0:T(8,128)(2,1)} fusion(bf16[10752,512]{1,0:T(8,128)(2,1)} %constant_dynamic-update-slice_fusion.6, bf16[2688,512]{1,0:T(8,128)(2,1)} %collective-permute-done.9), kind=kLoop, calls=%fused_computation.26 | loop fusion | bytes 5505024 | tf_op jit(solution)/shard_map/concatenate | solution.py:250
  180.6 12.8 %shard_map.91.ok.ov = bf16[512,1024]{1,0:T(8,128)(2,1)} custom-call(s32[16]{0:T(128)S(1)} %broadcast_select_fusion.4.slot_ref, bf16[512,5376]{1,0:T(8,128)(2,1)} %pad_maximum_fusion.x_ref, bf16[16,672,512]{2,1,0:T(8,128)(2,1)} %bitcast.7.refs_0_.refs_1_.refs_2_.refs_3_.refs_4_.refs_5_.refs_6_.refs_7_, ...), custom_call_target="tpu_custom_call" | custom-call | flops 5637144576 | bytes 16515072 | tf_op jit(solution)/shard_map/pallas_call | solution.py:73
  193.5 2.4 collective-permute-start.15
  195.9 2.3 broadcast_select_fusion.2
  198.2 2.4 collective-permute-start.12
  200.6 2.6 collective-permute-start.13
  203.2 2.5 collective-permute-start.14
  205.7 0.1 pad_add_fusion.flag_ref
  205.8 31.2 %collective-permute-done.12.ak.av = bf16[256,1024]{1,0:T(8,128)(2,1)} collective-permute-done((bf16[256,1024]{1,0:T(8,128)(2,1)}, bf16[256,1024]{1,0:T(8,128)(2,1)}, u32[]{:S(2)}, u32[]{:S(2)}) %collective-permute-start.12) | collective-permute-done | bytes 524320 | tf_op jit(solution)/shard_map/ppermute | solution.py:317
  237.1 3.4 %collective-permute-done.13.bk.bv = bf16[256,1024]{1,0:T(8,128)(2,1)} collective-permute-done((bf16[256,1024]{1,0:T(8,128)(2,1)}, bf16[256,1024]{1,0:T(8,128)(2,1)}, u32[]{:S(2)}, u32[]{:S(2)}) %collective-permute-start.13) | collective-permute-done | bytes 524320 | tf_op jit(solution)/shard_map/ppermute | solution.py:318
  240.5 7.9 %collective-permute-done.14.ck.cv = bf16[256,1024]{1,0:T(8,128)(2,1)} collective-permute-done((bf16[256,1024]{1,0:T(8,128)(2,1)}, bf16[256,1024]{1,0:T(8,128)(2,1)}, u32[]{:S(2)}, u32[]{:S(2)}) %collective-permute-start.14) | collective-permute-done | bytes 524320 | tf_op jit(solution)/shard_map/ppermute | solution.py:323
  248.3 12.0 %shard_map.92.q_ref = bf16[512,1024]{1,0:T(8,128)(2,1)S(1)} custom-call(bf16[512,5376]{1,0:T(8,128)(2,1)} %pad_maximum_fusion.x_ref, bf16[10752,1024]{1,0:T(8,128)(2,1)} %all-gather.2.cloned.1.call-done.w_ref.low_ref.high_ref, f32[1,128]{1,0:T(1,128)S(1)} %bitcast.15, f32[512,128]{1,0:T(8,128)S(1)} %get-tuple-element.52.refs_9_.cos_ref, ...), custom_call_target="tpu_custom_call" | custom-call | flops 5637144576 | bytes 16515072 | tf_op jit(solution)/shard_map/pallas_call | solution.py:90
  260.3 9.1 %shard_map.93.att_ref = bf16[512,1024]{1,0:T(8,128)(2,1)S(1)} custom-call(s32[3]{0:T(128)S(1)} %pad_add_fusion.flag_ref, bf16[512,1024]{1,0:T(8,128)(2,1)S(1)} %shard_map.92.q_ref, bf16[512,1024]{1,0:T(8,128)(2,1)} %shard_map.91.ok.ov, bf16[512,1024]{1,0:T(8,128)(2,1)} %shard_map.91.ok.ov, bf16[512,1024]{1,0:T(8,128)(2,1)} %collective-permute-done.15.zk.zv, ...), custom_call_target="tpu_custom_call" | custom-call | flops 2684354560 | bytes 6291456 | tf_op jit(solution)/shard_map/pallas_call | solution.py:147
  269.5 5.7 %shard_map.95 = (f32[256,2688]{1,0:T(8,128)S(1)}, bf16[256,2688]{1,0:T(8,128)(2,1)S(1)}) custom-call(bf16[512,1024]{1,0:T(8,128)(2,1)S(1)} %shard_map.93.att_ref, bf16[10752,1024]{1,0:T(8,128)(2,1)} %all-gather.2.cloned.1.call-done.w_ref.low_ref.high_ref, bf16[10752,1024]{1,0:T(8,128)(2,1)} %all-gather.2.cloned.1.call-done.w_ref.low_ref.high_ref), custom_call_target="tpu_custom_call" | custom-call | flops 2818572288 | bytes 10485760 | tf_op jit(solution)/shard_map/pallas_call | solution.py:170
  275.2 5.7 %shard_map.94 = (f32[256,2688]{1,0:T(8,128)S(1)}, bf16[256,2688]{1,0:T(8,128)(2,1)S(1)}) custom-call(bf16[512,1024]{1,0:T(8,128)(2,1)S(1)} %shard_map.93.att_ref, bf16[10752,1024]{1,0:T(8,128)(2,1)} %all-gather.2.cloned.1.call-done.w_ref.low_ref.high_ref, bf16[10752,1024]{1,0:T(8,128)(2,1)} %all-gather.2.cloned.1.call-done.w_ref.low_ref.high_ref), custom_call_target="tpu_custom_call" | custom-call | flops 2818572288 | bytes 10485760 | tf_op jit(solution)/shard_map/pallas_call | solution.py:170
  280.9 1.8 collective-permute-start.17
  282.7 0.1 collective-permute-start.16
  282.8 2.6 collective-permute-done.17.got1
  285.5 2.0 collective-permute-done.16.got0
  287.4 3.4 %shard_map.96 = bf16[256,5376]{1,0:T(8,128)(2,1)} custom-call(bf16[256,5376]{1,0:T(8,128)(2,1)S(1)} %copy-done, f32[256,2688]{1,0:T(8,128)S(1)} %get-tuple-element.19.own0, f32[256,2688]{1,0:T(8,128)S(1)} %get-tuple-element.20.own1, bf16[256,2688]{1,0:T(8,128)(2,1)S(1)} %collective-permute-done.16.got0, bf16[256,2688]{1,0:T(8,128)(2,1)S(1)} %collective-permute-done.17.got1, ...), custom_call_target="tpu_custom_call" | custom-call | flops 13762560 | bytes 14680064 | tf_op jit(solution)/shard_map/pallas_call | solution.py:208
  (38 shorter events, 0.3 us)
Async XLA Ops:
  6.5 7.5 %copy-start.4 = (bf16[84,512]{1,0:T(8,128)(2,1)S(1)}, bf16[84,512]{1,0:T(8,128)(2,1)}, u32[]{:S(2)}) copy-start(bf16[84,512]{1,0:T(8,128)(2,1)} %param.12) | copy-start | bytes 258052
  6.5 7.5 %copy-start.5 = (bf16[84,512]{1,0:T(8,128)(2,1)S(1)}, bf16[84,512]{1,0:T(8,128)(2,1)}, u32[]{:S(2)}) copy-start(bf16[84,512]{1,0:T(8,128)(2,1)} %param.13) | copy-start | bytes 258052
  6.5 241.8 %all-gather.2.cloned.1.call-start = ((), (), s32[]{:S(2)}) async-start(), calls=%async_computation.2 | async-start | bytes 22364160 | tf_op jit(solution)/shard_map/all_gather | solution.py:291
  8.6 26.6 %copy-start = (bf16[256,5376]{1,0:T(8,128)(2,1)S(1)}, bf16[256,5376]{1,0:T(8,128)(2,1)}, u32[]{:S(2)}) copy-start(bf16[256,5376]{1,0:T(8,128)(2,1)} %tok_ref.1) | copy-start | bytes 8257540
  18.7 12.1 %collective-permute-start.1 = (bf16[168,512]{1,0:T(8,128)(2,1)}, bf16[168,512]{1,0:T(8,128)(2,1)}, u32[]{:S(2)}, u32[]{:S(2)}) collective-permute-start(bf16[168,512]{1,0:T(8,128)(2,1)} %reshape.53), channel_id=1, source_target_pairs={{0,12},{1,13},{2,14},{3,15},{4,0},{5,1},{6,2},{7,3},{8,4},{9,5},{1... | collective-permute-start | bytes 516104 | tf_op jit(solution)/shard_map/ppermute | solution.py:243
  18.8 12.9 %collective-permute-start.2 = (bf16[168,512]{1,0:T(8,128)(2,1)}, bf16[168,512]{1,0:T(8,128)(2,1)}, u32[]{:S(2)}, u32[]{:S(2)}) collective-permute-start(bf16[168,512]{1,0:T(8,128)(2,1)} %reshape.53), channel_id=1, source_target_pairs={{0,8},{1,9},{2,10},{3,11},{4,12},{5,13},{6,14},{7,15},{8,0},{9,1},... | collective-permute-start | bytes 516104 | tf_op jit(solution)/shard_map/ppermute | solution.py:243
  19.0 13.7 %collective-permute-start.3 = (bf16[168,512]{1,0:T(8,128)(2,1)}, bf16[168,512]{1,0:T(8,128)(2,1)}, u32[]{:S(2)}, u32[]{:S(2)}) collective-permute-start(bf16[168,512]{1,0:T(8,128)(2,1)} %reshape.53), channel_id=1, source_target_pairs={{0,4},{1,5},{2,6},{3,7},{4,8},{5,9},{6,10},{7,11},{8,12},{9,13},{1... | collective-permute-start | bytes 516104 | tf_op jit(solution)/shard_map/ppermute | solution.py:243
  33.6 10.5 %collective-permute-start.5 = (bf16[672,512]{1,0:T(8,128)(2,1)S(1)}, bf16[672,512]{1,0:T(8,128)(2,1)S(1)}, u32[]{:S(2)}, u32[]{:S(2)}) collective-permute-start(bf16[672,512]{1,0:T(8,128)(2,1)S(1)} %constant_dynamic-update-slice_fusion.14), channel_id=1, source_target_pairs={{0,16},{1,17},{2,66},{3,67},{4,20},{5,21},{6,70},{7,71},{8,24},{9,... | collective-permute-start | bytes 2064392 | tf_op jit(solution)/shard_map/ppermute | solution.py:243
  34.6 10.6 %collective-permute-start.4 = (bf16[672,512]{1,0:T(8,128)(2,1)S(1)}, bf16[672,512]{1,0:T(8,128)(2,1)S(1)}, u32[]{:S(2)}, u32[]{:S(2)}) collective-permute-start(bf16[672,512]{1,0:T(8,128)(2,1)S(1)} %constant_dynamic-update-slice_fusion.14), channel_id=1, source_target_pairs={{0,48},{1,49},{2,67},{3,66},{4,52},{5,53},{6,71},{7,70},{8,56},{9,... | collective-permute-start | bytes 2064392 | tf_op jit(solution)/shard_map/ppermute | solution.py:243
  44.1 9.1 %collective-permute-start.6 = (bf16[336,512]{1,0:T(8,128)(2,1)S(1)}, bf16[336,512]{1,0:T(8,128)(2,1)S(1)}, u32[]{:S(2)}, u32[]{:S(2)}) collective-permute-start(bf16[336,512]{1,0:T(8,128)(2,1)S(1)} %slice.56), channel_id=1, source_target_pairs={{0,16},{1,17},{2,66},{3,67},{4,20},{5,21},{6,70},{7,71},{8,24},{9,... | collective-permute-start | bytes 1032200 | tf_op jit(solution)/shard_map/ppermute | solution.py:243
  45.2 10.6 %collective-permute-start.7 = (bf16[336,512]{1,0:T(8,128)(2,1)S(1)}, bf16[336,512]{1,0:T(8,128)(2,1)S(1)}, u32[]{:S(2)}, u32[]{:S(2)}) collective-permute-start(bf16[336,512]{1,0:T(8,128)(2,1)S(1)} %slice.57), channel_id=1, source_target_pairs={{0,48},{1,49},{2,67},{3,66},{4,52},{5,53},{6,71},{7,70},{8,56},{9,... | collective-permute-start | bytes 1032200 | tf_op jit(solution)/shard_map/ppermute | solution.py:243
  46.9 11.0 %copy-start.3 = (f32[5376]{0:T(1024)S(1)}, f32[5376]{0:T(1024)}, u32[]{:S(2)}) copy-start(f32[5376]{0:T(1024)} %param.10) | copy-start | bytes 64516
  58.0 68.5 %collective-permute-start.9 = (bf16[2688,512]{1,0:T(8,128)(2,1)}, bf16[2688,512]{1,0:T(8,128)(2,1)}, u32[]{:S(2)}, u32[]{:S(2)}) collective-permute-start(bf16[2688,512]{1,0:T(8,128)(2,1)} %get-tuple-element.27), channel_id=1, source_target_pairs={{0,64},{1,65},{2,18},{3,19},{4,68},{5,69},{6,22},{7,23},{8,72},{9,... | collective-permute-start | bytes 8257544 | tf_op jit(solution)/shard_map/ppermute | solution.py:243
  60.2 71.2 %collective-permute-start = (bf16[256,5376]{1,0:T(8,128)(2,1)}, bf16[256,5376]{1,0:T(8,128)(2,1)}, u32[]{:S(2)}, u32[]{:S(2)}) collective-permute-start(bf16[256,5376]{1,0:T(8,128)(2,1)} %fusion.2), channel_id=1, source_target_pairs={{0,2},{2,0},{1,3},{3,1},{4,6},{6,4},{5,7},{7,5},{8,10},{10,8},{9,1... | collective-permute-start | bytes 8257544 | tf_op jit(solution)/shard_map/ppermute | solution.py:303
  68.9 74.9 %collective-permute-start.8 = (bf16[2688,512]{1,0:T(8,128)(2,1)}, bf16[2688,512]{1,0:T(8,128)(2,1)}, u32[]{:S(2)}, u32[]{:S(2)}) collective-permute-start(bf16[2688,512]{1,0:T(8,128)(2,1)} %get-tuple-element.27), channel_id=1, source_target_pairs={{0,65},{1,64},{2,50},{3,51},{4,69},{5,68},{6,54},{7,55},{8,73},{9,... | collective-permute-start | bytes 8257544 | tf_op jit(solution)/shard_map/ppermute | solution.py:243
  127.9 42.8 %collective-permute-start.10 = (bf16[1344,512]{1,0:T(8,128)(2,1)S(1)}, bf16[1344,512]{1,0:T(8,128)(2,1)S(1)}, u32[]{:S(2)}, u32[]{:S(2)}) collective-permute-start(bf16[1344,512]{1,0:T(8,128)(2,1)S(1)} %slice.58), channel_id=1, source_target_pairs={{0,64},{1,65},{2,18},{3,19},{4,68},{5,69},{6,22},{7,23},{8,72},{9,... | collective-permute-start | bytes 4128776 | tf_op jit(solution)/shard_map/ppermute | solution.py:243
  145.3 30.7 %collective-permute-start.11 = (bf16[1344,512]{1,0:T(8,128)(2,1)S(1)}, bf16[1344,512]{1,0:T(8,128)(2,1)S(1)}, u32[]{:S(2)}, u32[]{:S(2)}) collective-permute-start(bf16[1344,512]{1,0:T(8,128)(2,1)S(1)} %slice.59), channel_id=1, source_target_pairs={{0,65},{1,64},{2,50},{3,51},{4,69},{5,68},{6,54},{7,55},{8,73},{9,... | collective-permute-start | bytes 4128776 | tf_op jit(solution)/shard_map/ppermute | solution.py:243
  177.2 3.5 %copy-start.1 = (f32[128]{0:T(128)S(1)}, f32[128]{0:T(128)}, u32[]{:S(2)}) copy-start(f32[128]{0:T(128)} %param.16) | copy-start | bytes 1540
  180.6 67.7 %copy-start.2 = (f32[128]{0:T(128)S(1)}, f32[128]{0:T(128)}, u32[]{:S(2)}) copy-start(f32[128]{0:T(128)} %param.15) | copy-start | bytes 1540
  193.5 54.8 %collective-permute-start.15 = (bf16[512,1024]{1,0:T(8,128)(2,1)}, bf16[512,1024]{1,0:T(8,128)(2,1)}, u32[]{:S(2)}, u32[]{:S(2)}) collective-permute-start(bf16[512,1024]{1,0:T(8,128)(2,1)} %shard_map.91.ok.ov), channel_id=1, source_target_pairs={{0,4},{4,8},{8,12},{12,16},{16,20},{20,24},{24,28},{28,32},{32,36}... | collective-permute-start | bytes 3145736 | tf_op jit(solution)/shard_map/ppermute | solution.py:324
  198.2 38.8 %collective-permute-start.12 = (bf16[256,1024]{1,0:T(8,128)(2,1)}, bf16[256,1024]{1,0:T(8,128)(2,1)}, u32[]{:S(2)}, u32[]{:S(2)}) collective-permute-start(bf16[256,1024]{1,0:T(8,128)(2,1)} %get-tuple-element.26), channel_id=1, source_target_pairs={{0,1},{1,4},{4,5},{5,8},{8,9},{9,12},{12,13},{13,16},{16,17},{17,2... | collective-permute-start | bytes 1572872 | tf_op jit(solution)/shard_map/ppermute | solution.py:317
  200.6 39.8 %collective-permute-start.13 = (bf16[256,1024]{1,0:T(8,128)(2,1)}, bf16[256,1024]{1,0:T(8,128)(2,1)}, u32[]{:S(2)}, u32[]{:S(2)}) collective-permute-start(bf16[256,1024]{1,0:T(8,128)(2,1)} %get-tuple-element.25), channel_id=1, source_target_pairs={{1,4},{5,8},{9,12},{13,16},{17,20},{21,24},{25,28},{29,32},{33,36}... | collective-permute-start | bytes 1572872 | tf_op jit(solution)/shard_map/ppermute | solution.py:318
  203.2 45.1 %collective-permute-start.14 = (bf16[256,1024]{1,0:T(8,128)(2,1)}, bf16[256,1024]{1,0:T(8,128)(2,1)}, u32[]{:S(2)}, u32[]{:S(2)}) collective-permute-start(bf16[256,1024]{1,0:T(8,128)(2,1)} %get-tuple-element.25), channel_id=1, source_target_pairs={{0,1},{1,0},{2,3},{3,2},{4,5},{5,4},{6,7},{7,6},{8,9},{9,8},{10,11... | collective-permute-start | bytes 1572872 | tf_op jit(solution)/shard_map/ppermute | solution.py:323
  275.2 7.6 %copy-start.6 = (f32[5376]{0:T(1024)S(1)}, f32[5376]{0:T(1024)}, u32[]{:S(2)}) copy-start(f32[5376]{0:T(1024)} %param.17) | copy-start | bytes 64516
  280.9 4.6 %collective-permute-start.17 = (bf16[256,2688]{1,0:T(8,128)(2,1)S(1)}, bf16[256,2688]{1,0:T(8,128)(2,1)S(1)}, u32[]{:S(2)}, u32[]{:S(2)}) collective-permute-start(bf16[256,2688]{1,0:T(8,128)(2,1)S(1)} %get-tuple-element.22), channel_id=1, source_target_pairs={{0,2},{2,0},{1,3},{3,1},{4,6},{6,4},{5,7},{7,5},{8,10},{10,8},{9,1... | collective-permute-start | bytes 4128776 | tf_op jit(solution)/shard_map/ppermute | solution.py:336
  282.7 4.7 %collective-permute-start.16 = (bf16[256,2688]{1,0:T(8,128)(2,1)S(1)}, bf16[256,2688]{1,0:T(8,128)(2,1)S(1)}, u32[]{:S(2)}, u32[]{:S(2)}) collective-permute-start(bf16[256,2688]{1,0:T(8,128)(2,1)S(1)} %get-tuple-element.21), channel_id=1, source_target_pairs={{0,2},{2,0},{1,3},{3,1},{4,6},{6,4},{5,7},{7,5},{8,10},{10,8},{9,1... | collective-permute-start | bytes 4128776 | tf_op jit(solution)/shard_map/ppermute | solution.py:334
Sparse Core Ops, SparseCore 0:
  14.1 154.9 all-gather.1

commit v4 on v2

--- a/solution.py
+++ b/solution.py
@@ -20,6 +20,7 @@
 BF = jnp.bfloat16
 F32 = jnp.float32
 MIB = 1 << 20
+SCALARS = pl.BlockSpec(memory_space=pltpu.SMEM)
 
 
 def cost(flops, size, exps=0):
@@ -59,6 +60,24 @@
         out_ref[:, at] = query.astype(BF)
 
 
+def chip_rows_kernel(core_ref, mine_ref, other_ref, out_ref):
+    core = core_ref[0]
+    for ref, which in ((mine_ref, core), (other_ref, 1 - core)):
+        out_ref[pl.ds(pl.multiple_of(which * BLOCK, BLOCK), BLOCK), :] = ref[...]
+
+
+def chip_rows(core, mine, other):
+    whole = pl.BlockSpec(memory_space=pltpu.VMEM)
+    return pl.pallas_call(
+        chip_rows_kernel,
+        out_shape=pltpu.VMEM((2 * BLOCK, WIDTH), BF),
+        in_specs=[SCALARS, whole, whole],
+        out_specs=whole,
+        compiler_params=params(16),
+        cost_estimate=cost(0, 12 * MIB),
+    )(core.astype(jnp.int32).reshape(1), mine, other)
+
+
 def projection(kernel, x, weights, gain, cosine, sine, where):
     rows = x.shape[0]
     whole = pl.BlockSpec(memory_space=pltpu.VMEM)
@@ -68,67 +87,103 @@
         grid=(4,),
         in_specs=[whole, pl.BlockSpec((WIDTH, 256), where), whole, whole, whole],
         out_specs=pl.BlockSpec((rows, 256), lambda t: (0, t)),
-        compiler_params=params(48),
+        compiler_params=params(20),
         cost_estimate=cost(2 * rows * WIDTH * 1024, 2 * WIDTH * 1536),
     )(x, weights, gain, cosine, sine)
 
 
-def attention_kernel(flag_ref, q_ref, ok, ov, zk, zv, ak, av, bk, bv, ck, cv, out_ref):
-    core = flag_ref[2]
-    lane = lax.broadcasted_iota(jnp.int32, (BLOCK, HEAD), 1)
-    ones = jnp.where(lane == 0, 1.0, 0.0).astype(F32)
-    early = (ones * flag_ref[0].astype(F32)).astype(BF)
-    before = (ones * flag_ref[1].astype(F32)).astype(BF)
-    ones = ones.astype(BF)
-    first, second = slice(0, BLOCK), slice(BLOCK, 2 * BLOCK)
-    own0 = (ok.at[first], ov.at[first], ones)
-    own1 = (ok.at[second], ov.at[second], ones)
-    far = (zk.at[first], zv.at[first], early)
-    mid = (zk.at[second], zv.at[second], early)
-    prior = (ak, av, before)
-    gap = (bk, bv, early)
-    link = (ck, cv, ones)
+def attend(query, keys, total):
     row = lax.rem(lax.broadcasted_iota(jnp.int32, (2 * BLOCK, BLOCK), 0), BLOCK)
     col = lax.broadcasted_iota(jnp.int32, (2 * BLOCK, BLOCK), 1)
-    for part, keys in enumerate(((far, gap, mid, prior, own0), (mid, prior, own0, link, own1))):
-        at = slice(part * BLOCK, (part + 1) * BLOCK)
-        query = jnp.concatenate([q_ref[at, :HEAD], q_ref[at, HEAD:]], axis=0)
-        total = jnp.zeros((2 * BLOCK, 2 * HEAD), F32)
-        for n, (k, v, tail) in enumerate(keys):
-            score = lax.dot_general(
-                query, k[...], (((1,), (1,)), ((), ())), preferred_element_type=F32
-            )
-            raised = jnp.exp2(score)
-            if n == 0:
-                raised = jnp.where(col > row, raised, 0.0)
-            if n == 4:
-                raised = jnp.where(col <= row, raised, 0.0)
-            value = jnp.concatenate([v[...], tail], axis=1)
-            total += jnp.dot(raised.astype(BF), value, preferred_element_type=F32)
+    for key, value, count, edge in keys:
+        score = lax.dot_general(query, key, (((1,), (1,)), ((), ())), preferred_element_type=F32)
+        raised = jnp.exp2(score)
+        if edge == "oldest":
+            raised = jnp.where(col > row, raised, 0.0)
+        if edge == "own":
+            raised = jnp.where(col <= row, raised, 0.0)
+        counted = jnp.concatenate([value, count], axis=1)
+        total += jnp.dot(raised.astype(BF), counted, preferred_element_type=F32)
+    return total
+
+
+def counts(flag):
+    lane = lax.broadcasted_iota(jnp.int32, (BLOCK, HEAD), 1)
+    return jnp.where(lane == 0, flag.astype(F32), 0.0).astype(BF)
+
+
+def both_heads(q_ref, part):
+    at = slice(part * BLOCK, (part + 1) * BLOCK)
+    return jnp.concatenate([q_ref[at, :HEAD], q_ref[at, HEAD:]], axis=0)
+
+
+def near_kernel(flag_ref, q_ref, ok, ov, zk, zv, sum_ref):
+    early, always = counts(flag_ref[0]), counts(jnp.int32(1))
+    first, second = slice(0, BLOCK), slice(BLOCK, 2 * BLOCK)
+    keys = (
+        (
+            (zk[first], zv[first], early, "oldest"),
+            (zk[second], zv[second], early, ""),
+            (ok[first], ov[first], always, "own"),
+        ),
+        (
+            (zk[second], zv[second], early, "oldest"),
+            (ok[first], ov[first], always, ""),
+            (ok[second], ov[second], always, "own"),
+        ),
+    )
+    for part in range(2):
+        start = jnp.zeros((2 * BLOCK, 2 * HEAD), F32)
+        sum_ref[0, part] = attend(both_heads(q_ref, part), keys[part], start)
+
+
+def far_kernel(flag_ref, q_ref, sum_ref, pk, pv, gk, gv, lk, lv, out_ref):
+    core = flag_ref[2]
+    early, late, always = counts(flag_ref[0]), counts(flag_ref[1]), counts(jnp.int32(1))
+    gap = (gk[...], gv[...], early, "")
+    prior = (pk[...], pv[...], late, "")
+    link = (lk[...], lv[...], always, "")
+    for part, keys in enumerate(((gap, prior), (prior, link))):
+        total = attend(both_heads(q_ref, part), keys, sum_ref[0, part])
         mixed = (total[:, :HEAD] / total[:, HEAD : HEAD + 1]).astype(BF)
         to = pl.multiple_of(lax.rem(part + core, 2) * BLOCK, BLOCK)
         out_ref[pl.ds(to, BLOCK), :HEAD] = mixed[:BLOCK]
         out_ref[pl.ds(to, BLOCK), HEAD:] = mixed[BLOCK:]
 
 
-def attention(flags, queries, own, behind, prior, gap, link):
-    def pair(rows):
-        return [
-            pl.BlockSpec((rows, HEAD), lambda j: (0, j)),
-            pl.BlockSpec((rows, HEAD), lambda j: (0, j + 4)),
-        ]
-
-    wide = pl.BlockSpec((2 * BLOCK, 2 * HEAD), lambda j: (0, j))
-    return pl.pallas_call(
-        attention_kernel,
+def head_pair(rows):
+    return [
+        pl.BlockSpec((rows, HEAD), lambda j: (0, j)),
+        pl.BlockSpec((rows, HEAD), lambda j: (0, j + 4)),
+    ]
+
+
+QUERY_PAIR = pl.BlockSpec((2 * BLOCK, 2 * HEAD), lambda j: (0, j))
+SUMS = pl.BlockSpec((1, 2, 2 * BLOCK, 2 * HEAD), lambda j: (j, 0, 0, 0))
+
+
+def near_attention(flags, queries, own, behind):
+    return pl.pallas_call(
+        near_kernel,
+        out_shape=jax.ShapeDtypeStruct((4, 2, 2 * BLOCK, 2 * HEAD), F32),
+        grid=(4,),
+        in_specs=[SCALARS, QUERY_PAIR] + head_pair(512) + head_pair(512),
+        out_specs=SUMS,
+        compiler_params=params(16),
+        cost_estimate=cost(8 * 512 * 768 * 512, 6 * MIB, 8 * 512 * 768),
+    )(flags, queries, own, own, behind, behind)
+
+
+def far_attention(flags, queries, sums, prior, gap, link):
+    return pl.pallas_call(
+        far_kernel,
         out_shape=jax.ShapeDtypeStruct((2 * BLOCK, 1024), BF),
         grid=(4,),
-        in_specs=[pl.BlockSpec(memory_space=pltpu.SMEM), wide]
-        + pair(512) + pair(512) + pair(256) + pair(256) + pair(256),
-        out_specs=wide,
-        compiler_params=params(32),
-        cost_estimate=cost(8 * 512 * 1280 * 512, 6 * MIB, 8 * 512 * 1280),
-    )(flags, queries, own, own, behind, behind, prior, prior, gap, gap, link, link)
+        in_specs=[SCALARS, QUERY_PAIR, SUMS] + head_pair(256) * 3,
+        out_specs=QUERY_PAIR,
+        compiler_params=params(16),
+        cost_estimate=cost(8 * 512 * 512 * 512, 6 * MIB, 8 * 512 * 512),
+    )(flags, queries, sums, prior, prior, gap, gap, link, link)
 
 
 def out_kernel(att_ref, low_ref, high_ref, own_ref, other_ref):
@@ -151,14 +206,14 @@
         grid=(steps,),
         in_specs=[
             pl.BlockSpec(memory_space=pltpu.VMEM),
-            pl.BlockSpec((tile, 512), lambda i: (first + i, 2)),
-            pl.BlockSpec((tile, 512), lambda i: (first + i + 2 * steps, 2)),
+            pl.BlockSpec((tile, 512), lambda i: (first + i, 0)),
+            pl.BlockSpec((tile, 512), lambda i: (first + i + 2 * steps, 0)),
         ],
         out_specs=(
             pl.BlockSpec((BLOCK, tile), lambda i: (0, i)),
             pl.BlockSpec((BLOCK, tile), lambda i: (0, i)),
         ),
-        compiler_params=params(32),
+        compiler_params=params(16),
         cost_estimate=cost(2 * 512 * 1024 * WIDTH // 2, 10 * MIB),
     )(attended, weights, weights)
 
@@ -186,7 +241,7 @@
         grid=(BLOCK // rows,),
         in_specs=[wide, half, half, half, half, pl.BlockSpec((1, WIDTH), lambda i: (0, 0))],
         out_specs=wide,
-        compiler_params=params(32),
+        compiler_params=params(16),
         cost_estimate=cost(10 * BLOCK * WIDTH, 14 * MIB),
     )(tokens, own0, own1, got0, got1, gain)
 
@@ -237,42 +292,40 @@
     mean_square = jnp.mean(plain * plain, axis=-1, keepdims=True)
     normed = (plain * lax.rsqrt(mean_square + epsilon) * norm_gain).astype(BF)
     other = lax.ppermute(normed, "core", [(0, 1), (1, 0)])
-    x = jnp.concatenate(
-        [jnp.where(core == 0, normed, other), jnp.where(core == 0, other, normed)], axis=0
-    )
+    x = chip_rows(core, normed, other)
     row = jnp.arange(2 * BLOCK, dtype=jnp.int32)
     positions = (4 * chip + side) * BLOCK + row + (row // BLOCK) * BLOCK
     cosine, sine = rotations(positions)
 
-    full, x, cosine, sine = lax.optimization_barrier((full, x, cosine, sine))
 
     own = projection(
         key_value_kernel, x, full, key_gain.reshape(1, HEAD), cosine, sine,
         lambda t: (lax.rem(t, 2), 2 + t // 2),
     )
     first, second = own[:BLOCK], own[BLOCK:]
-    mine = jnp.where(side == 0, first, second)
-    swap = jnp.where(side == 0, second, first)
     line = CHIPS + ("x_hi",)
     chips = 32
-    prior = lax.ppermute(mine, line, [(i, i + 1) for i in range(2 * chips - 1)])
-    gap = lax.ppermute(
-        swap, line,
-        [(2 * i + 1, 2 * i + 2) for i in range(chips - 1)]
-        + [(2 * i, 2 * i + 3) for i in range(chips - 1)],
-    )
-    link = lax.ppermute(swap, "x_hi", [(0, 1), (1, 0)])
+    swap = [(0, 1), (1, 0)]
     behind = lax.ppermute(own, CHIPS, [(i, i + 1) for i in range(chips - 1)])
+    link = lax.ppermute(jnp.where(side == 0, second, first), "x_hi", swap)
+    prior = lax.ppermute(
+        jnp.where(side == 0, first, second), line, [(i, i + 1) for i in range(2 * chips - 1)]
+    )
     queries = projection(
         query_kernel, x, full, query_gain.reshape(1, HEAD), cosine, sine,
         lambda t: (t // 2, lax.rem(t, 2)),
     )
+    queries, behind = lax.optimization_barrier((queries, behind))
+    gap = lax.ppermute(jnp.where(side == 0, behind[BLOCK:], behind[:BLOCK]), "x_hi", swap)
     later = (chip > 0).astype(jnp.int32)
     flags = jnp.stack([later, jnp.maximum(later, side), core]).astype(jnp.int32)
-    attended = attention(flags, queries, own, behind, prior, gap, link)
-    own0, send0 = out_projection(attended, full, 0)
+    sums = near_attention(flags, queries, own, behind)
+    out_rows, _ = lax.optimization_barrier((full, own))
+    out_rows = out_rows[:, 1024:]
+    attended = far_attention(flags, queries, sums, prior, gap, link)
+    own0, send0 = out_projection(attended, out_rows, 0)
     got0 = lax.ppermute(send0, "core", [(0, 1), (1, 0)])
-    own1, send1 = out_projection(attended, full, 1)
+    own1, send1 = out_projection(attended, out_rows, 1)
     got1 = lax.ppermute(send1, "core", [(0, 1), (1, 0)])
     return ending(tokens, own0, own1, got0, got1, post_gain.reshape(1, WIDTH))
 

time: 280 us -> 282 us (level)
  waiting for transfers between devices: 183 us -> 165 us
  local copies, waits for them, and re-layouts: 4.62 us -> 18.8 us
  starting transfers between devices: 14.8 us -> 24.2 us
  other arithmetic: 11.5 us -> 8.59 us
    ppermute x3, waiting for transfers between devices: 30.7 us -> 11.7 us  [the longest x1 11.1 us: on_device(): lax.ppermute(jnp.where(side == 0, behind[BLOCK:], behind[:BLOCK]), 'x_hi'...]
    ppermute x3, starting transfers between devices: 8.5 us -> 17.9 us  [the longest x1 12.9 us: on_device(): lax.ppermute(jnp.where(side == 0, behind[BLOCK:], behind[:BLOCK]), 'x_hi'...]
    unnamed x10 -> x20, local copies, waits for them, and re-layouts: 0.03 us -> 8.57 us
    slice x0 -> x1, local copies, waits for them, and re-layouts: none -> 5.69 us  [on_device(): out_rows = out_rows[:, 1024:]]
    pallas_call x1 -> x3, Pallas kernels: 9.21 us -> 14.3 us  [the longest x1 6.32 us: near_attention(): pl.pallas_call(near_kernel, out_shape=jax.ShapeDtypeStruct((4, 2, 2 * BLO...]
    pallas_call x2, Pallas kernels: 23.6 us -> 20.3 us  [projection(): pl.pallas_call(kernel, out_shape=jax.ShapeDtypeStruct((rows, 1024), BF),...]
    pallas_call x2, Pallas kernels: 11.4 us -> 8.33 us  [out_projection(): pl.pallas_call(out_kernel, out_shape=(jax.ShapeDtypeStruct((BLOCK, WIDTH...]
  transfers between devices with their start and end apart: 8 -> 8, of which waited for: 5 -> 7; matrix products, arithmetic and copies ran while one was open for 4% -> 5% of each run, Pallas kernels for 4% -> 7%
where the time goes in v4:
time: 282 us; the launch traced here: 281 us
  waiting for transfers between devices  165 us (59%)
  Pallas kernels  46.3 us (16%)
  starting transfers between devices  24.2 us (9%)
  local copies, waits for them, and re-layouts  18.8 us (7%)
  between operations  13.6 us (5%)
  other arithmetic  8.59 us (3%)
  blocking collectives  4.44 us (2%)
    all_gather x1, waiting for transfers between devices, on_device(): lax.all_gather(quarter_rows([query_weight, key_matrix, value_matrix, out_...  144 us
    pallas_call x2, Pallas kernels, projection(): pl.pallas_call(kernel, out_shape=jax.ShapeDtypeStruct((rows, 1024), BF),...  20.3 us
    ppermute x1, starting transfers between devices, on_device(): lax.ppermute(jnp.where(side == 0, behind[BLOCK:], behind[:BLOCK]), 'x_hi'...  12.9 us
    ppermute x1, waiting for transfers between devices, on_device(): lax.ppermute(jnp.where(side == 0, behind[BLOCK:], behind[:BLOCK]), 'x_hi'...  11.1 us
    unnamed x20, local copies, waits for them, and re-layouts  8.57 us
    pallas_call x2, Pallas kernels, out_projection(): pl.pallas_call(out_kernel, out_shape=(jax.ShapeDtypeStruct((BLOCK, WIDTH...  8.33 us
    pallas_call x1, Pallas kernels, near_attention(): pl.pallas_call(near_kernel, out_shape=jax.ShapeDtypeStruct((4, 2, 2 * BLO...  6.32 us
    slice x1, local copies, waits for them, and re-layouts, on_device(): out_rows = out_rows[:, 1024:]  5.69 us
  transfers between devices with their start and end apart: 8, of which 7 were waited for; matrix products, arithmetic and copies ran while one was open for 5% of the time, Pallas kernels for 7%

profile of v4, /device:TPU:125, one launch (start us, length us, event | category | flops | bytes accessed | tf_op | source)
XLA Modules:
  0.0 281.2 jit_solution(1081428671183945048)
XLA Ops:
  6.5 0.0 all-gather.2.cloned.1.call-start
  6.5 0.9 fusion.11
  7.5 0.0 copy-start.3
  7.5 1.0 fusion.13
  8.5 0.8 fusion.12
  9.3 0.9 fusion.10
  10.3 0.1 pad_maximum_fusion
  10.3 0.0 copy-start.8
  10.4 4.4 %all_to_all.5 = bf16[2,84,1536]{2,1,0:T(8,128)(2,1)S(1)} all-to-all(bf16[2,84,1536]{2,1,0:T(8,128)(2,1)S(1)} %pad_maximum_fusion), channel_id=1, replica_groups=mesh['x_lo'=2,'y'=4,'z'=4,'core'=2,'x_hi'=2] {'core'}, dimensions={0} | all-to-all | bytes 1032192 | tf_op jit(solution)/shard_map/all_to_all | solution.py:266
  14.8 0.9 reshape.47
  15.7 0.0 all-gather.2.cloned.1.call-update
  15.7 0.0 copy-done.3
  15.7 0.6 fusion
  16.4 0.0 copy-done.8
  16.4 2.3 fusion.2.mine_ref
  18.6 0.4 collective-permute-start
  19.0 1.0 fusion.3
  20.0 0.2 pad_maximum_fusion.1
  20.2 3.8 %collective-permute-done.other_ref = bf16[256,5376]{1,0:T(8,128)(2,1)} collective-permute-done((bf16[256,5376]{1,0:T(8,128)(2,1)}, bf16[256,5376]{1,0:T(8,128)(2,1)}, u32[]{:S(2)}, u32[]{:S(2)}) %collective-permute-start) | collective-permute-done | bytes 2752544 | tf_op jit(solution)/shard_map/ppermute | solution.py:294
  24.1 0.0 copy-start.6
  24.1 3.0 %shard_map.91.x_ref = bf16[512,5376]{1,0:T(8,128)(2,1)S(1)} custom-call(s32[1]{0:T(128)} %bitcast.2.core_ref, bf16[256,5376]{1,0:T(8,128)(2,1)} %fusion.2.mine_ref, bf16[256,5376]{1,0:T(8,128)(2,1)} %collective-permute-done.other_ref), custom_call_target="tpu_custom_call" | custom-call | bytes 12582912 | tf_op jit(solution)/shard_map/pallas_call | solution.py:71
  27.0 0.0 copy-start
  27.1 2.5 copy-done
  29.5 144.0 %all-gather.2.cloned.1.call-done.w_ref = bf16[10752,1536]{1,0:T(8,128)(2,1)} async-done(((bf16[168,1536]{1,0:T(8,128)(2,1)}), bf16[10752,1536]{1,0:T(8,128)(2,1)}) %all-gather.2.cloned.1.call-update) | async-done | bytes 33030160 | tf_op jit(solution)/shard_map/all_gather | solution.py:284
  173.5 0.0 copy-done.6
  173.5 0.0 copy-start.1
  173.5 2.6 copy-done.1
  176.1 0.0 copy-start.7
  176.1 10.0 %shard_map.93.ok.ov = bf16[512,1024]{1,0:T(8,128)(2,1)} custom-call(bf16[512,5376]{1,0:T(8,128)(2,1)S(1)} %copy-done.1, bf16[10752,1536]{1,0:T(8,128)(2,1)} %all-gather.2.cloned.1.call-done.w_ref, f32[1,128]{1,0:T(1,128)S(1)} %bitcast.9, f32[512,128]{1,0:T(8,128)S(1)} %get-tuple-element.34.cos_ref, f32[512,128]{1,0:T(8,128)S(1)} %get-tuple-element.35.sin_ref), custom_call_target="tpu_custom_call" | custom-call | flops 5637144576 | bytes 16515072 | tf_op jit(solution)/shard_map/pallas_call | solution.py:84
  186.1 4.2 %collective-permute-start.1 = (bf16[512,1024]{1,0:T(8,128)(2,1)}, bf16[512,1024]{1,0:T(8,128)(2,1)}, u32[]{:S(2)}, u32[]{:S(2)}) collective-permute-start(bf16[512,1024]{1,0:T(8,128)(2,1)} %shard_map.93.ok.ov), channel_id=1, source_target_pairs={{0,4},{4,8},{8,12},{12,16},{16,20},{20,24},{24,28},{28,32},{32,36}... | collective-permute-start | bytes 3145736 | tf_op jit(solution)/shard_map/ppermute | solution.py:309
  190.3 2.2 broadcast_select_fusion
  192.6 2.4 collective-permute-start.2
  194.9 2.6 collective-permute-start.4
  197.5 0.0 copy-done.7
  197.5 0.0 copy-start.2
  197.5 2.6 copy-done.2
  200.1 10.3 %shard_map.92.q_ref = bf16[512,1024]{1,0:T(8,128)(2,1)S(1)} custom-call(bf16[512,5376]{1,0:T(8,128)(2,1)S(1)} %copy-done.2, bf16[10752,1536]{1,0:T(8,128)(2,1)} %all-gather.2.cloned.1.call-done.w_ref, f32[1,128]{1,0:T(1,128)S(1)} %bitcast.10, f32[512,128]{1,0:T(8,128)S(1)} %get-tuple-element.34.cos_ref, f32[512,128]{1,0:T(8,128)S(1)} %get-tuple-element.35.sin_ref), custom_call_target="tpu_custom_call" | custom-call | flops 5637144576 | bytes 16515072 | tf_op jit(solution)/shard_map/pallas_call | solution.py:84
  210.4 0.0 copy-start.4
  210.4 1.0 copy-done.4
  211.3 1.1 collective-permute-done.1.zk.zv
  212.4 2.1 slice_select_fusion
  214.5 12.9 %collective-permute-start.3 = (bf16[256,1024]{1,0:T(8,128)(2,1)}, bf16[256,1024]{1,0:T(8,128)(2,1)S(1)}, u32[]{:S(2)}, u32[]{:S(2)}) collective-permute-start(bf16[256,1024]{1,0:T(8,128)(2,1)} %slice_select_fusion), channel_id=1, source_target_pairs={{0,1},{1,0},{2,3},{3,2},{4,5},{5,4},{6,7},{7,6},{8,9},{9,8},{10,11... | collective-permute-start | bytes 1572872 | tf_op jit(solution)/shard_map/ppermute | solution.py:319
  227.4 0.1 pad_add_fusion.flag_ref
  227.5 0.0 copy-start.5
  227.5 5.7 %slice.51.low_ref.high_ref = bf16[10752,512]{1,0:T(8,128)(2,1)S(1)} slice(bf16[10752,1536]{1,0:T(8,128)(2,1)} %all-gather.2.cloned.1.call-done.w_ref), slice={[0:10752], [1024:1536]} | slice | bytes 22020096 | tf_op jit(solution)/shard_map/slice | solution.py:324
  233.2 0.0 copy-done.5
  233.2 6.3 %shard_map.94.sum_ref = f32[4,2,512,256]{3,2,1,0:T(8,128)S(1)} custom-call(s32[3]{0:T(128)S(1)} %pad_add_fusion.flag_ref, bf16[512,1024]{1,0:T(8,128)(2,1)S(1)} %copy-done.5, bf16[512,1024]{1,0:T(8,128)(2,1)} %shard_map.93.ok.ov, bf16[512,1024]{1,0:T(8,128)(2,1)} %shard_map.93.ok.ov, bf16[512,1024]{1,0:T(8,128)(2,1)} %collective-permute-done.1.zk.zv, ...), custom_call_target="tpu_custom_call" | custom-call | flops 1610612736 | bytes 6291456 | tf_op jit(solution)/shard_map/pallas_call | solution.py:166
  239.5 0.0 collective-permute-done.2.pk.pv
  239.5 0.5 collective-permute-done.4.lk.lv
  240.1 11.1 %collective-permute-done.3.gk.gv = bf16[256,1024]{1,0:T(8,128)(2,1)S(1)} collective-permute-done((bf16[256,1024]{1,0:T(8,128)(2,1)}, bf16[256,1024]{1,0:T(8,128)(2,1)S(1)}, u32[]{:S(2)}, u32[]{:S(2)}) %collective-permute-start.3) | collective-permute-done | bytes 524320 | tf_op jit(solution)/shard_map/ppermute | solution.py:319
  251.2 5.0 %shard_map.95.att_ref = bf16[512,1024]{1,0:T(8,128)(2,1)S(1)} custom-call(s32[3]{0:T(128)S(1)} %pad_add_fusion.flag_ref, bf16[512,1024]{1,0:T(8,128)(2,1)S(1)} %copy-done.5, f32[4,2,512,256]{3,2,1,0:T(8,128)S(1)} %shard_map.94.sum_ref, bf16[256,1024]{1,0:T(8,128)(2,1)} %collective-permute-done.2.pk.pv, bf16[256,1024]{1,0:T(8,128)(2,1)} %collective-permute-done.2.pk.pv, ...), custom_call_target="tpu_custom_call" | custom-call | flops 1073741824 | bytes 6291456 | tf_op jit(solution)/shard_map/pallas_call | solution.py:178
  256.2 4.2 %shard_map.96 = (f32[256,2688]{1,0:T(8,128)S(1)}, bf16[256,2688]{1,0:T(8,128)(2,1)S(1)}) custom-call(bf16[512,1024]{1,0:T(8,128)(2,1)S(1)} %shard_map.95.att_ref, bf16[10752,512]{1,0:T(8,128)(2,1)S(1)} %slice.51.low_ref.high_ref, bf16[10752,512]{1,0:T(8,128)(2,1)S(1)} %slice.51.low_ref.high_ref), custom_call_target="tpu_custom_call" | custom-call | flops 2818572288 | bytes 10485760 | tf_op jit(solution)/shard_map/pallas_call | solution.py:200
  260.4 0.0 copy-start.9
  260.4 4.2 %shard_map.97 = (f32[256,2688]{1,0:T(8,128)S(1)}, bf16[256,2688]{1,0:T(8,128)(2,1)S(1)}) custom-call(bf16[512,1024]{1,0:T(8,128)(2,1)S(1)} %shard_map.95.att_ref, bf16[10752,512]{1,0:T(8,128)(2,1)S(1)} %slice.51.low_ref.high_ref, bf16[10752,512]{1,0:T(8,128)(2,1)S(1)} %slice.51.low_ref.high_ref), custom_call_target="tpu_custom_call" | custom-call | flops 2818572288 | bytes 10485760 | tf_op jit(solution)/shard_map/pallas_call | solution.py:200
  264.6 1.6 collective-permute-start.5
  266.2 0.1 collective-permute-start.6
  266.3 0.0 copy-done.9
  266.3 2.6 collective-permute-done.5.got0
  269.0 2.0 collective-permute-done.6.got1
  270.9 3.4 %shard_map.98 = bf16[256,5376]{1,0:T(8,128)(2,1)} custom-call(bf16[256,5376]{1,0:T(8,128)(2,1)S(1)} %copy-done.3, f32[256,2688]{1,0:T(8,128)S(1)} %get-tuple-element.15.own0, f32[256,2688]{1,0:T(8,128)S(1)} %get-tuple-element.16.own1, bf16[256,2688]{1,0:T(8,128)(2,1)S(1)} %collective-permute-done.5.got0, bf16[256,2688]{1,0:T(8,128)(2,1)S(1)} %collective-permute-done.6.got1, ...), custom_call_target="tpu_custom_call" | custom-call | flops 13762560 | bytes 14680064 | tf_op jit(solution)/shard_map/pallas_call | solution.py:238
  (5 shorter events, 0.1 us)
Async XLA Ops:
  6.5 167.0 %all-gather.2.cloned.1.call-start = ((), (), s32[]{:S(2)}) async-start(), calls=%async_computation.1 | async-start | bytes 33546240 | tf_op jit(solution)/shard_map/all_gather | solution.py:284
  7.5 8.2 %copy-start.3 = (bf16[256,5376]{1,0:T(8,128)(2,1)S(1)}, bf16[256,5376]{1,0:T(8,128)(2,1)}, u32[]{:S(2)}) copy-start(bf16[256,5376]{1,0:T(8,128)(2,1)} %tok_ref.1) | copy-start | bytes 8257540
  10.3 6.0 %copy-start.8 = (f32[5376]{0:T(1024)S(1)}, f32[5376]{0:T(1024)}, u32[]{:S(2)}) copy-start(f32[5376]{0:T(1024)} %param.10) | copy-start | bytes 64516
  18.6 5.4 %collective-permute-start = (bf16[256,5376]{1,0:T(8,128)(2,1)}, bf16[256,5376]{1,0:T(8,128)(2,1)}, u32[]{:S(2)}, u32[]{:S(2)}) collective-permute-start(bf16[256,5376]{1,0:T(8,128)(2,1)} %fusion.2.mine_ref), channel_id=1, source_target_pairs={{0,2},{2,0},{1,3},{3,1},{4,6},{6,4},{5,7},{7,5},{8,10},{10,8},{9,1... | collective-permute-start | bytes 8257544 | tf_op jit(solution)/shard_map/ppermute | solution.py:294
  24.1 149.4 %copy-start.6 = (f32[128]{0:T(128)S(1)}, f32[128]{0:T(128)}, u32[]{:S(2)}) copy-start(f32[128]{0:T(128)} %param.16) | copy-start | bytes 1540
  27.0 2.5 copy-start
  173.5 2.6 copy-start.1
  176.1 21.5 %copy-start.7 = (f32[128]{0:T(128)S(1)}, f32[128]{0:T(128)}, u32[]{:S(2)}) copy-start(f32[128]{0:T(128)} %param.15) | copy-start | bytes 1540
  186.1 26.3 %collective-permute-start.1 = (bf16[512,1024]{1,0:T(8,128)(2,1)}, bf16[512,1024]{1,0:T(8,128)(2,1)}, u32[]{:S(2)}, u32[]{:S(2)}) collective-permute-start(bf16[512,1024]{1,0:T(8,128)(2,1)} %shard_map.93.ok.ov), channel_id=1, source_target_pairs={{0,4},{4,8},{8,12},{12,16},{16,20},{20,24},{24,28},{28,32},{32,36}... | collective-permute-start | bytes 3145736 | tf_op jit(solution)/shard_map/ppermute | solution.py:309
  192.6 47.0 %collective-permute-start.2 = (bf16[256,1024]{1,0:T(8,128)(2,1)}, bf16[256,1024]{1,0:T(8,128)(2,1)}, u32[]{:S(2)}, u32[]{:S(2)}) collective-permute-start(bf16[256,1024]{1,0:T(8,128)(2,1)} %get-tuple-element.20), channel_id=1, source_target_pairs={{0,1},{1,4},{4,5},{5,8},{8,9},{9,12},{12,13},{13,16},{16,17},{17,2... | collective-permute-start | bytes 1572872 | tf_op jit(solution)/shard_map/ppermute | solution.py:311
  194.9 45.1 %collective-permute-start.4 = (bf16[256,1024]{1,0:T(8,128)(2,1)}, bf16[256,1024]{1,0:T(8,128)(2,1)}, u32[]{:S(2)}, u32[]{:S(2)}) collective-permute-start(bf16[256,1024]{1,0:T(8,128)(2,1)} %get-tuple-element.19), channel_id=1, source_target_pairs={{0,1},{1,0},{2,3},{3,2},{4,5},{5,4},{6,7},{7,6},{8,9},{9,8},{10,11... | collective-permute-start | bytes 1572872 | tf_op jit(solution)/shard_map/ppermute | solution.py:310
  197.5 2.6 copy-start.2
  210.4 1.0 copy-start.4
  214.5 36.7 %collective-permute-start.3 = (bf16[256,1024]{1,0:T(8,128)(2,1)}, bf16[256,1024]{1,0:T(8,128)(2,1)S(1)}, u32[]{:S(2)}, u32[]{:S(2)}) collective-permute-start(bf16[256,1024]{1,0:T(8,128)(2,1)} %slice_select_fusion), channel_id=1, source_target_pairs={{0,1},{1,0},{2,3},{3,2},{4,5},{5,4},{6,7},{7,6},{8,9},{9,8},{10,11... | collective-permute-start | bytes 1572872 | tf_op jit(solution)/shard_map/ppermute | solution.py:319
  227.5 5.7 %copy-start.5 = (bf16[512,1024]{1,0:T(8,128)(2,1)S(1)}, bf16[512,1024]{1,0:T(8,128)(2,1)}, u32[]{:S(2)}) copy-start(bf16[512,1024]{1,0:T(8,128)(2,1)} %copy-done.4) | copy-start | bytes 3145732
  260.4 5.9 %copy-start.9 = (f32[5376]{0:T(1024)S(1)}, f32[5376]{0:T(1024)}, u32[]{:S(2)}) copy-start(f32[5376]{0:T(1024)} %param.17) | copy-start | bytes 64516
  264.6 4.4 %collective-permute-start.5 = (bf16[256,2688]{1,0:T(8,128)(2,1)S(1)}, bf16[256,2688]{1,0:T(8,128)(2,1)S(1)}, u32[]{:S(2)}, u32[]{:S(2)}) collective-permute-start(bf16[256,2688]{1,0:T(8,128)(2,1)S(1)} %get-tuple-element.17), channel_id=1, source_target_pairs={{0,2},{2,0},{1,3},{3,1},{4,6},{6,4},{5,7},{7,5},{8,10},{10,8},{9,1... | collective-permute-start | bytes 4128776 | tf_op jit(solution)/shard_map/ppermute | solution.py:327
  266.2 4.7 %collective-permute-start.6 = (bf16[256,2688]{1,0:T(8,128)(2,1)S(1)}, bf16[256,2688]{1,0:T(8,128)(2,1)S(1)}, u32[]{:S(2)}, u32[]{:S(2)}) collective-permute-start(bf16[256,2688]{1,0:T(8,128)(2,1)S(1)} %get-tuple-element.18), channel_id=1, source_target_pairs={{0,2},{2,0},{1,3},{3,1},{4,6},{6,4},{5,7},{7,5},{8,10},{10,8},{9,1... | collective-permute-start | bytes 4128776 | tf_op jit(solution)/shard_map/ppermute | solution.py:329
Sparse Core Ops, SparseCore 0:
  15.8 157.6 all-gather.1

commit v5 on v4

--- a/solution.py
+++ b/solution.py
@@ -37,19 +37,56 @@
     return unit * cosine + pltpu.roll(unit, HALF, axis=1) * sine
 
 
-def key_value_kernel(x_ref, w_ref, gain_ref, cos_ref, sin_ref, out_ref):
-    raw = jnp.dot(x_ref[...], w_ref[...], preferred_element_type=F32)
-
-    @pl.when(pl.program_id(0) < 2)
+def key_value_kernel(x_ref, low_ref, high_ref, gain_ref, cos_ref, sin_ref, out_ref, sum_ref):
+    step = pl.program_id(0)
+    terms = [
+        jnp.dot(x_ref[...], ref[...], preferred_element_type=F32) for ref in (low_ref, high_ref)
+    ]
+
+    @pl.when(step == 0)
     def _():
-        for h in range(2):
-            at = slice(h * HEAD, (h + 1) * HEAD)
-            key = turned(raw[:, at], gain_ref[...], cos_ref[...], sin_ref[...], 1.0)
-            out_ref[:, at] = key.astype(BF)
-
-    @pl.when(pl.program_id(0) >= 2)
+        for n in range(2):
+            sum_ref[n] = terms[n]
+
+    @pl.when(step > 0)
     def _():
-        out_ref[...] = raw.astype(BF)
+        for n in range(2):
+            sum_ref[n] += terms[n]
+
+    @pl.when(step == pl.num_programs(0) - 1)
+    def _():
+        for n in range(2):
+            for h in range(2):
+                raw = sum_ref[n, :, h * HEAD : (h + 1) * HEAD]
+                key = turned(raw, gain_ref[...], cos_ref[...], sin_ref[...], 1.0)
+                out_ref[:, (2 * n + h) * HEAD : (2 * n + h + 1) * HEAD] = key.astype(BF)
+            out_ref[:, 512 + 256 * n : 768 + 256 * n] = sum_ref[n, :, 256:].astype(BF)
+
+
+def key_values(x, weights, gain, cosine, sine):
+    rows, steps = x.shape[0], 3
+    depth = WIDTH // steps
+
+    def whole(shape):
+        return pl.BlockSpec(shape, lambda t: (0, 0))
+
+    return pl.pallas_call(
+        key_value_kernel,
+        out_shape=jax.ShapeDtypeStruct((rows, 1024), BF),
+        grid=(steps,),
+        in_specs=[
+            pl.BlockSpec((rows, depth), lambda t: (0, t)),
+            pl.BlockSpec((depth, 512), lambda t: (t, 1)),
+            pl.BlockSpec((depth, 512), lambda t: (t + steps, 1)),
+            whole((1, HEAD)),
+            whole((rows, HEAD)),
+            whole((rows, HEAD)),
+        ],
+        out_specs=whole((rows, 1024)),
+        scratch_shapes=[pltpu.VMEM((2, rows, 512), F32)],
+        compiler_params=params(60),
+        cost_estimate=cost(2 * rows * WIDTH * 1024, 2 * WIDTH * 1536),
+    )(x, weights, weights, gain, cosine, sine)
 
 
 def query_kernel(x_ref, w_ref, gain_ref, cos_ref, sin_ref, out_ref):
@@ -70,7 +107,7 @@
     whole = pl.BlockSpec(memory_space=pltpu.VMEM)
     return pl.pallas_call(
         chip_rows_kernel,
-        out_shape=pltpu.VMEM((2 * BLOCK, WIDTH), BF),
+        out_shape=jax.ShapeDtypeStruct((2 * BLOCK, WIDTH), BF),
         in_specs=[SCALARS, whole, whole],
         out_specs=whole,
         compiler_params=params(16),
@@ -137,12 +174,15 @@
         sum_ref[0, part] = attend(both_heads(q_ref, part), keys[part], start)
 
 
-def far_kernel(flag_ref, q_ref, sum_ref, pk, pv, gk, gv, lk, lv, out_ref):
-    core = flag_ref[2]
+def far_kernel(flag_ref, q_ref, sum_ref, nk, nv, ck, cv, out_ref):
+    core, side = flag_ref[2], flag_ref[3]
     early, late, always = counts(flag_ref[0]), counts(flag_ref[1]), counts(jnp.int32(1))
-    gap = (gk[...], gv[...], early, "")
-    prior = (pk[...], pv[...], late, "")
-    link = (lk[...], lv[...], always, "")
+    before = pl.ds(pl.multiple_of((1 - side) * BLOCK, BLOCK), BLOCK)
+    beside = pl.ds(pl.multiple_of(side * BLOCK, BLOCK), BLOCK)
+    gap = tuple(jnp.where(side == 0, n[beside], c[...]) for n, c in ((nk, ck), (nv, cv)))
+    link = tuple(jnp.where(side == 0, c[...], n[beside]) for n, c in ((nk, ck), (nv, cv)))
+    gap, link = gap + (early, ""), link + (always, "")
+    prior = (nk[before], nv[before], late, "")
     for part, keys in enumerate(((gap, prior), (prior, link))):
         total = attend(both_heads(q_ref, part), keys, sum_ref[0, part])
         mixed = (total[:, :HEAD] / total[:, HEAD : HEAD + 1]).astype(BF)
@@ -174,76 +214,61 @@
     )(flags, queries, own, own, behind, behind)
 
 
-def far_attention(flags, queries, sums, prior, gap, link):
+def far_attention(flags, queries, sums, near, cross):
     return pl.pallas_call(
         far_kernel,
         out_shape=jax.ShapeDtypeStruct((2 * BLOCK, 1024), BF),
         grid=(4,),
-        in_specs=[SCALARS, QUERY_PAIR, SUMS] + head_pair(256) * 3,
+        in_specs=[SCALARS, QUERY_PAIR, SUMS] + head_pair(512) + head_pair(256),
         out_specs=QUERY_PAIR,
         compiler_params=params(16),
         cost_estimate=cost(8 * 512 * 512 * 512, 6 * MIB, 8 * 512 * 512),
-    )(flags, queries, sums, prior, prior, gap, gap, link, link)
-
-
-def out_kernel(att_ref, low_ref, high_ref, own_ref, other_ref):
+    )(flags, queries, sums, near, near, cross, cross)
+
+
+def out_kernel(att_ref, low_ref, high_ref, out_ref):
     dims = (((1,), (1,)), ((), ()))
     got = lax.dot_general(att_ref[:, :512], low_ref[...], dims, preferred_element_type=F32)
     got += lax.dot_general(att_ref[:, 512:], high_ref[...], dims, preferred_element_type=F32)
-    own_ref[...] = got[:BLOCK]
-    other_ref[...] = got[BLOCK:].astype(BF)
-
-
-def out_projection(attended, weights, half):
-    tile, steps = 896, 3
-    first = half * steps
+    out_ref[...] = got.astype(out_ref.dtype)
+
+
+def out_projection(attended, weights, which, kind):
+    tile, steps = 896, 6
     return pl.pallas_call(
         out_kernel,
-        out_shape=(
-            jax.ShapeDtypeStruct((BLOCK, WIDTH // 2), F32),
-            jax.ShapeDtypeStruct((BLOCK, WIDTH // 2), BF),
-        ),
+        out_shape=jax.ShapeDtypeStruct((BLOCK, WIDTH), kind),
         grid=(steps,),
         in_specs=[
-            pl.BlockSpec(memory_space=pltpu.VMEM),
-            pl.BlockSpec((tile, 512), lambda i: (first + i, 0)),
-            pl.BlockSpec((tile, 512), lambda i: (first + i + 2 * steps, 0)),
+            pl.BlockSpec((BLOCK, 1024), lambda i: (which, 0)),
+            pl.BlockSpec((tile, 512), lambda i: (i, 0)),
+            pl.BlockSpec((tile, 512), lambda i: (i + steps, 0)),
         ],
-        out_specs=(
-            pl.BlockSpec((BLOCK, tile), lambda i: (0, i)),
-            pl.BlockSpec((BLOCK, tile), lambda i: (0, i)),
-        ),
+        out_specs=pl.BlockSpec((BLOCK, tile), lambda i: (0, i)),
         compiler_params=params(16),
-        cost_estimate=cost(2 * 512 * 1024 * WIDTH // 2, 10 * MIB),
+        cost_estimate=cost(2 * BLOCK * 1024 * WIDTH, 15 * MIB),
     )(attended, weights, weights)
 
 
-def end_kernel(tok_ref, own0, own1, got0, got1, gain_ref, out_ref):
-    middle = WIDTH // 2
-    left = own0[...] + got0[...].astype(F32)
-    right = own1[...] + got1[...].astype(F32)
-    square = jnp.sum(left * left, axis=-1, keepdims=True)
-    square += jnp.sum(right * right, axis=-1, keepdims=True)
-    factor = lax.rsqrt(square * (1.0 / WIDTH) + epsilon)
-    for n, part in enumerate((left, right)):
-        at = slice(n * middle, (n + 1) * middle)
-        scaled = part * factor * gain_ref[:, at]
-        out_ref[:, at] = (tok_ref[:, at].astype(F32) + scaled).astype(BF)
-
-
-def ending(tokens, own0, own1, got0, got1, gain):
+def end_kernel(tok_ref, own_ref, got_ref, gain_ref, out_ref):
+    whole = own_ref[...] + got_ref[...].astype(F32)
+    mean_square = jnp.mean(whole * whole, axis=-1, keepdims=True)
+    scaled = whole * lax.rsqrt(mean_square + epsilon) * gain_ref[...]
+    out_ref[...] = (tok_ref[...].astype(F32) + scaled).astype(BF)
+
+
+def ending(tokens, own, got, gain):
     rows = 64
-    half = pl.BlockSpec((rows, WIDTH // 2), lambda i: (i, 0))
     wide = pl.BlockSpec((rows, WIDTH), lambda i: (i, 0))
     return pl.pallas_call(
         end_kernel,
         out_shape=jax.ShapeDtypeStruct((BLOCK, WIDTH), BF),
         grid=(BLOCK // rows,),
-        in_specs=[wide, half, half, half, half, pl.BlockSpec((1, WIDTH), lambda i: (0, 0))],
+        in_specs=[wide, wide, wide, pl.BlockSpec((1, WIDTH), lambda i: (0, 0))],
         out_specs=wide,
-        compiler_params=params(16),
+        compiler_params=params(24),
         cost_estimate=cost(10 * BLOCK * WIDTH, 14 * MIB),
-    )(tokens, own0, own1, got0, got1, gain)
+    )(tokens, own, got, gain)
 
 
 def rotations(positions):
@@ -257,14 +282,36 @@
     )
 
 
-def quarter_rows(pieces):
-    rows = pieces[0].shape[0]
-    sides = [
-        jnp.concatenate([p[:, s * p.shape[1] // 2 : (s + 1) * p.shape[1] // 2] for p in pieces], 1)
-        for s in range(2)
-    ]
-    swapped = lax.all_to_all(jnp.stack(sides), "core", 0, 0, tiled=True)
-    return swapped.reshape(2 * rows, -1)
+def pack_kernel(core_ref, q_ref, k_ref, v_ref, o_ref, keep_ref, send_ref):
+    def pack(to_ref, side):
+        at = 0
+        for ref in (q_ref, k_ref, v_ref, o_ref):
+            width = ref.shape[1] // 2
+            to_ref[:, at : at + width] = ref[:, side * width : (side + 1) * width]
+            at += width
+
+    for core in range(2):
+
+        @pl.when(core_ref[0] == core)
+        def _():
+            pack(keep_ref, core)
+            pack(send_ref, 1 - core)
+
+
+def chip_weights(core, q, k, v, o):
+    rows = q.shape[0]
+    whole = pl.BlockSpec(memory_space=pltpu.VMEM)
+    keep, send = pl.pallas_call(
+        pack_kernel,
+        out_shape=(jax.ShapeDtypeStruct((rows, 1536), BF),) * 2,
+        in_specs=[SCALARS, whole, whole, whole, whole],
+        out_specs=(whole, whole),
+        compiler_params=params(60),
+        cost_estimate=cost(0, 1 * MIB),
+    )(core.astype(jnp.int32).reshape(1), q, k, v, o)
+    got = lax.ppermute(send, "core", [(0, 1), (1, 0)])
+    first, second = jnp.where(core == 0, keep, got), jnp.where(core == 0, got, keep)
+    return jnp.concatenate([first, second], axis=0)
 
 
 def on_device(
@@ -282,7 +329,7 @@
     side = lax.axis_index("x_hi")
     chip = lax.axis_index(CHIPS)
     full = lax.all_gather(
-        quarter_rows([query_weight, key_matrix, value_matrix, out_weight]),
+        chip_weights(core, query_weight, key_matrix, value_matrix, out_weight),
         GATHER,
         axis=0,
         tiled=True,
@@ -298,36 +345,31 @@
     cosine, sine = rotations(positions)
 
 
-    own = projection(
-        key_value_kernel, x, full, key_gain.reshape(1, HEAD), cosine, sine,
-        lambda t: (lax.rem(t, 2), 2 + t // 2),
-    )
-    first, second = own[:BLOCK], own[BLOCK:]
+    own = key_values(x, full, key_gain.reshape(1, HEAD), cosine, sine)
     line = CHIPS + ("x_hi",)
     chips = 32
-    swap = [(0, 1), (1, 0)]
+    single = jnp.where(side == 0, own[BLOCK:], own[:BLOCK])
+    near = lax.ppermute(own, line, [(i, i + 1) for i in range(2 * chips - 1)])
     behind = lax.ppermute(own, CHIPS, [(i, i + 1) for i in range(chips - 1)])
-    link = lax.ppermute(jnp.where(side == 0, second, first), "x_hi", swap)
-    prior = lax.ppermute(
-        jnp.where(side == 0, first, second), line, [(i, i + 1) for i in range(2 * chips - 1)]
+    cross = lax.ppermute(
+        single, line,
+        [(2 * i + 1, 2 * i) for i in range(chips)]
+        + [(2 * i, 2 * i + 3) for i in range(chips - 1)],
     )
     queries = projection(
         query_kernel, x, full, query_gain.reshape(1, HEAD), cosine, sine,
         lambda t: (t // 2, lax.rem(t, 2)),
     )
-    queries, behind = lax.optimization_barrier((queries, behind))
-    gap = lax.ppermute(jnp.where(side == 0, behind[BLOCK:], behind[:BLOCK]), "x_hi", swap)
     later = (chip > 0).astype(jnp.int32)
-    flags = jnp.stack([later, jnp.maximum(later, side), core]).astype(jnp.int32)
+    flags = jnp.stack([later, jnp.maximum(later, side), core, side]).astype(jnp.int32)
     sums = near_attention(flags, queries, own, behind)
     out_rows, _ = lax.optimization_barrier((full, own))
     out_rows = out_rows[:, 1024:]
-    attended = far_attention(flags, queries, sums, prior, gap, link)
-    own0, send0 = out_projection(attended, out_rows, 0)
-    got0 = lax.ppermute(send0, "core", [(0, 1), (1, 0)])
-    own1, send1 = out_projection(attended, out_rows, 1)
-    got1 = lax.ppermute(send1, "core", [(0, 1), (1, 0)])
-    return ending(tokens, own0, own1, got0, got1, post_gain.reshape(1, WIDTH))
+    attended = far_attention(flags, queries, sums, near, cross)
+    theirs = out_projection(attended, out_rows, 1, BF)
+    got = lax.ppermute(theirs, "core", [(0, 1), (1, 0)])
+    ours = out_projection(attended, out_rows, 0, F32)
+    return ending(tokens, ours, got, post_gain.reshape(1, WIDTH))
 
 
 def solution(mesh):

time: 282 us -> 270 us (0.957); the launches traced: 281 us -> 266 us
  local copies, waits for them, and re-layouts: 18.8 us -> 8.11 us
  starting transfers between devices: 24.2 us -> 13.8 us
  Pallas kernels: 46.3 us -> 52.4 us
  blocking collectives: 4.44 us -> 0 us
  waiting for transfers between devices: 165 us -> 168 us
    pallas_call x3 -> x5, Pallas kernels: 11.3 us -> 26.9 us  [the longest x1 12 us: key_values(): pl.pallas_call(key_value_kernel, out_shape=jax.ShapeDtypeStruct((rows, 10...]
    ppermute x5 -> x4, starting transfers between devices: 19.6 us -> 9.22 us  [the longest x1 4.54 us: on_device(): lax.ppermute(single, line, [(2 * i + 1, 2 * i) for i in range(chips)] + [...]
    pallas_call x2 -> x1, Pallas kernels: 20.3 us -> 10.4 us  [projection(): pl.pallas_call(kernel, out_shape=jax.ShapeDtypeStruct((rows, 1024), BF),...]
    ppermute x5 -> x4, waiting for transfers between devices: 16.3 us -> 23.4 us  [the longest x1 15.6 us: on_device(): near = lax.ppermute(own, line, [(i, i + 1) for i in range(2 * chips - 1)])]
    unnamed x20, local copies, waits for them, and re-layouts: 8.57 us -> 2.49 us
    all_to_all x1 -> x0, blocking collectives: 4.44 us -> none  [quarter_rows(): swapped = lax.all_to_all(jnp.stack(sides), 'core', 0, 0, tiled=True)]
    slice x4 -> x0, local copies, waits for them, and re-layouts: 3.68 us -> none  [quarter_rows(): p[:, s * p.shape[1] // 2:(s + 1) * p.shape[1] // 2]]
  transfers between devices with their start and end apart: 8 -> 7, of which waited for: 7 -> 5; matrix products, arithmetic and copies ran while one was open for 5% -> 5% of each run, Pallas kernels for 7% -> 9%
where the time goes in v5:
time: 270 us; the launch traced here: 266 us
  waiting for transfers between devices  168 us (62%)
  Pallas kernels  52.4 us (19%)
  starting transfers between devices  13.8 us (5%)
  between operations  13.6 us (5%)
  other arithmetic  10 us (4%)
  local copies, waits for them, and re-layouts  8.11 us (3%)
    all_gather x1, waiting for transfers between devices, on_device(): lax.all_gather(chip_weights(core, query_weight, key_matrix, value_matrix,...  142 us
    ppermute x1, waiting for transfers between devices, on_device(): near = lax.ppermute(own, line, [(i, i + 1) for i in range(2 * chips - 1)])  15.6 us
    pallas_call x1, Pallas kernels, key_values(): pl.pallas_call(key_value_kernel, out_shape=jax.ShapeDtypeStruct((rows, 10...  12 us
    pallas_call x1, Pallas kernels, projection(): pl.pallas_call(kernel, out_shape=jax.ShapeDtypeStruct((rows, 1024), BF),...  10.4 us
    pallas_call x2, Pallas kernels, out_projection(): pl.pallas_call(out_kernel, out_shape=jax.ShapeDtypeStruct((BLOCK, WIDTH),...  9.44 us
    ppermute x1, waiting for transfers between devices, on_device(): lax.ppermute(single, line, [(2 * i + 1, 2 * i) for i in range(chips)] + [...  6.41 us
    pallas_call x1, Pallas kernels, near_attention(): pl.pallas_call(near_kernel, out_shape=jax.ShapeDtypeStruct((4, 2, 2 * BLO...  6.39 us
    slice x1, local copies, waits for them, and re-layouts, on_device(): out_rows = out_rows[:, 1024:]  5.61 us
  transfers between devices with their start and end apart: 7, of which 5 were waited for; matrix products, arithmetic and copies ran while one was open for 5% of the time, Pallas kernels for 9%

profile of v5, /device:TPU:125, one launch (start us, length us, event | category | flops | bytes accessed | tf_op | source)
XLA Modules:
  0.0 266.3 jit_solution(4309080113245925676)
XLA Ops:
  6.5 0.0 copy-start.1
  6.5 0.0 copy-start.6
  6.5 0.0 all-gather.2.cloned.1.call-start
  6.5 2.1 shard_map.92
  8.6 0.7 collective-permute-start.1
  9.3 1.4 collective-permute-done.1
  10.7 1.0 broadcast_select_fusion.1
  11.7 0.9 pad_maximum_fusion
  12.5 0.0 all-gather.2.cloned.1.call-update
  12.6 2.4 fusion
  15.0 0.0 copy-done.1
  15.0 0.0 copy-done.6
  15.0 2.3 fusion.2.mine_ref
  17.3 0.4 collective-permute-start
  17.7 1.0 fusion.3
  18.7 1.0 pad_maximum_fusion.1
  19.7 3.0 %collective-permute-done.other_ref = bf16[256,5376]{1,0:T(8,128)(2,1)} collective-permute-done((bf16[256,5376]{1,0:T(8,128)(2,1)}, bf16[256,5376]{1,0:T(8,128)(2,1)}, u32[]{:S(2)}, u32[]{:S(2)}) %collective-permute-start) | collective-permute-done | bytes 2752544 | tf_op jit(solution)/shard_map/ppermute | solution.py:341
  22.7 3.3 %shard_map.91.x_ref = bf16[512,5376]{1,0:T(8,128)(2,1)S(1)} custom-call(s32[1]{0:T(128)} %bitcast.2.core_ref, bf16[256,5376]{1,0:T(8,128)(2,1)} %fusion.2.mine_ref, bf16[256,5376]{1,0:T(8,128)(2,1)} %collective-permute-done.other_ref), custom_call_target="tpu_custom_call" | custom-call | bytes 12582912 | tf_op jit(solution)/shard_map/pallas_call | solution.py:108
  26.0 0.0 copy-start
  26.0 2.4 copy-done
  28.5 141.9 %all-gather.2.cloned.1.call-done.w_ref.low_ref.high_ref = bf16[10752,1536]{1,0:T(8,128)(2,1)} async-done(((bf16[168,1536]{1,0:T(8,128)(2,1)}), bf16[10752,1536]{1,0:T(8,128)(2,1)}) %all-gather.2.cloned.1.call-update) | async-done | bytes 33030160 | tf_op jit(solution)/shard_map/all_gather | solution.py:331
  170.4 12.0 %shard_map.94.ok.ov = bf16[512,1024]{1,0:T(8,128)(2,1)} custom-call(bf16[512,5376]{1,0:T(8,128)(2,1)} %copy-done, bf16[10752,1536]{1,0:T(8,128)(2,1)} %all-gather.2.cloned.1.call-done.w_ref.low_ref.high_ref, bf16[10752,1536]{1,0:T(8,128)(2,1)} %all-gather.2.cloned.1.call-done.w_ref.low_ref.high_ref, f32[1,128]{1,0:T(1,128)} %bitcast.9, ...), custom_call_target="tpu_custom_call" | custom-call | flops 5637144576 | bytes 16515072 | tf_op jit(solution)/shard_map/pallas_call | solution.py:73
  182.4 4.2 %collective-permute-start.2 = (bf16[512,1024]{1,0:T(8,128)(2,1)}, bf16[512,1024]{1,0:T(8,128)(2,1)}, u32[]{:S(2)}, u32[]{:S(2)}) collective-permute-start(bf16[512,1024]{1,0:T(8,128)(2,1)} %shard_map.94.ok.ov), channel_id=1, source_target_pairs={{0,4},{4,8},{8,12},{12,16},{16,20},{20,24},{24,28},{28,32},{32,36}... | collective-permute-start | bytes 3145736 | tf_op jit(solution)/shard_map/ppermute | solution.py:353
  186.6 2.4 collective-permute-start.3
  189.0 0.1 pad_add_fusion.flag_ref
  189.1 0.0 slice-start
  189.1 1.4 slice_select_fusion
  190.5 0.0 slice-start.1
  190.5 0.0 copy-start.3
  190.5 0.0 copy-start.4
  190.5 0.0 copy-start.5
  190.5 4.5 %collective-permute-start.4 = (bf16[256,1024]{1,0:T(8,128)(2,1)S(1)}, bf16[256,1024]{1,0:T(8,128)(2,1)S(1)}, u32[]{:S(2)}, u32[]{:S(2)}) collective-permute-start(bf16[256,1024]{1,0:T(8,128)(2,1)S(1)} %slice_select_fusion), channel_id=1, source_target_pairs={{1,0},{5,4},{9,8},{13,12},{17,16},{21,20},{25,24},{29,28},{33,32},... | collective-permute-start | bytes 1572872 | tf_op jit(solution)/shard_map/ppermute | solution.py:354
  195.1 5.6 %slice.11.low_ref.high_ref = bf16[10752,512]{1,0:T(8,128)(2,1)S(1)} slice(bf16[10752,1536]{1,0:T(8,128)(2,1)} %all-gather.2.cloned.1.call-done.w_ref.low_ref.high_ref), slice={[0:10752], [1024:1536]} | slice | bytes 22020096 | tf_op jit(solution)/shard_map/slice | solution.py:367
  200.7 0.0 slice-done
  200.7 0.0 slice-done.1
  200.7 0.0 copy-done.3
  200.7 0.0 copy-done.4
  200.7 0.0 copy-done.5
  200.8 0.0 copy-start.2
  200.8 10.4 %shard_map.93.q_ref = bf16[512,1024]{1,0:T(8,128)(2,1)S(1)} custom-call(bf16[512,5376]{1,0:T(8,128)(2,1)S(1)} %bitcast.7, bf16[10752,1536]{1,0:T(8,128)(2,1)} %all-gather.2.cloned.1.call-done.w_ref.low_ref.high_ref, f32[1,128]{1,0:T(1,128)S(1)} %bitcast.8, f32[512,128]{1,0:T(8,128)S(1)} %copy-done.3, f32[512,128]{1,0:T(8,128)S(1)} %copy-done.4), custom_call_target="tpu_custom_call" | custom-call | flops 5637144576 | bytes 16515072 | tf_op jit(solution)/shard_map/pallas_call | solution.py:121
  211.2 0.0 collective-permute-done.2.zk.zv
  211.2 0.0 copy-done.2
  211.2 6.4 %shard_map.95.sum_ref = f32[4,2,512,256]{3,2,1,0:T(8,128)S(1)} custom-call(s32[4]{0:T(128)S(1)} %pad_add_fusion.flag_ref, bf16[512,1024]{1,0:T(8,128)(2,1)S(1)} %shard_map.93.q_ref, bf16[512,1024]{1,0:T(8,128)(2,1)S(1)} %copy-done.2, bf16[512,1024]{1,0:T(8,128)(2,1)S(1)} %copy-done.2, bf16[512,1024]{1,0:T(8,128)(2,1)} %collective-permute-done.2.zk.zv, ...), custom_call_target="tpu_custom_call" | custom-call | flops 1610612736 | bytes 6291456 | tf_op jit(solution)/shard_map/pallas_call | solution.py:206
  217.6 6.4 %collective-permute-done.4.ck.cv = bf16[256,1024]{1,0:T(8,128)(2,1)S(1)} collective-permute-done((bf16[256,1024]{1,0:T(8,128)(2,1)S(1)}, bf16[256,1024]{1,0:T(8,128)(2,1)S(1)}, u32[]{:S(2)}, u32[]{:S(2)}) %collective-permute-start.4) | collective-permute-done | bytes 524320 | tf_op jit(solution)/shard_map/ppermute | solution.py:354
  224.0 15.6 %collective-permute-done.3.nk.nv = bf16[512,1024]{1,0:T(8,128)(2,1)} collective-permute-done((bf16[512,1024]{1,0:T(8,128)(2,1)}, bf16[512,1024]{1,0:T(8,128)(2,1)}, u32[]{:S(2)}, u32[]{:S(2)}) %collective-permute-start.3) | collective-permute-done | bytes 1048608 | tf_op jit(solution)/shard_map/ppermute | solution.py:352
  239.6 5.0 %shard_map.96.att_ref = bf16[512,1024]{1,0:T(8,128)(2,1)S(1)} custom-call(s32[4]{0:T(128)S(1)} %pad_add_fusion.flag_ref, bf16[512,1024]{1,0:T(8,128)(2,1)S(1)} %shard_map.93.q_ref, f32[4,2,512,256]{3,2,1,0:T(8,128)S(1)} %shard_map.95.sum_ref, bf16[512,1024]{1,0:T(8,128)(2,1)} %collective-permute-done.3.nk.nv, ...), custom_call_target="tpu_custom_call" | custom-call | flops 1073741824 | bytes 6291456 | tf_op jit(solution)/shard_map/pallas_call | solution.py:218
  244.7 0.0 copy-start.7
  244.7 4.7 %shard_map.98 = bf16[256,5376]{1,0:T(8,128)(2,1)S(1)} custom-call(bf16[512,1024]{1,0:T(8,128)(2,1)S(1)} %shard_map.96.att_ref, bf16[10752,512]{1,0:T(8,128)(2,1)S(1)} %slice.11.low_ref.high_ref, bf16[10752,512]{1,0:T(8,128)(2,1)S(1)} %slice.11.low_ref.high_ref), custom_call_target="tpu_custom_call" | custom-call | flops 2818572288 | bytes 15728640 | tf_op jit(solution)/shard_map/pallas_call | solution.py:238
  249.4 1.6 collective-permute-start.5
  251.0 0.0 copy-done.7
  251.0 4.8 %shard_map.97.own_ref = f32[256,5376]{1,0:T(8,128)S(1)} custom-call(bf16[512,1024]{1,0:T(8,128)(2,1)S(1)} %shard_map.96.att_ref, bf16[10752,512]{1,0:T(8,128)(2,1)S(1)} %slice.11.low_ref.high_ref, bf16[10752,512]{1,0:T(8,128)(2,1)S(1)} %slice.11.low_ref.high_ref), custom_call_target="tpu_custom_call" | custom-call | flops 2818572288 | bytes 15728640 | tf_op jit(solution)/shard_map/pallas_call | solution.py:238
  255.8 0.0 collective-permute-done.5.got_ref
  255.8 3.6 %shard_map.99 = bf16[256,5376]{1,0:T(8,128)(2,1)} custom-call(bf16[256,5376]{1,0:T(8,128)(2,1)S(1)} %copy-done.1, f32[256,5376]{1,0:T(8,128)S(1)} %shard_map.97.own_ref, bf16[256,5376]{1,0:T(8,128)(2,1)S(1)} %collective-permute-done.5.got_ref, f32[1,5376]{1,0:T(1,128)S(1)} %reshape.47.gain_ref), custom_call_target="tpu_custom_call" | custom-call | flops 13762560 | bytes 14680064 | tf_op jit(solution)/shard_map/pallas_call | solution.py:263
  (5 shorter events, 0.0 us)
Async XLA Ops:
  6.5 8.5 %copy-start.1 = (bf16[256,5376]{1,0:T(8,128)(2,1)S(1)}, bf16[256,5376]{1,0:T(8,128)(2,1)}, u32[]{:S(2)}) copy-start(bf16[256,5376]{1,0:T(8,128)(2,1)} %tok_ref.1) | copy-start | bytes 8257540
  6.5 8.5 %copy-start.6 = (f32[5376]{0:T(1024)S(1)}, f32[5376]{0:T(1024)}, u32[]{:S(2)}) copy-start(f32[5376]{0:T(1024)} %param.10) | copy-start | bytes 64516
  6.5 163.8 %all-gather.2.cloned.1.call-start = ((), (), s32[]{:S(2)}) async-start(), calls=%async_computation | async-start | bytes 33546240 | tf_op jit(solution)/shard_map/all_gather | solution.py:331
  8.6 2.1 collective-permute-start.1
  17.3 5.4 %collective-permute-start = (bf16[256,5376]{1,0:T(8,128)(2,1)}, bf16[256,5376]{1,0:T(8,128)(2,1)}, u32[]{:S(2)}, u32[]{:S(2)}) collective-permute-start(bf16[256,5376]{1,0:T(8,128)(2,1)} %fusion.2.mine_ref), channel_id=1, source_target_pairs={{0,2},{2,0},{1,3},{3,1},{4,6},{6,4},{5,7},{7,5},{8,10},{10,8},{9,1... | collective-permute-start | bytes 8257544 | tf_op jit(solution)/shard_map/ppermute | solution.py:341
  26.0 2.5 copy-start
  182.4 28.8 %collective-permute-start.2 = (bf16[512,1024]{1,0:T(8,128)(2,1)}, bf16[512,1024]{1,0:T(8,128)(2,1)}, u32[]{:S(2)}, u32[]{:S(2)}) collective-permute-start(bf16[512,1024]{1,0:T(8,128)(2,1)} %shard_map.94.ok.ov), channel_id=1, source_target_pairs={{0,4},{4,8},{8,12},{12,16},{16,20},{20,24},{24,28},{28,32},{32,36}... | collective-permute-start | bytes 3145736 | tf_op jit(solution)/shard_map/ppermute | solution.py:353
  186.6 53.0 %collective-permute-start.3 = (bf16[512,1024]{1,0:T(8,128)(2,1)}, bf16[512,1024]{1,0:T(8,128)(2,1)}, u32[]{:S(2)}, u32[]{:S(2)}) collective-permute-start(bf16[512,1024]{1,0:T(8,128)(2,1)} %shard_map.94.ok.ov), channel_id=1, source_target_pairs={{0,1},{1,4},{4,5},{5,8},{8,9},{9,12},{12,13},{13,16},{16,17},{17,2... | collective-permute-start | bytes 3145736 | tf_op jit(solution)/shard_map/ppermute | solution.py:352
  189.1 11.6 %slice-start = ((s8[5505024]{0:T(1024)(128)(4,1)}), s8[4194304]{0:T(1024)(128)(4,1)S(1)}, s32[]{:S(2)}) async-start(s8[5505024]{0:T(1024)(128)(4,1)} %bitcast.6), calls=%async_computation.1 | async-start | bytes 8388608
  190.5 10.2 %slice-start.1 = ((s8[5505024]{0:T(1024)(128)(4,1)}), s8[1310720]{0:T(1024)(128)(4,1)S(1)}, s32[]{:S(2)}) async-start(s8[5505024]{0:T(1024)(128)(4,1)} %bitcast.6), calls=%async_computation.2 | async-start | bytes 2621440
  190.5 10.2 %copy-start.3 = (f32[512,128]{1,0:T(8,128)S(1)}, f32[512,128]{1,0:T(8,128)}, u32[]{:S(2)}) copy-start(f32[512,128]{1,0:T(8,128)} %get-tuple-element.16.cos_ref) | copy-start | bytes 786436
  190.5 10.2 %copy-start.4 = (f32[512,128]{1,0:T(8,128)S(1)}, f32[512,128]{1,0:T(8,128)}, u32[]{:S(2)}) copy-start(f32[512,128]{1,0:T(8,128)} %get-tuple-element.17.sin_ref) | copy-start | bytes 786436
  190.5 10.2 %copy-start.5 = (f32[128]{0:T(128)S(1)}, f32[128]{0:T(128)}, u32[]{:S(2)}) copy-start(f32[128]{0:T(128)} %param.15) | copy-start | bytes 1540
  190.5 33.5 %collective-permute-start.4 = (bf16[256,1024]{1,0:T(8,128)(2,1)S(1)}, bf16[256,1024]{1,0:T(8,128)(2,1)S(1)}, u32[]{:S(2)}, u32[]{:S(2)}) collective-permute-start(bf16[256,1024]{1,0:T(8,128)(2,1)S(1)} %slice_select_fusion), channel_id=1, source_target_pairs={{1,0},{5,4},{9,8},{13,12},{17,16},{21,20},{25,24},{29,28},{33,32},... | collective-permute-start | bytes 1572872 | tf_op jit(solution)/shard_map/ppermute | solution.py:354
  200.8 10.5 %copy-start.2 = (bf16[512,1024]{1,0:T(8,128)(2,1)S(1)}, bf16[512,1024]{1,0:T(8,128)(2,1)}, u32[]{:S(2)}) copy-start(bf16[512,1024]{1,0:T(8,128)(2,1)} %shard_map.94.ok.ov) | copy-start | bytes 3145732
  244.7 6.3 %copy-start.7 = (f32[5376]{0:T(1024)S(1)}, f32[5376]{0:T(1024)}, u32[]{:S(2)}) copy-start(f32[5376]{0:T(1024)} %param.17) | copy-start | bytes 64516
  249.4 6.4 %collective-permute-start.5 = (bf16[256,5376]{1,0:T(8,128)(2,1)S(1)}, bf16[256,5376]{1,0:T(8,128)(2,1)S(1)}, u32[]{:S(2)}, u32[]{:S(2)}) collective-permute-start(bf16[256,5376]{1,0:T(8,128)(2,1)S(1)} %shard_map.98), channel_id=1, source_target_pairs={{0,2},{2,0},{1,3},{3,1},{4,6},{6,4},{5,7},{7,5},{8,10},{10,8},{9,1... | collective-permute-start | bytes 8257544 | tf_op jit(solution)/shard_map/ppermute | solution.py:370
Sparse Core Ops, SparseCore 0:
  12.7 157.6 all-gather.1

commit v6 on v5

--- a/solution.py
+++ b/solution.py
@@ -226,28 +226,35 @@
     )(flags, queries, sums, near, near, cross, cross)
 
 
-def out_kernel(att_ref, low_ref, high_ref, out_ref):
+OUT_TILE = 1792
+
+
+def out_kernel(att_ref, weight_ref, out_ref):
     dims = (((1,), (1,)), ((), ()))
-    got = lax.dot_general(att_ref[:, :512], low_ref[...], dims, preferred_element_type=F32)
-    got += lax.dot_general(att_ref[:, 512:], high_ref[...], dims, preferred_element_type=F32)
+    at = pl.multiple_of(pl.program_id(0) * OUT_TILE, 128)
+    got = lax.dot_general(
+        att_ref[:, :512], weight_ref[pl.ds(at, OUT_TILE), :], dims, preferred_element_type=F32
+    )
+    got += lax.dot_general(
+        att_ref[:, 512:], weight_ref[pl.ds(at + WIDTH, OUT_TILE), :], dims,
+        preferred_element_type=F32,
+    )
     out_ref[...] = got.astype(out_ref.dtype)
 
 
 def out_projection(attended, weights, which, kind):
-    tile, steps = 896, 6
     return pl.pallas_call(
         out_kernel,
         out_shape=jax.ShapeDtypeStruct((BLOCK, WIDTH), kind),
-        grid=(steps,),
+        grid=(WIDTH // OUT_TILE,),
         in_specs=[
             pl.BlockSpec((BLOCK, 1024), lambda i: (which, 0)),
-            pl.BlockSpec((tile, 512), lambda i: (i, 0)),
-            pl.BlockSpec((tile, 512), lambda i: (i + steps, 0)),
+            pl.BlockSpec(memory_space=pltpu.VMEM),
         ],
-        out_specs=pl.BlockSpec((BLOCK, tile), lambda i: (0, i)),
-        compiler_params=params(16),
+        out_specs=pl.BlockSpec((BLOCK, OUT_TILE), lambda i: (0, i)),
+        compiler_params=params(24),
         cost_estimate=cost(2 * BLOCK * 1024 * WIDTH, 15 * MIB),
-    )(attended, weights, weights)
+    )(attended, weights)
 
 
 def end_kernel(tok_ref, own_ref, got_ref, gain_ref, out_ref):
@@ -258,7 +265,7 @@
 
 
 def ending(tokens, own, got, gain):
-    rows = 64
+    rows = 128
     wide = pl.BlockSpec((rows, WIDTH), lambda i: (i, 0))
     return pl.pallas_call(
         end_kernel,

time: 270 us -> 268 us (level)
  transfers between devices with their start and end apart: 7 -> 7, of which waited for: 5 -> 6; matrix products, arithmetic and copies ran while one was open for 5% -> 5% of each run, Pallas kernels for 9% -> 9%
where the time goes in v6:
time: 268 us; the launch traced here: 265 us
  waiting for transfers between devices  169 us (63%)
  Pallas kernels  50.3 us (19%)
  starting transfers between devices  13.8 us (5%)
  between operations  13.6 us (5%)
  other arithmetic  10 us (4%)
  local copies, waits for them, and re-layouts  8.11 us (3%)
    all_gather x1, waiting for transfers between devices, on_device(): lax.all_gather(chip_weights(core, query_weight, key_matrix, value_matrix,...  142 us
    ppermute x1, waiting for transfers between devices, on_device(): near = lax.ppermute(own, line, [(i, i + 1) for i in range(2 * chips - 1)])  15.6 us
    pallas_call x1, Pallas kernels, key_values(): pl.pallas_call(key_value_kernel, out_shape=jax.ShapeDtypeStruct((rows, 10...  12 us
    pallas_call x1, Pallas kernels, projection(): pl.pallas_call(kernel, out_shape=jax.ShapeDtypeStruct((rows, 1024), BF),...  10.4 us
    pallas_call x2, Pallas kernels, out_projection(): pl.pallas_call(out_kernel, out_shape=jax.ShapeDtypeStruct((BLOCK, WIDTH),...  7.44 us
    ppermute x1, waiting for transfers between devices, on_device(): lax.ppermute(single, line, [(2 * i + 1, 2 * i) for i in range(chips)] + [...  6.43 us
    pallas_call x1, Pallas kernels, near_attention(): pl.pallas_call(near_kernel, out_shape=jax.ShapeDtypeStruct((4, 2, 2 * BLO...  6.39 us
    slice x1, local copies, waits for them, and re-layouts, on_device(): out_rows = out_rows[:, 1024:]  5.61 us
  transfers between devices with their start and end apart: 7, of which 6 were waited for; matrix products, arithmetic and copies ran while one was open for 5% of the time, Pallas kernels for 9%

profile of v6, /device:TPU:125, one launch (start us, length us, event | category | flops | bytes accessed | tf_op | source)
XLA Modules:
  0.0 265.1 jit_solution(4873278411719009116)
XLA Ops:
  6.5 0.0 copy-start.1
  6.5 0.0 copy-start.6
  6.5 0.0 all-gather.2.cloned.1.call-start
  6.5 2.1 shard_map.92
  8.6 0.7 collective-permute-start.1
  9.3 1.4 collective-permute-done.1
  10.7 1.0 broadcast_select_fusion.1
  11.7 0.9 pad_maximum_fusion
  12.5 0.0 all-gather.2.cloned.1.call-update
  12.6 2.4 fusion
  15.0 0.0 copy-done.1
  15.0 0.0 copy-done.6
  15.0 2.3 fusion.2.mine_ref
  17.3 0.4 collective-permute-start
  17.7 1.0 fusion.3
  18.7 1.0 pad_maximum_fusion.1
  19.7 3.0 %collective-permute-done.other_ref = bf16[256,5376]{1,0:T(8,128)(2,1)} collective-permute-done((bf16[256,5376]{1,0:T(8,128)(2,1)}, bf16[256,5376]{1,0:T(8,128)(2,1)}, u32[]{:S(2)}, u32[]{:S(2)}) %collective-permute-start) | collective-permute-done | bytes 2752544 | tf_op jit(solution)/shard_map/ppermute | solution.py:348
  22.7 3.3 %shard_map.91.x_ref = bf16[512,5376]{1,0:T(8,128)(2,1)S(1)} custom-call(s32[1]{0:T(128)} %bitcast.2.core_ref, bf16[256,5376]{1,0:T(8,128)(2,1)} %fusion.2.mine_ref, bf16[256,5376]{1,0:T(8,128)(2,1)} %collective-permute-done.other_ref), custom_call_target="tpu_custom_call" | custom-call | bytes 12582912 | tf_op jit(solution)/shard_map/pallas_call | solution.py:108
  26.0 0.0 copy-start
  26.0 2.4 copy-done
  28.5 141.9 %all-gather.2.cloned.1.call-done.w_ref.low_ref.high_ref = bf16[10752,1536]{1,0:T(8,128)(2,1)} async-done(((bf16[168,1536]{1,0:T(8,128)(2,1)}), bf16[10752,1536]{1,0:T(8,128)(2,1)}) %all-gather.2.cloned.1.call-update) | async-done | bytes 33030160 | tf_op jit(solution)/shard_map/all_gather | solution.py:338
  170.4 12.0 %shard_map.94.ok.ov = bf16[512,1024]{1,0:T(8,128)(2,1)} custom-call(bf16[512,5376]{1,0:T(8,128)(2,1)} %copy-done, bf16[10752,1536]{1,0:T(8,128)(2,1)} %all-gather.2.cloned.1.call-done.w_ref.low_ref.high_ref, bf16[10752,1536]{1,0:T(8,128)(2,1)} %all-gather.2.cloned.1.call-done.w_ref.low_ref.high_ref, f32[1,128]{1,0:T(1,128)} %bitcast.9, ...), custom_call_target="tpu_custom_call" | custom-call | flops 5637144576 | bytes 16515072 | tf_op jit(solution)/shard_map/pallas_call | solution.py:73
  182.4 4.2 %collective-permute-start.2 = (bf16[512,1024]{1,0:T(8,128)(2,1)}, bf16[512,1024]{1,0:T(8,128)(2,1)}, u32[]{:S(2)}, u32[]{:S(2)}) collective-permute-start(bf16[512,1024]{1,0:T(8,128)(2,1)} %shard_map.94.ok.ov), channel_id=1, source_target_pairs={{0,4},{4,8},{8,12},{12,16},{16,20},{20,24},{24,28},{28,32},{32,36}... | collective-permute-start | bytes 3145736 | tf_op jit(solution)/shard_map/ppermute | solution.py:360
  186.6 2.4 collective-permute-start.3
  189.0 0.1 pad_add_fusion.flag_ref
  189.1 0.0 slice-start
  189.1 1.4 slice_select_fusion
  190.5 0.0 slice-start.1
  190.5 0.0 copy-start.3
  190.5 0.0 copy-start.4
  190.5 0.0 copy-start.5
  190.5 4.5 %collective-permute-start.4 = (bf16[256,1024]{1,0:T(8,128)(2,1)S(1)}, bf16[256,1024]{1,0:T(8,128)(2,1)S(1)}, u32[]{:S(2)}, u32[]{:S(2)}) collective-permute-start(bf16[256,1024]{1,0:T(8,128)(2,1)S(1)} %slice_select_fusion), channel_id=1, source_target_pairs={{1,0},{5,4},{9,8},{13,12},{17,16},{21,20},{25,24},{29,28},{33,32},... | collective-permute-start | bytes 1572872 | tf_op jit(solution)/shard_map/ppermute | solution.py:361
  195.1 5.6 %slice.11.weight_ref = bf16[10752,512]{1,0:T(8,128)(2,1)S(1)} slice(bf16[10752,1536]{1,0:T(8,128)(2,1)} %all-gather.2.cloned.1.call-done.w_ref.low_ref.high_ref), slice={[0:10752], [1024:1536]} | slice | bytes 22020096 | tf_op jit(solution)/shard_map/slice | solution.py:374
  200.7 0.0 slice-done
  200.7 0.0 slice-done.1
  200.7 0.0 copy-done.3
  200.7 0.0 copy-done.4
  200.7 0.0 copy-done.5
  200.8 0.0 copy-start.2
  200.8 10.4 %shard_map.93.q_ref = bf16[512,1024]{1,0:T(8,128)(2,1)S(1)} custom-call(bf16[512,5376]{1,0:T(8,128)(2,1)S(1)} %bitcast.7, bf16[10752,1536]{1,0:T(8,128)(2,1)} %all-gather.2.cloned.1.call-done.w_ref.low_ref.high_ref, f32[1,128]{1,0:T(1,128)S(1)} %bitcast.8, f32[512,128]{1,0:T(8,128)S(1)} %copy-done.3, f32[512,128]{1,0:T(8,128)S(1)} %copy-done.4), custom_call_target="tpu_custom_call" | custom-call | flops 5637144576 | bytes 16515072 | tf_op jit(solution)/shard_map/pallas_call | solution.py:121
  211.2 0.0 collective-permute-done.2.zk.zv
  211.2 0.0 copy-done.2
  211.2 6.4 %shard_map.95.sum_ref = f32[4,2,512,256]{3,2,1,0:T(8,128)S(1)} custom-call(s32[4]{0:T(128)S(1)} %pad_add_fusion.flag_ref, bf16[512,1024]{1,0:T(8,128)(2,1)S(1)} %shard_map.93.q_ref, bf16[512,1024]{1,0:T(8,128)(2,1)S(1)} %copy-done.2, bf16[512,1024]{1,0:T(8,128)(2,1)S(1)} %copy-done.2, bf16[512,1024]{1,0:T(8,128)(2,1)} %collective-permute-done.2.zk.zv, ...), custom_call_target="tpu_custom_call" | custom-call | flops 1610612736 | bytes 6291456 | tf_op jit(solution)/shard_map/pallas_call | solution.py:206
  217.6 6.4 %collective-permute-done.4.ck.cv = bf16[256,1024]{1,0:T(8,128)(2,1)S(1)} collective-permute-done((bf16[256,1024]{1,0:T(8,128)(2,1)S(1)}, bf16[256,1024]{1,0:T(8,128)(2,1)S(1)}, u32[]{:S(2)}, u32[]{:S(2)}) %collective-permute-start.4) | collective-permute-done | bytes 524320 | tf_op jit(solution)/shard_map/ppermute | solution.py:361
  224.0 15.6 %collective-permute-done.3.nk.nv = bf16[512,1024]{1,0:T(8,128)(2,1)} collective-permute-done((bf16[512,1024]{1,0:T(8,128)(2,1)}, bf16[512,1024]{1,0:T(8,128)(2,1)}, u32[]{:S(2)}, u32[]{:S(2)}) %collective-permute-start.3) | collective-permute-done | bytes 1048608 | tf_op jit(solution)/shard_map/ppermute | solution.py:359
  239.6 5.0 %shard_map.96.att_ref = bf16[512,1024]{1,0:T(8,128)(2,1)S(1)} custom-call(s32[4]{0:T(128)S(1)} %pad_add_fusion.flag_ref, bf16[512,1024]{1,0:T(8,128)(2,1)S(1)} %shard_map.93.q_ref, f32[4,2,512,256]{3,2,1,0:T(8,128)S(1)} %shard_map.95.sum_ref, bf16[512,1024]{1,0:T(8,128)(2,1)} %collective-permute-done.3.nk.nv, ...), custom_call_target="tpu_custom_call" | custom-call | flops 1073741824 | bytes 6291456 | tf_op jit(solution)/shard_map/pallas_call | solution.py:218
  244.7 0.0 copy-start.7
  244.7 3.6 %shard_map.98 = bf16[256,5376]{1,0:T(8,128)(2,1)S(1)} custom-call(bf16[512,1024]{1,0:T(8,128)(2,1)S(1)} %shard_map.96.att_ref, bf16[10752,512]{1,0:T(8,128)(2,1)S(1)} %slice.11.weight_ref), custom_call_target="tpu_custom_call" | custom-call | flops 2818572288 | bytes 15728640 | tf_op jit(solution)/shard_map/pallas_call | solution.py:246
  248.3 1.6 collective-permute-start.5
  249.9 0.0 copy-done.7
  249.9 3.8 %shard_map.97.own_ref = f32[256,5376]{1,0:T(8,128)S(1)} custom-call(bf16[512,1024]{1,0:T(8,128)(2,1)S(1)} %shard_map.96.att_ref, bf16[10752,512]{1,0:T(8,128)(2,1)S(1)} %slice.11.weight_ref), custom_call_target="tpu_custom_call" | custom-call | flops 2818572288 | bytes 15728640 | tf_op jit(solution)/shard_map/pallas_call | solution.py:246
  253.8 0.9 collective-permute-done.5.got_ref
  254.6 3.6 %shard_map.99 = bf16[256,5376]{1,0:T(8,128)(2,1)} custom-call(bf16[256,5376]{1,0:T(8,128)(2,1)S(1)} %copy-done.1, f32[256,5376]{1,0:T(8,128)S(1)} %shard_map.97.own_ref, bf16[256,5376]{1,0:T(8,128)(2,1)S(1)} %collective-permute-done.5.got_ref, f32[1,5376]{1,0:T(1,128)S(1)} %reshape.47.gain_ref), custom_call_target="tpu_custom_call" | custom-call | flops 13762560 | bytes 14680064 | tf_op jit(solution)/shard_map/pallas_call | solution.py:270
  (5 shorter events, 0.0 us)
Async XLA Ops:
  6.5 8.5 %copy-start.1 = (bf16[256,5376]{1,0:T(8,128)(2,1)S(1)}, bf16[256,5376]{1,0:T(8,128)(2,1)}, u32[]{:S(2)}) copy-start(bf16[256,5376]{1,0:T(8,128)(2,1)} %tok_ref.1) | copy-start | bytes 8257540
  6.5 8.5 %copy-start.6 = (f32[5376]{0:T(1024)S(1)}, f32[5376]{0:T(1024)}, u32[]{:S(2)}) copy-start(f32[5376]{0:T(1024)} %param.10) | copy-start | bytes 64516
  6.5 163.8 %all-gather.2.cloned.1.call-start = ((), (), s32[]{:S(2)}) async-start(), calls=%async_computation | async-start | bytes 33546240 | tf_op jit(solution)/shard_map/all_gather | solution.py:338
  8.6 2.1 collective-permute-start.1
  17.3 5.4 %collective-permute-start = (bf16[256,5376]{1,0:T(8,128)(2,1)}, bf16[256,5376]{1,0:T(8,128)(2,1)}, u32[]{:S(2)}, u32[]{:S(2)}) collective-permute-start(bf16[256,5376]{1,0:T(8,128)(2,1)} %fusion.2.mine_ref), channel_id=1, source_target_pairs={{0,2},{2,0},{1,3},{3,1},{4,6},{6,4},{5,7},{7,5},{8,10},{10,8},{9,1... | collective-permute-start | bytes 8257544 | tf_op jit(solution)/shard_map/ppermute | solution.py:348
  26.0 2.5 copy-start
  182.4 28.8 %collective-permute-start.2 = (bf16[512,1024]{1,0:T(8,128)(2,1)}, bf16[512,1024]{1,0:T(8,128)(2,1)}, u32[]{:S(2)}, u32[]{:S(2)}) collective-permute-start(bf16[512,1024]{1,0:T(8,128)(2,1)} %shard_map.94.ok.ov), channel_id=1, source_target_pairs={{0,4},{4,8},{8,12},{12,16},{16,20},{20,24},{24,28},{28,32},{32,36}... | collective-permute-start | bytes 3145736 | tf_op jit(solution)/shard_map/ppermute | solution.py:360
  186.6 53.0 %collective-permute-start.3 = (bf16[512,1024]{1,0:T(8,128)(2,1)}, bf16[512,1024]{1,0:T(8,128)(2,1)}, u32[]{:S(2)}, u32[]{:S(2)}) collective-permute-start(bf16[512,1024]{1,0:T(8,128)(2,1)} %shard_map.94.ok.ov), channel_id=1, source_target_pairs={{0,1},{1,4},{4,5},{5,8},{8,9},{9,12},{12,13},{13,16},{16,17},{17,2... | collective-permute-start | bytes 3145736 | tf_op jit(solution)/shard_map/ppermute | solution.py:359
  189.1 11.6 %slice-start = ((s8[5505024]{0:T(1024)(128)(4,1)}), s8[4194304]{0:T(1024)(128)(4,1)S(1)}, s32[]{:S(2)}) async-start(s8[5505024]{0:T(1024)(128)(4,1)} %bitcast.6), calls=%async_computation.1 | async-start | bytes 8388608
  190.5 10.2 %slice-start.1 = ((s8[5505024]{0:T(1024)(128)(4,1)}), s8[1310720]{0:T(1024)(128)(4,1)S(1)}, s32[]{:S(2)}) async-start(s8[5505024]{0:T(1024)(128)(4,1)} %bitcast.6), calls=%async_computation.2 | async-start | bytes 2621440
  190.5 10.2 %copy-start.3 = (f32[512,128]{1,0:T(8,128)S(1)}, f32[512,128]{1,0:T(8,128)}, u32[]{:S(2)}) copy-start(f32[512,128]{1,0:T(8,128)} %get-tuple-element.16.cos_ref) | copy-start | bytes 786436
  190.5 10.2 %copy-start.4 = (f32[512,128]{1,0:T(8,128)S(1)}, f32[512,128]{1,0:T(8,128)}, u32[]{:S(2)}) copy-start(f32[512,128]{1,0:T(8,128)} %get-tuple-element.17.sin_ref) | copy-start | bytes 786436
  190.5 10.2 %copy-start.5 = (f32[128]{0:T(128)S(1)}, f32[128]{0:T(128)}, u32[]{:S(2)}) copy-start(f32[128]{0:T(128)} %param.15) | copy-start | bytes 1540
  190.5 33.5 %collective-permute-start.4 = (bf16[256,1024]{1,0:T(8,128)(2,1)S(1)}, bf16[256,1024]{1,0:T(8,128)(2,1)S(1)}, u32[]{:S(2)}, u32[]{:S(2)}) collective-permute-start(bf16[256,1024]{1,0:T(8,128)(2,1)S(1)} %slice_select_fusion), channel_id=1, source_target_pairs={{1,0},{5,4},{9,8},{13,12},{17,16},{21,20},{25,24},{29,28},{33,32},... | collective-permute-start | bytes 1572872 | tf_op jit(solution)/shard_map/ppermute | solution.py:361
  200.8 10.4 %copy-start.2 = (bf16[512,1024]{1,0:T(8,128)(2,1)S(1)}, bf16[512,1024]{1,0:T(8,128)(2,1)}, u32[]{:S(2)}) copy-start(bf16[512,1024]{1,0:T(8,128)(2,1)} %shard_map.94.ok.ov) | copy-start | bytes 3145732
  244.7 5.3 %copy-start.7 = (f32[5376]{0:T(1024)S(1)}, f32[5376]{0:T(1024)}, u32[]{:S(2)}) copy-start(f32[5376]{0:T(1024)} %param.17) | copy-start | bytes 64516
  248.3 6.3 %collective-permute-start.5 = (bf16[256,5376]{1,0:T(8,128)(2,1)S(1)}, bf16[256,5376]{1,0:T(8,128)(2,1)S(1)}, u32[]{:S(2)}, u32[]{:S(2)}) collective-permute-start(bf16[256,5376]{1,0:T(8,128)(2,1)S(1)} %shard_map.98), channel_id=1, source_target_pairs={{0,2},{2,0},{1,3},{3,1},{4,6},{6,4},{5,7},{7,5},{8,10},{10,8},{9,1... | collective-permute-start | bytes 8257544 | tf_op jit(solution)/shard_map/ppermute | solution.py:377
Sparse Core Ops, SparseCore 0:
  12.7 157.6 all-gather.1

commit v7 on v6

--- a/solution.py
+++ b/solution.py
@@ -179,16 +179,23 @@
     early, late, always = counts(flag_ref[0]), counts(flag_ref[1]), counts(jnp.int32(1))
     before = pl.ds(pl.multiple_of((1 - side) * BLOCK, BLOCK), BLOCK)
     beside = pl.ds(pl.multiple_of(side * BLOCK, BLOCK), BLOCK)
-    gap = tuple(jnp.where(side == 0, n[beside], c[...]) for n, c in ((nk, ck), (nv, cv)))
-    link = tuple(jnp.where(side == 0, c[...], n[beside]) for n, c in ((nk, ck), (nv, cv)))
-    gap, link = gap + (early, ""), link + (always, "")
-    prior = (nk[before], nv[before], late, "")
-    for part, keys in enumerate(((gap, prior), (prior, link))):
-        total = attend(both_heads(q_ref, part), keys, sum_ref[0, part])
-        mixed = (total[:, :HEAD] / total[:, HEAD : HEAD + 1]).astype(BF)
-        to = pl.multiple_of(lax.rem(part + core, 2) * BLOCK, BLOCK)
-        out_ref[pl.ds(to, BLOCK), :HEAD] = mixed[:BLOCK]
-        out_ref[pl.ds(to, BLOCK), HEAD:] = mixed[BLOCK:]
+    for head in range(2):
+        lanes = slice(head * HEAD, (head + 1) * HEAD)
+        wide = slice(head * 2 * HEAD, (head + 1) * 2 * HEAD)
+        gap = tuple(
+            jnp.where(side == 0, n[beside, lanes], c[:, lanes]) for n, c in ((nk, ck), (nv, cv))
+        )
+        link = tuple(
+            jnp.where(side == 0, c[:, lanes], n[beside, lanes]) for n, c in ((nk, ck), (nv, cv))
+        )
+        gap, link = gap + (early, ""), link + (always, "")
+        prior = (nk[before, lanes], nv[before, lanes], late, "")
+        for part, keys in enumerate(((gap, prior), (prior, link))):
+            query = both_heads(q_ref.at[:, wide], part)
+            total = attend(query, keys, sum_ref[head, part])
+            mixed = (total[:, :HEAD] / total[:, HEAD : HEAD + 1]).astype(BF)
+            to = pl.ds(pl.multiple_of(lax.rem(part + core, 2) * BLOCK, BLOCK), BLOCK)
+            out_ref[to, wide] = jnp.concatenate([mixed[:BLOCK], mixed[BLOCK:]], axis=1)
 
 
 def head_pair(rows):
@@ -198,6 +205,7 @@
     ]
 
 
+QUERY_QUAD = pl.BlockSpec((2 * BLOCK, 4 * HEAD), lambda j: (0, j))
 QUERY_PAIR = pl.BlockSpec((2 * BLOCK, 2 * HEAD), lambda j: (0, j))
 SUMS = pl.BlockSpec((1, 2, 2 * BLOCK, 2 * HEAD), lambda j: (j, 0, 0, 0))
 
@@ -218,9 +226,18 @@
     return pl.pallas_call(
         far_kernel,
         out_shape=jax.ShapeDtypeStruct((2 * BLOCK, 1024), BF),
-        grid=(4,),
-        in_specs=[SCALARS, QUERY_PAIR, SUMS] + head_pair(512) + head_pair(256),
-        out_specs=QUERY_PAIR,
+        grid=(2,),
+        in_specs=[
+            SCALARS,
+            QUERY_QUAD,
+            pl.BlockSpec((2, 2, 2 * BLOCK, 2 * HEAD), lambda j: (j, 0, 0, 0)),
+        ]
+        + [
+            pl.BlockSpec((rows, 2 * HEAD), lambda j, shift=shift: (0, j + shift))
+            for rows in (512, 256)
+            for shift in (0, 2)
+        ],
+        out_specs=QUERY_QUAD,
         compiler_params=params(16),
         cost_estimate=cost(8 * 512 * 512 * 512, 6 * MIB, 8 * 512 * 512),
     )(flags, queries, sums, near, near, cross, cross)

time: 268 us -> 268 us (level)
  no operation moved by 1% of the time
where the time goes in v7:
time: 268 us; the launch traced here: 264 us
  waiting for transfers between devices  169 us (63%)
  Pallas kernels  49.4 us (18%)
  starting transfers between devices  14 us (5%)
  between operations  13.6 us (5%)
  other arithmetic  10 us (4%)
  local copies, waits for them, and re-layouts  8.11 us (3%)
    all_gather x1, waiting for transfers between devices, on_device(): lax.all_gather(chip_weights(core, query_weight, key_matrix, value_matrix,...  142 us
    ppermute x1, waiting for transfers between devices, on_device(): near = lax.ppermute(own, line, [(i, i + 1) for i in range(2 * chips - 1)])  15.6 us
    pallas_call x1, Pallas kernels, key_values(): pl.pallas_call(key_value_kernel, out_shape=jax.ShapeDtypeStruct((rows, 10...  12 us
    pallas_call x1, Pallas kernels, projection(): pl.pallas_call(kernel, out_shape=jax.ShapeDtypeStruct((rows, 1024), BF),...  10.4 us
    pallas_call x2, Pallas kernels, out_projection(): pl.pallas_call(out_kernel, out_shape=jax.ShapeDtypeStruct((BLOCK, WIDTH),...  7.44 us
    ppermute x1, waiting for transfers between devices, on_device(): lax.ppermute(single, line, [(2 * i + 1, 2 * i) for i in range(chips)] + [...  6.44 us
    pallas_call x1, Pallas kernels, near_attention(): pl.pallas_call(near_kernel, out_shape=jax.ShapeDtypeStruct((4, 2, 2 * BLO...  6.39 us
    slice x1, local copies, waits for them, and re-layouts, on_device(): out_rows = out_rows[:, 1024:]  5.61 us
  transfers between devices with their start and end apart: 7, of which 6 were waited for; matrix products, arithmetic and copies ran while one was open for 5% of the time, Pallas kernels for 9%

profile of v7, /device:TPU:125, one launch (start us, length us, event | category | flops | bytes accessed | tf_op | source)
XLA Modules:
  0.0 264.4 jit_solution(13221436744778246683)
XLA Ops:
  6.5 0.0 copy-start.1
  6.5 0.0 copy-start.6
  6.5 0.0 all-gather.2.cloned.1.call-start
  6.5 2.1 shard_map.92
  8.6 0.7 collective-permute-start.1
  9.3 1.4 collective-permute-done.1
  10.7 1.0 broadcast_select_fusion.1
  11.7 0.9 pad_maximum_fusion
  12.5 0.0 all-gather.2.cloned.1.call-update
  12.6 2.4 fusion
  15.0 0.0 copy-done.1
  15.0 0.0 copy-done.6
  15.0 2.3 fusion.2.mine_ref
  17.3 0.4 collective-permute-start
  17.7 1.0 fusion.3
  18.7 1.0 pad_maximum_fusion.1
  19.7 3.0 %collective-permute-done.other_ref = bf16[256,5376]{1,0:T(8,128)(2,1)} collective-permute-done((bf16[256,5376]{1,0:T(8,128)(2,1)}, bf16[256,5376]{1,0:T(8,128)(2,1)}, u32[]{:S(2)}, u32[]{:S(2)}) %collective-permute-start) | collective-permute-done | bytes 2752544 | tf_op jit(solution)/shard_map/ppermute | solution.py:365
  22.7 3.3 %shard_map.91.x_ref = bf16[512,5376]{1,0:T(8,128)(2,1)S(1)} custom-call(s32[1]{0:T(128)} %bitcast.2.core_ref, bf16[256,5376]{1,0:T(8,128)(2,1)} %fusion.2.mine_ref, bf16[256,5376]{1,0:T(8,128)(2,1)} %collective-permute-done.other_ref), custom_call_target="tpu_custom_call" | custom-call | bytes 12582912 | tf_op jit(solution)/shard_map/pallas_call | solution.py:108
  26.0 0.0 copy-start
  26.0 2.4 copy-done
  28.5 141.9 %all-gather.2.cloned.1.call-done.w_ref.low_ref.high_ref = bf16[10752,1536]{1,0:T(8,128)(2,1)} async-done(((bf16[168,1536]{1,0:T(8,128)(2,1)}), bf16[10752,1536]{1,0:T(8,128)(2,1)}) %all-gather.2.cloned.1.call-update) | async-done | bytes 33030160 | tf_op jit(solution)/shard_map/all_gather | solution.py:355
  170.4 12.0 %shard_map.94.ok.ov = bf16[512,1024]{1,0:T(8,128)(2,1)} custom-call(bf16[512,5376]{1,0:T(8,128)(2,1)} %copy-done, bf16[10752,1536]{1,0:T(8,128)(2,1)} %all-gather.2.cloned.1.call-done.w_ref.low_ref.high_ref, bf16[10752,1536]{1,0:T(8,128)(2,1)} %all-gather.2.cloned.1.call-done.w_ref.low_ref.high_ref, f32[1,128]{1,0:T(1,128)} %bitcast.9, ...), custom_call_target="tpu_custom_call" | custom-call | flops 5637144576 | bytes 16515072 | tf_op jit(solution)/shard_map/pallas_call | solution.py:73
  182.4 4.2 %collective-permute-start.2 = (bf16[512,1024]{1,0:T(8,128)(2,1)}, bf16[512,1024]{1,0:T(8,128)(2,1)}, u32[]{:S(2)}, u32[]{:S(2)}) collective-permute-start(bf16[512,1024]{1,0:T(8,128)(2,1)} %shard_map.94.ok.ov), channel_id=1, source_target_pairs={{0,4},{4,8},{8,12},{12,16},{16,20},{20,24},{24,28},{28,32},{32,36}... | collective-permute-start | bytes 3145736 | tf_op jit(solution)/shard_map/ppermute | solution.py:377
  186.6 2.4 collective-permute-start.3
  189.0 0.1 pad_add_fusion.flag_ref
  189.1 0.0 slice-start
  189.1 1.4 slice_select_fusion
  190.5 0.0 slice-start.1
  190.5 0.0 copy-start.3
  190.5 0.0 copy-start.4
  190.5 0.0 copy-start.5
  190.5 4.5 %collective-permute-start.4 = (bf16[256,1024]{1,0:T(8,128)(2,1)S(1)}, bf16[256,1024]{1,0:T(8,128)(2,1)S(1)}, u32[]{:S(2)}, u32[]{:S(2)}) collective-permute-start(bf16[256,1024]{1,0:T(8,128)(2,1)S(1)} %slice_select_fusion), channel_id=1, source_target_pairs={{1,0},{5,4},{9,8},{13,12},{17,16},{21,20},{25,24},{29,28},{33,32},... | collective-permute-start | bytes 1572872 | tf_op jit(solution)/shard_map/ppermute | solution.py:378
  195.1 5.6 %slice.11.weight_ref = bf16[10752,512]{1,0:T(8,128)(2,1)S(1)} slice(bf16[10752,1536]{1,0:T(8,128)(2,1)} %all-gather.2.cloned.1.call-done.w_ref.low_ref.high_ref), slice={[0:10752], [1024:1536]} | slice | bytes 22020096 | tf_op jit(solution)/shard_map/slice | solution.py:391
  200.7 0.0 slice-done
  200.7 0.0 slice-done.1
  200.7 0.0 copy-done.3
  200.7 0.0 copy-done.4
  200.7 0.0 copy-done.5
  200.8 0.0 copy-start.2
  200.8 10.4 %shard_map.93.q_ref = bf16[512,1024]{1,0:T(8,128)(2,1)S(1)} custom-call(bf16[512,5376]{1,0:T(8,128)(2,1)S(1)} %bitcast.7, bf16[10752,1536]{1,0:T(8,128)(2,1)} %all-gather.2.cloned.1.call-done.w_ref.low_ref.high_ref, f32[1,128]{1,0:T(1,128)S(1)} %bitcast.8, f32[512,128]{1,0:T(8,128)S(1)} %copy-done.3, f32[512,128]{1,0:T(8,128)S(1)} %copy-done.4), custom_call_target="tpu_custom_call" | custom-call | flops 5637144576 | bytes 16515072 | tf_op jit(solution)/shard_map/pallas_call | solution.py:121
  211.2 0.0 collective-permute-done.2.zk.zv
  211.2 0.0 copy-done.2
  211.2 6.4 %shard_map.95.sum_ref = f32[4,2,512,256]{3,2,1,0:T(8,128)S(1)} custom-call(s32[4]{0:T(128)S(1)} %pad_add_fusion.flag_ref, bf16[512,1024]{1,0:T(8,128)(2,1)S(1)} %shard_map.93.q_ref, bf16[512,1024]{1,0:T(8,128)(2,1)S(1)} %copy-done.2, bf16[512,1024]{1,0:T(8,128)(2,1)S(1)} %copy-done.2, bf16[512,1024]{1,0:T(8,128)(2,1)} %collective-permute-done.2.zk.zv, ...), custom_call_target="tpu_custom_call" | custom-call | flops 1610612736 | bytes 6291456 | tf_op jit(solution)/shard_map/pallas_call | solution.py:214
  217.6 6.4 %collective-permute-done.4.ck.cv = bf16[256,1024]{1,0:T(8,128)(2,1)S(1)} collective-permute-done((bf16[256,1024]{1,0:T(8,128)(2,1)S(1)}, bf16[256,1024]{1,0:T(8,128)(2,1)S(1)}, u32[]{:S(2)}, u32[]{:S(2)}) %collective-permute-start.4) | collective-permute-done | bytes 524320 | tf_op jit(solution)/shard_map/ppermute | solution.py:378
  224.0 15.6 %collective-permute-done.3.nk.nv = bf16[512,1024]{1,0:T(8,128)(2,1)} collective-permute-done((bf16[512,1024]{1,0:T(8,128)(2,1)}, bf16[512,1024]{1,0:T(8,128)(2,1)}, u32[]{:S(2)}, u32[]{:S(2)}) %collective-permute-start.3) | collective-permute-done | bytes 1048608 | tf_op jit(solution)/shard_map/ppermute | solution.py:376
  239.6 4.1 %shard_map.96.att_ref = bf16[512,1024]{1,0:T(8,128)(2,1)S(1)} custom-call(s32[4]{0:T(128)S(1)} %pad_add_fusion.flag_ref, bf16[512,1024]{1,0:T(8,128)(2,1)S(1)} %shard_map.93.q_ref, f32[4,2,512,256]{3,2,1,0:T(8,128)S(1)} %shard_map.95.sum_ref, bf16[512,1024]{1,0:T(8,128)(2,1)} %collective-permute-done.3.nk.nv, ...), custom_call_target="tpu_custom_call" | custom-call | flops 1073741824 | bytes 6291456 | tf_op jit(solution)/shard_map/pallas_call | solution.py:226
  243.8 0.0 copy-start.7
  243.8 3.6 %shard_map.98 = bf16[256,5376]{1,0:T(8,128)(2,1)S(1)} custom-call(bf16[512,1024]{1,0:T(8,128)(2,1)S(1)} %shard_map.96.att_ref, bf16[10752,512]{1,0:T(8,128)(2,1)S(1)} %slice.11.weight_ref), custom_call_target="tpu_custom_call" | custom-call | flops 2818572288 | bytes 15728640 | tf_op jit(solution)/shard_map/pallas_call | solution.py:263
  247.4 1.8 collective-permute-start.5
  249.2 0.0 copy-done.7
  249.2 3.8 %shard_map.97.own_ref = f32[256,5376]{1,0:T(8,128)S(1)} custom-call(bf16[512,1024]{1,0:T(8,128)(2,1)S(1)} %shard_map.96.att_ref, bf16[10752,512]{1,0:T(8,128)(2,1)S(1)} %slice.11.weight_ref), custom_call_target="tpu_custom_call" | custom-call | flops 2818572288 | bytes 15728640 | tf_op jit(solution)/shard_map/pallas_call | solution.py:263
  253.0 0.9 collective-permute-done.5.got_ref
  253.9 3.6 %shard_map.99 = bf16[256,5376]{1,0:T(8,128)(2,1)} custom-call(bf16[256,5376]{1,0:T(8,128)(2,1)S(1)} %copy-done.1, f32[256,5376]{1,0:T(8,128)S(1)} %shard_map.97.own_ref, bf16[256,5376]{1,0:T(8,128)(2,1)S(1)} %collective-permute-done.5.got_ref, f32[1,5376]{1,0:T(1,128)S(1)} %reshape.47.gain_ref), custom_call_target="tpu_custom_call" | custom-call | flops 13762560 | bytes 14680064 | tf_op jit(solution)/shard_map/pallas_call | solution.py:287
  (5 shorter events, 0.0 us)
Async XLA Ops:
  6.5 8.5 %copy-start.1 = (bf16[256,5376]{1,0:T(8,128)(2,1)S(1)}, bf16[256,5376]{1,0:T(8,128)(2,1)}, u32[]{:S(2)}) copy-start(bf16[256,5376]{1,0:T(8,128)(2,1)} %tok_ref.1) | copy-start | bytes 8257540
  6.5 8.5 %copy-start.6 = (f32[5376]{0:T(1024)S(1)}, f32[5376]{0:T(1024)}, u32[]{:S(2)}) copy-start(f32[5376]{0:T(1024)} %param.10) | copy-start | bytes 64516
  6.5 163.8 %all-gather.2.cloned.1.call-start = ((), (), s32[]{:S(2)}) async-start(), calls=%async_computation | async-start | bytes 33546240 | tf_op jit(solution)/shard_map/all_gather | solution.py:355
  8.6 2.1 collective-permute-start.1
  17.3 5.4 %collective-permute-start = (bf16[256,5376]{1,0:T(8,128)(2,1)}, bf16[256,5376]{1,0:T(8,128)(2,1)}, u32[]{:S(2)}, u32[]{:S(2)}) collective-permute-start(bf16[256,5376]{1,0:T(8,128)(2,1)} %fusion.2.mine_ref), channel_id=1, source_target_pairs={{0,2},{2,0},{1,3},{3,1},{4,6},{6,4},{5,7},{7,5},{8,10},{10,8},{9,1... | collective-permute-start | bytes 8257544 | tf_op jit(solution)/shard_map/ppermute | solution.py:365
  26.0 2.5 copy-start
  182.4 28.8 %collective-permute-start.2 = (bf16[512,1024]{1,0:T(8,128)(2,1)}, bf16[512,1024]{1,0:T(8,128)(2,1)}, u32[]{:S(2)}, u32[]{:S(2)}) collective-permute-start(bf16[512,1024]{1,0:T(8,128)(2,1)} %shard_map.94.ok.ov), channel_id=1, source_target_pairs={{0,4},{4,8},{8,12},{12,16},{16,20},{20,24},{24,28},{28,32},{32,36}... | collective-permute-start | bytes 3145736 | tf_op jit(solution)/shard_map/ppermute | solution.py:377
  186.6 53.0 %collective-permute-start.3 = (bf16[512,1024]{1,0:T(8,128)(2,1)}, bf16[512,1024]{1,0:T(8,128)(2,1)}, u32[]{:S(2)}, u32[]{:S(2)}) collective-permute-start(bf16[512,1024]{1,0:T(8,128)(2,1)} %shard_map.94.ok.ov), channel_id=1, source_target_pairs={{0,1},{1,4},{4,5},{5,8},{8,9},{9,12},{12,13},{13,16},{16,17},{17,2... | collective-permute-start | bytes 3145736 | tf_op jit(solution)/shard_map/ppermute | solution.py:376
  189.1 11.6 %slice-start = ((s8[5505024]{0:T(1024)(128)(4,1)}), s8[4194304]{0:T(1024)(128)(4,1)S(1)}, s32[]{:S(2)}) async-start(s8[5505024]{0:T(1024)(128)(4,1)} %bitcast.6), calls=%async_computation.1 | async-start | bytes 8388608
  190.5 10.2 %slice-start.1 = ((s8[5505024]{0:T(1024)(128)(4,1)}), s8[1310720]{0:T(1024)(128)(4,1)S(1)}, s32[]{:S(2)}) async-start(s8[5505024]{0:T(1024)(128)(4,1)} %bitcast.6), calls=%async_computation.2 | async-start | bytes 2621440
  190.5 10.2 %copy-start.3 = (f32[512,128]{1,0:T(8,128)S(1)}, f32[512,128]{1,0:T(8,128)}, u32[]{:S(2)}) copy-start(f32[512,128]{1,0:T(8,128)} %get-tuple-element.16.cos_ref) | copy-start | bytes 786436
  190.5 10.2 %copy-start.4 = (f32[512,128]{1,0:T(8,128)S(1)}, f32[512,128]{1,0:T(8,128)}, u32[]{:S(2)}) copy-start(f32[512,128]{1,0:T(8,128)} %get-tuple-element.17.sin_ref) | copy-start | bytes 786436
  190.5 10.2 %copy-start.5 = (f32[128]{0:T(128)S(1)}, f32[128]{0:T(128)}, u32[]{:S(2)}) copy-start(f32[128]{0:T(128)} %param.15) | copy-start | bytes 1540
  190.5 33.5 %collective-permute-start.4 = (bf16[256,1024]{1,0:T(8,128)(2,1)S(1)}, bf16[256,1024]{1,0:T(8,128)(2,1)S(1)}, u32[]{:S(2)}, u32[]{:S(2)}) collective-permute-start(bf16[256,1024]{1,0:T(8,128)(2,1)S(1)} %slice_select_fusion), channel_id=1, source_target_pairs={{1,0},{5,4},{9,8},{13,12},{17,16},{21,20},{25,24},{29,28},{33,32},... | collective-permute-start | bytes 1572872 | tf_op jit(solution)/shard_map/ppermute | solution.py:378
  200.8 10.4 %copy-start.2 = (bf16[512,1024]{1,0:T(8,128)(2,1)S(1)}, bf16[512,1024]{1,0:T(8,128)(2,1)}, u32[]{:S(2)}) copy-start(bf16[512,1024]{1,0:T(8,128)(2,1)} %shard_map.94.ok.ov) | copy-start | bytes 3145732
  243.8 5.5 %copy-start.7 = (f32[5376]{0:T(1024)S(1)}, f32[5376]{0:T(1024)}, u32[]{:S(2)}) copy-start(f32[5376]{0:T(1024)} %param.17) | copy-start | bytes 64516
  247.4 6.5 %collective-permute-start.5 = (bf16[256,5376]{1,0:T(8,128)(2,1)S(1)}, bf16[256,5376]{1,0:T(8,128)(2,1)S(1)}, u32[]{:S(2)}, u32[]{:S(2)}) collective-permute-start(bf16[256,5376]{1,0:T(8,128)(2,1)S(1)} %shard_map.98), channel_id=1, source_target_pairs={{0,2},{2,0},{1,3},{3,1},{4,6},{6,4},{5,7},{7,5},{8,10},{10,8},{9,1... | collective-permute-start | bytes 8257544 | tf_op jit(solution)/shard_map/ppermute | solution.py:394
Sparse Core Ops, SparseCore 0:
  12.7 157.6 all-gather.1

commit v8 on v7

--- a/solution.py
+++ b/solution.py
@@ -243,7 +243,7 @@
     )(flags, queries, sums, near, near, cross, cross)
 
 
-OUT_TILE = 1792
+OUT_TILE = 2688
 
 
 def out_kernel(att_ref, weight_ref, out_ref):

time: 268 us -> 268 us (level)
  no operation moved by 1% of the time
where the time goes in v8:
time: 268 us; the launch traced here: 264 us
  waiting for transfers between devices  169 us (63%)
  Pallas kernels  49.3 us (18%)
  starting transfers between devices  14 us (5%)
  between operations  13.6 us (5%)
  other arithmetic  10 us (4%)
  local copies, waits for them, and re-layouts  8.11 us (3%)
    all_gather x1, waiting for transfers between devices, on_device(): lax.all_gather(chip_weights(core, query_weight, key_matrix, value_matrix,...  142 us
    ppermute x1, waiting for transfers between devices, on_device(): near = lax.ppermute(own, line, [(i, i + 1) for i in range(2 * chips - 1)])  15.6 us
    pallas_call x1, Pallas kernels, key_values(): pl.pallas_call(key_value_kernel, out_shape=jax.ShapeDtypeStruct((rows, 10...  12 us
    pallas_call x1, Pallas kernels, projection(): pl.pallas_call(kernel, out_shape=jax.ShapeDtypeStruct((rows, 1024), BF),...  10.4 us
    pallas_call x2, Pallas kernels, out_projection(): pl.pallas_call(out_kernel, out_shape=jax.ShapeDtypeStruct((BLOCK, WIDTH),...  7.34 us
    pallas_call x1, Pallas kernels, near_attention(): pl.pallas_call(near_kernel, out_shape=jax.ShapeDtypeStruct((4, 2, 2 * BLO...  6.39 us
    ppermute x1, waiting for transfers between devices, on_device(): lax.ppermute(single, line, [(2 * i + 1, 2 * i) for i in range(chips)] + [...  6.26 us
    slice x1, local copies, waits for them, and re-layouts, on_device(): out_rows = out_rows[:, 1024:]  5.61 us
  transfers between devices with their start and end apart: 7, of which 6 were waited for; matrix products, arithmetic and copies ran while one was open for 5% of the time, Pallas kernels for 9%

profile of v8, /device:TPU:125, one launch (start us, length us, event | category | flops | bytes accessed | tf_op | source)
XLA Modules:
  0.0 264.2 jit_solution(14562246052297116021)
XLA Ops:
  6.5 0.0 copy-start.1
  6.5 0.0 copy-start.6
  6.5 0.0 all-gather.2.cloned.1.call-start
  6.5 2.1 shard_map.92
  8.6 0.7 collective-permute-start.1
  9.3 1.4 collective-permute-done.1
  10.7 1.0 broadcast_select_fusion.1
  11.7 0.9 pad_maximum_fusion
  12.5 0.0 all-gather.2.cloned.1.call-update
  12.6 2.4 fusion
  15.0 0.0 copy-done.1
  15.0 0.0 copy-done.6
  15.0 2.3 fusion.2.mine_ref
  17.3 0.4 collective-permute-start
  17.7 1.0 fusion.3
  18.7 1.0 pad_maximum_fusion.1
  19.7 3.0 %collective-permute-done.other_ref = bf16[256,5376]{1,0:T(8,128)(2,1)} collective-permute-done((bf16[256,5376]{1,0:T(8,128)(2,1)}, bf16[256,5376]{1,0:T(8,128)(2,1)}, u32[]{:S(2)}, u32[]{:S(2)}) %collective-permute-start) | collective-permute-done | bytes 2752544 | tf_op jit(solution)/shard_map/ppermute | solution.py:365
  22.7 3.3 %shard_map.91.x_ref = bf16[512,5376]{1,0:T(8,128)(2,1)S(1)} custom-call(s32[1]{0:T(128)} %bitcast.2.core_ref, bf16[256,5376]{1,0:T(8,128)(2,1)} %fusion.2.mine_ref, bf16[256,5376]{1,0:T(8,128)(2,1)} %collective-permute-done.other_ref), custom_call_target="tpu_custom_call" | custom-call | bytes 12582912 | tf_op jit(solution)/shard_map/pallas_call | solution.py:108
  26.0 0.0 copy-start
  26.0 2.4 copy-done
  28.5 141.9 %all-gather.2.cloned.1.call-done.w_ref.low_ref.high_ref = bf16[10752,1536]{1,0:T(8,128)(2,1)} async-done(((bf16[168,1536]{1,0:T(8,128)(2,1)}), bf16[10752,1536]{1,0:T(8,128)(2,1)}) %all-gather.2.cloned.1.call-update) | async-done | bytes 33030160 | tf_op jit(solution)/shard_map/all_gather | solution.py:355
  170.4 12.0 %shard_map.94.ok.ov = bf16[512,1024]{1,0:T(8,128)(2,1)} custom-call(bf16[512,5376]{1,0:T(8,128)(2,1)} %copy-done, bf16[10752,1536]{1,0:T(8,128)(2,1)} %all-gather.2.cloned.1.call-done.w_ref.low_ref.high_ref, bf16[10752,1536]{1,0:T(8,128)(2,1)} %all-gather.2.cloned.1.call-done.w_ref.low_ref.high_ref, f32[1,128]{1,0:T(1,128)} %bitcast.9, ...), custom_call_target="tpu_custom_call" | custom-call | flops 5637144576 | bytes 16515072 | tf_op jit(solution)/shard_map/pallas_call | solution.py:73
  182.4 4.2 %collective-permute-start.2 = (bf16[512,1024]{1,0:T(8,128)(2,1)}, bf16[512,1024]{1,0:T(8,128)(2,1)}, u32[]{:S(2)}, u32[]{:S(2)}) collective-permute-start(bf16[512,1024]{1,0:T(8,128)(2,1)} %shard_map.94.ok.ov), channel_id=1, source_target_pairs={{0,4},{4,8},{8,12},{12,16},{16,20},{20,24},{24,28},{28,32},{32,36}... | collective-permute-start | bytes 3145736 | tf_op jit(solution)/shard_map/ppermute | solution.py:377
  186.6 2.4 collective-permute-start.3
  189.0 0.1 pad_add_fusion.flag_ref
  189.1 0.0 slice-start
  189.1 1.4 slice_select_fusion
  190.5 0.0 slice-start.1
  190.5 0.0 copy-start.3
  190.5 0.0 copy-start.4
  190.5 0.0 copy-start.5
  190.5 4.7 %collective-permute-start.4 = (bf16[256,1024]{1,0:T(8,128)(2,1)S(1)}, bf16[256,1024]{1,0:T(8,128)(2,1)S(1)}, u32[]{:S(2)}, u32[]{:S(2)}) collective-permute-start(bf16[256,1024]{1,0:T(8,128)(2,1)S(1)} %slice_select_fusion), channel_id=1, source_target_pairs={{1,0},{5,4},{9,8},{13,12},{17,16},{21,20},{25,24},{29,28},{33,32},... | collective-permute-start | bytes 1572872 | tf_op jit(solution)/shard_map/ppermute | solution.py:378
  195.3 5.6 %slice.11.weight_ref = bf16[10752,512]{1,0:T(8,128)(2,1)S(1)} slice(bf16[10752,1536]{1,0:T(8,128)(2,1)} %all-gather.2.cloned.1.call-done.w_ref.low_ref.high_ref), slice={[0:10752], [1024:1536]} | slice | bytes 22020096 | tf_op jit(solution)/shard_map/slice | solution.py:391
  200.9 0.0 slice-done
  200.9 0.0 slice-done.1
  200.9 0.0 copy-done.3
  200.9 0.0 copy-done.4
  200.9 0.0 copy-done.5
  200.9 0.0 copy-start.2
  201.0 10.4 %shard_map.93.q_ref = bf16[512,1024]{1,0:T(8,128)(2,1)S(1)} custom-call(bf16[512,5376]{1,0:T(8,128)(2,1)S(1)} %bitcast.7, bf16[10752,1536]{1,0:T(8,128)(2,1)} %all-gather.2.cloned.1.call-done.w_ref.low_ref.high_ref, f32[1,128]{1,0:T(1,128)S(1)} %bitcast.8, f32[512,128]{1,0:T(8,128)S(1)} %copy-done.3, f32[512,128]{1,0:T(8,128)S(1)} %copy-done.4), custom_call_target="tpu_custom_call" | custom-call | flops 5637144576 | bytes 16515072 | tf_op jit(solution)/shard_map/pallas_call | solution.py:121
  211.4 0.0 collective-permute-done.2.zk.zv
  211.4 0.0 copy-done.2
  211.4 6.4 %shard_map.95.sum_ref = f32[4,2,512,256]{3,2,1,0:T(8,128)S(1)} custom-call(s32[4]{0:T(128)S(1)} %pad_add_fusion.flag_ref, bf16[512,1024]{1,0:T(8,128)(2,1)S(1)} %shard_map.93.q_ref, bf16[512,1024]{1,0:T(8,128)(2,1)S(1)} %copy-done.2, bf16[512,1024]{1,0:T(8,128)(2,1)S(1)} %copy-done.2, bf16[512,1024]{1,0:T(8,128)(2,1)} %collective-permute-done.2.zk.zv, ...), custom_call_target="tpu_custom_call" | custom-call | flops 1610612736 | bytes 6291456 | tf_op jit(solution)/shard_map/pallas_call | solution.py:214
  217.8 6.3 %collective-permute-done.4.ck.cv = bf16[256,1024]{1,0:T(8,128)(2,1)S(1)} collective-permute-done((bf16[256,1024]{1,0:T(8,128)(2,1)S(1)}, bf16[256,1024]{1,0:T(8,128)(2,1)S(1)}, u32[]{:S(2)}, u32[]{:S(2)}) %collective-permute-start.4) | collective-permute-done | bytes 524320 | tf_op jit(solution)/shard_map/ppermute | solution.py:378
  224.0 15.6 %collective-permute-done.3.nk.nv = bf16[512,1024]{1,0:T(8,128)(2,1)} collective-permute-done((bf16[512,1024]{1,0:T(8,128)(2,1)}, bf16[512,1024]{1,0:T(8,128)(2,1)}, u32[]{:S(2)}, u32[]{:S(2)}) %collective-permute-start.3) | collective-permute-done | bytes 1048608 | tf_op jit(solution)/shard_map/ppermute | solution.py:376
  239.6 4.1 %shard_map.96.att_ref = bf16[512,1024]{1,0:T(8,128)(2,1)S(1)} custom-call(s32[4]{0:T(128)S(1)} %pad_add_fusion.flag_ref, bf16[512,1024]{1,0:T(8,128)(2,1)S(1)} %shard_map.93.q_ref, f32[4,2,512,256]{3,2,1,0:T(8,128)S(1)} %shard_map.95.sum_ref, bf16[512,1024]{1,0:T(8,128)(2,1)} %collective-permute-done.3.nk.nv, ...), custom_call_target="tpu_custom_call" | custom-call | flops 1073741824 | bytes 6291456 | tf_op jit(solution)/shard_map/pallas_call | solution.py:226
  243.8 0.0 copy-start.7
  243.8 3.6 %shard_map.98 = bf16[256,5376]{1,0:T(8,128)(2,1)S(1)} custom-call(bf16[512,1024]{1,0:T(8,128)(2,1)S(1)} %shard_map.96.att_ref, bf16[10752,512]{1,0:T(8,128)(2,1)S(1)} %slice.11.weight_ref), custom_call_target="tpu_custom_call" | custom-call | flops 2818572288 | bytes 15728640 | tf_op jit(solution)/shard_map/pallas_call | solution.py:263
  247.4 1.6 collective-permute-start.5
  249.0 0.0 copy-done.7
  249.0 3.8 %shard_map.97.own_ref = f32[256,5376]{1,0:T(8,128)S(1)} custom-call(bf16[512,1024]{1,0:T(8,128)(2,1)S(1)} %shard_map.96.att_ref, bf16[10752,512]{1,0:T(8,128)(2,1)S(1)} %slice.11.weight_ref), custom_call_target="tpu_custom_call" | custom-call | flops 2818572288 | bytes 15728640 | tf_op jit(solution)/shard_map/pallas_call | solution.py:263
  252.8 0.9 collective-permute-done.5.got_ref
  253.7 3.6 %shard_map.99 = bf16[256,5376]{1,0:T(8,128)(2,1)} custom-call(bf16[256,5376]{1,0:T(8,128)(2,1)S(1)} %copy-done.1, f32[256,5376]{1,0:T(8,128)S(1)} %shard_map.97.own_ref, bf16[256,5376]{1,0:T(8,128)(2,1)S(1)} %collective-permute-done.5.got_ref, f32[1,5376]{1,0:T(1,128)S(1)} %reshape.47.gain_ref), custom_call_target="tpu_custom_call" | custom-call | flops 13762560 | bytes 14680064 | tf_op jit(solution)/shard_map/pallas_call | solution.py:287
  (5 shorter events, 0.0 us)
Async XLA Ops:
  6.5 8.5 %copy-start.1 = (bf16[256,5376]{1,0:T(8,128)(2,1)S(1)}, bf16[256,5376]{1,0:T(8,128)(2,1)}, u32[]{:S(2)}) copy-start(bf16[256,5376]{1,0:T(8,128)(2,1)} %tok_ref.1) | copy-start | bytes 8257540
  6.5 8.5 %copy-start.6 = (f32[5376]{0:T(1024)S(1)}, f32[5376]{0:T(1024)}, u32[]{:S(2)}) copy-start(f32[5376]{0:T(1024)} %param.10) | copy-start | bytes 64516
  6.5 163.8 %all-gather.2.cloned.1.call-start = ((), (), s32[]{:S(2)}) async-start(), calls=%async_computation | async-start | bytes 33546240 | tf_op jit(solution)/shard_map/all_gather | solution.py:355
  8.6 2.1 collective-permute-start.1
  17.3 5.4 %collective-permute-start = (bf16[256,5376]{1,0:T(8,128)(2,1)}, bf16[256,5376]{1,0:T(8,128)(2,1)}, u32[]{:S(2)}, u32[]{:S(2)}) collective-permute-start(bf16[256,5376]{1,0:T(8,128)(2,1)} %fusion.2.mine_ref), channel_id=1, source_target_pairs={{0,2},{2,0},{1,3},{3,1},{4,6},{6,4},{5,7},{7,5},{8,10},{10,8},{9,1... | collective-permute-start | bytes 8257544 | tf_op jit(solution)/shard_map/ppermute | solution.py:365
  26.0 2.5 copy-start
  182.4 29.0 %collective-permute-start.2 = (bf16[512,1024]{1,0:T(8,128)(2,1)}, bf16[512,1024]{1,0:T(8,128)(2,1)}, u32[]{:S(2)}, u32[]{:S(2)}) collective-permute-start(bf16[512,1024]{1,0:T(8,128)(2,1)} %shard_map.94.ok.ov), channel_id=1, source_target_pairs={{0,4},{4,8},{8,12},{12,16},{16,20},{20,24},{24,28},{28,32},{32,36}... | collective-permute-start | bytes 3145736 | tf_op jit(solution)/shard_map/ppermute | solution.py:377
  186.6 53.0 %collective-permute-start.3 = (bf16[512,1024]{1,0:T(8,128)(2,1)}, bf16[512,1024]{1,0:T(8,128)(2,1)}, u32[]{:S(2)}, u32[]{:S(2)}) collective-permute-start(bf16[512,1024]{1,0:T(8,128)(2,1)} %shard_map.94.ok.ov), channel_id=1, source_target_pairs={{0,1},{1,4},{4,5},{5,8},{8,9},{9,12},{12,13},{13,16},{16,17},{17,2... | collective-permute-start | bytes 3145736 | tf_op jit(solution)/shard_map/ppermute | solution.py:376
  189.1 11.8 %slice-start = ((s8[5505024]{0:T(1024)(128)(4,1)}), s8[4194304]{0:T(1024)(128)(4,1)S(1)}, s32[]{:S(2)}) async-start(s8[5505024]{0:T(1024)(128)(4,1)} %bitcast.6), calls=%async_computation.1 | async-start | bytes 8388608
  190.5 10.4 %slice-start.1 = ((s8[5505024]{0:T(1024)(128)(4,1)}), s8[1310720]{0:T(1024)(128)(4,1)S(1)}, s32[]{:S(2)}) async-start(s8[5505024]{0:T(1024)(128)(4,1)} %bitcast.6), calls=%async_computation.2 | async-start | bytes 2621440
  190.5 10.4 %copy-start.3 = (f32[512,128]{1,0:T(8,128)S(1)}, f32[512,128]{1,0:T(8,128)}, u32[]{:S(2)}) copy-start(f32[512,128]{1,0:T(8,128)} %get-tuple-element.16.cos_ref) | copy-start | bytes 786436
  190.5 10.4 %copy-start.4 = (f32[512,128]{1,0:T(8,128)S(1)}, f32[512,128]{1,0:T(8,128)}, u32[]{:S(2)}) copy-start(f32[512,128]{1,0:T(8,128)} %get-tuple-element.17.sin_ref) | copy-start | bytes 786436
  190.5 10.4 %copy-start.5 = (f32[128]{0:T(128)S(1)}, f32[128]{0:T(128)}, u32[]{:S(2)}) copy-start(f32[128]{0:T(128)} %param.15) | copy-start | bytes 1540
  190.5 33.5 %collective-permute-start.4 = (bf16[256,1024]{1,0:T(8,128)(2,1)S(1)}, bf16[256,1024]{1,0:T(8,128)(2,1)S(1)}, u32[]{:S(2)}, u32[]{:S(2)}) collective-permute-start(bf16[256,1024]{1,0:T(8,128)(2,1)S(1)} %slice_select_fusion), channel_id=1, source_target_pairs={{1,0},{5,4},{9,8},{13,12},{17,16},{21,20},{25,24},{29,28},{33,32},... | collective-permute-start | bytes 1572872 | tf_op jit(solution)/shard_map/ppermute | solution.py:378
  200.9 10.4 %copy-start.2 = (bf16[512,1024]{1,0:T(8,128)(2,1)S(1)}, bf16[512,1024]{1,0:T(8,128)(2,1)}, u32[]{:S(2)}) copy-start(bf16[512,1024]{1,0:T(8,128)(2,1)} %shard_map.94.ok.ov) | copy-start | bytes 3145732
  243.8 5.2 %copy-start.7 = (f32[5376]{0:T(1024)S(1)}, f32[5376]{0:T(1024)}, u32[]{:S(2)}) copy-start(f32[5376]{0:T(1024)} %param.17) | copy-start | bytes 64516
  247.4 6.3 %collective-permute-start.5 = (bf16[256,5376]{1,0:T(8,128)(2,1)S(1)}, bf16[256,5376]{1,0:T(8,128)(2,1)S(1)}, u32[]{:S(2)}, u32[]{:S(2)}) collective-permute-start(bf16[256,5376]{1,0:T(8,128)(2,1)S(1)} %shard_map.98), channel_id=1, source_target_pairs={{0,2},{2,0},{1,3},{3,1},{4,6},{6,4},{5,7},{7,5},{8,10},{10,8},{9,1... | collective-permute-start | bytes 8257544 | tf_op jit(solution)/shard_map/ppermute | solution.py:394
Sparse Core Ops, SparseCore 0:
  12.7 157.6 all-gather.1
